TPU v7x, 32 devices: a whole 2x2x4 slice. The times are simulated.
32 devices in a mesh: fsdp: 4 (over y, x), seq: 8 (over z, core).
Axes of the slice: x: 2, y: 2, z: 4, core: 2. Of those that a mesh axis runs over, the one named last changes fastest.
Arguments:
- tokens: bfloat16 [8, 1024, 2048], P('fsdp', 'seq'), may hold values from -6 to 6
- positions: int32 [8, 1024], P('fsdp', 'seq'), may hold values from 0 to 2046, as said below
- gain_attn: bfloat16 [2048], P('fsdp'), may hold values from 0.099609375 to 1.8984375
- w_query: bfloat16 [2048, 2048], P('fsdp'), may hold values from -0.1875 to 0.1875
- w_key: bfloat16 [2048, 512], P('fsdp'), may hold values from -0.1875 to 0.1875
- w_value: bfloat16 [2048, 512], P('fsdp'), may hold values from -0.125 to 0.125
- w_out: bfloat16 [2048, 2048], P('fsdp'), may hold values from -0.5 to 0.5
- gain_ffn: bfloat16 [2048], P('fsdp'), may hold values from 0.099609375 to 1.8984375
- w_gate: bfloat16 [2048, 8192], P('fsdp'), may hold values from -0.125 to 0.125
- w_up: bfloat16 [2048, 8192], P('fsdp'), may hold values from -0.125 to 0.125
- w_down: bfloat16 [8192, 2048], P('fsdp'), may hold values from -0.0625 to 0.0625
- grad_out: bfloat16 [8, 1024, 2048], P('fsdp', 'seq'), may hold values from -6 to 6
Outputs:
- layer_out: bfloat16 [8, 1024, 2048], P('fsdp', 'seq')
- grad_tokens: bfloat16 [8, 1024, 2048], P('fsdp', 'seq')
- grad_gain_attn: float32 [2048], P('fsdp')
- grad_w_query: float32 [2048, 2048], P('fsdp')
- grad_w_key: float32 [2048, 512], P('fsdp')
- grad_w_value: float32 [2048, 512], P('fsdp')
- grad_w_out: float32 [2048, 2048], P('fsdp')
- grad_gain_ffn: float32 [2048], P('fsdp')
- grad_w_gate: float32 [2048, 8192], P('fsdp')
- grad_w_up: float32 [2048, 8192], P('fsdp')
- grad_w_down: float32 [8192, 2048], P('fsdp')
Inputs may be any that keep to these rules, and one draw needn't show every extreme that they name: Along each sequence the positions rise strictly, by 1 or 2 from one token to the next.
All inputs are finite; a program needn't handle non-finite values.
Results may differ from a plain program's by a relative error of at most 0.02.
Values may be sent and summed in bfloat16 or wider, within the bound.
No kernel may reach another device: no remote copies, remote signals or barrier semaphores. Data moves between devices by JAX's collectives and lax.ppermute only.
A program may use at most 512 MiB of HBM per device.

v0:
```python
import math

import jax
import jax.numpy as jnp
from jax import lax
from jax.sharding import PartitionSpec as P

HEADS = 32
KV_HEADS = 8
HEAD_DIM = 64


norm_eps = 1e-05
theta_log = math.log(500000.0)


def rope_tables(places, half_dim):
    freqs = jnp.exp(jnp.arange(half_dim, dtype=jnp.float32) * (-2.0 * theta_log / (2 * half_dim)))
    angles = places.astype(jnp.float32)[..., None] * freqs
    return (jnp.cos(angles), jnp.sin(angles))


def rotate(field, cos_tab, sin_tab):
    half_dim = field.shape[-1] // 2
    lower_half = field[..., :half_dim]
    upper_half = field[..., half_dim:]
    return jnp.concatenate(
        [lower_half * cos_tab - upper_half * sin_tab, upper_half * cos_tab + lower_half * sin_tab],
        -1,
    )


def unrotate(field, cos_tab, sin_tab):
    half_dim = field.shape[-1] // 2
    lower_half = field[..., :half_dim]
    upper_half = field[..., half_dim:]
    return jnp.concatenate(
        [lower_half * cos_tab + upper_half * sin_tab, upper_half * cos_tab - lower_half * sin_tab],
        -1,
    )


def times_transposed(inputs, weight):
    return lax.dot_general(
        inputs, weight, (((1,), (1,)), ((), ())), preferred_element_type=jnp.float32
    )


def rows_of(inputs, grads):
    return lax.psum_scatter(
        lax.dot_general(
            inputs, grads, (((0,), (0,)), ((), ())), preferred_element_type=jnp.float32
        ).astype(jnp.bfloat16),
        "fsdp",
        scatter_dimension=0,
        tiled=True,
    ).astype(jnp.float32)


def body(
    tokens,
    positions,
    gain_attn,
    w_query,
    w_key,
    w_value,
    w_out,
    gain_ffn,
    w_gate,
    w_up,
    w_down,
    grad_out,
):
    seq_count, tok_span, width = tokens.shape
    tok_rows = seq_count * tok_span
    seq_devs = lax.axis_size("seq")
    copies = max(KV_HEADS, seq_devs)
    repeats = copies // KV_HEADS
    q_local = HEADS // seq_devs
    kv_local = copies // seq_devs
    per_copy = HEADS // copies
    full_len = tok_span * seq_devs
    block_len = min(512, full_len)
    n_blocks = full_len // block_len
    logit_scale = HEAD_DIM ** (-0.5)
    gain_a, wq_all, wk_all, wv_all, wo_all, gain_f = (
        lax.all_gather(gain_attn, "fsdp", axis=0, tiled=True),
        lax.all_gather(w_query, "fsdp", axis=0, tiled=True),
        lax.all_gather(w_key, "fsdp", axis=0, tiled=True),
        lax.all_gather(w_value, "fsdp", axis=0, tiled=True),
        lax.all_gather(w_out, "fsdp", axis=0, tiled=True),
        lax.all_gather(gain_ffn, "fsdp", axis=0, tiled=True),
    )
    x_float = tokens.reshape(tok_rows, width).astype(jnp.float32)
    inv_one = lax.rsqrt(jnp.mean(x_float * x_float, -1, keepdims=True) + norm_eps)
    x_hat = x_float * inv_one
    gain_one = gain_a.astype(jnp.float32)
    normed_one = (x_hat * gain_one).astype(jnp.bfloat16)
    query = jnp.dot(normed_one, wq_all, preferred_element_type=jnp.float32).reshape(
        tok_rows, HEADS, HEAD_DIM
    )
    key_raw = jnp.dot(normed_one, wk_all, preferred_element_type=jnp.float32).reshape(
        tok_rows, KV_HEADS, HEAD_DIM
    )
    value_raw = jnp.dot(normed_one, wv_all, preferred_element_type=jnp.float32).reshape(
        tok_rows, KV_HEADS, HEAD_DIM
    )
    cos_tab, sin_tab = rope_tables(positions.reshape(tok_rows), HEAD_DIM // 2)
    cos_tab = cos_tab[:, None, :]
    sin_tab = sin_tab[:, None, :]
    q_rot = (
        rotate(query, cos_tab, sin_tab)
        .astype(jnp.bfloat16)
        .reshape(seq_count, tok_span, HEADS * HEAD_DIM)
    )
    k_rot = rotate(key_raw, cos_tab, sin_tab).astype(jnp.bfloat16)
    v_low = value_raw.astype(jnp.bfloat16)
    kv_pair = jnp.stack([jnp.repeat(k_rot, repeats, 1), jnp.repeat(v_low, repeats, 1)], 2)
    kv_pair = kv_pair.reshape(seq_count, tok_span, copies * 2 * HEAD_DIM)
    q_heads, kv_heads = (
        lax.all_to_all(q_rot, "seq", split_axis=2, concat_axis=1, tiled=True),
        lax.all_to_all(kv_pair, "seq", split_axis=2, concat_axis=1, tiled=True),
    )
    q_heads = q_heads.reshape(seq_count, full_len, kv_local, per_copy, HEAD_DIM)
    kv_heads = kv_heads.reshape(seq_count, full_len, kv_local, 2, HEAD_DIM)
    k_heads = kv_heads[:, :, :, 0]
    v_heads = kv_heads[:, :, :, 1]
    key_index = jnp.arange(full_len, dtype=jnp.int32)

    def block_logits(offset):
        q_block = lax.dynamic_slice_in_dim(q_heads, offset, block_len, 1)
        logits = (
            jnp.einsum("sqcgd,skcd->scgqk", q_block, k_heads, preferred_element_type=jnp.float32)
            * logit_scale
        )
        query_index = offset + jnp.arange(block_len, dtype=jnp.int32)
        allowed = key_index[None, :] <= query_index[:, None]
        return (q_block, jnp.where(allowed, logits, -1e30))

    def forward_block(block_idx, state_pair):
        attended, log_sums = state_pair
        offset = block_idx * block_len
        _, logits = block_logits(offset)
        row_max = jnp.max(logits, -1, keepdims=True)
        weights_exp = jnp.exp(logits - row_max)
        row_sum = jnp.sum(weights_exp, -1, keepdims=True)
        prob_low = (weights_exp / row_sum).astype(jnp.bfloat16)
        block_out = jnp.einsum(
            "scgqk,skcd->sqcgd", prob_low, v_heads, preferred_element_type=jnp.float32
        )
        block_out = block_out.astype(jnp.bfloat16).reshape(seq_count, block_len, q_local * HEAD_DIM)
        attended = lax.dynamic_update_slice_in_dim(attended, block_out, offset, 1)
        log_sums = lax.dynamic_update_slice_in_dim(log_sums, row_max + jnp.log(row_sum), offset, 3)
        return (attended, log_sums)

    empty_out = jnp.zeros((seq_count, full_len, q_local * HEAD_DIM), jnp.bfloat16)
    empty_lse = jnp.zeros((seq_count, kv_local, per_copy, full_len, 1), jnp.float32)
    attended, log_sums = lax.fori_loop(0, n_blocks, forward_block, (empty_out, empty_lse))
    o_tokens = lax.all_to_all(attended, "seq", split_axis=1, concat_axis=2, tiled=True).reshape(
        tok_rows, HEADS * HEAD_DIM
    )
    resid = x_float + jnp.dot(o_tokens, wo_all, preferred_element_type=jnp.float32)
    inv_two = lax.rsqrt(jnp.mean(resid * resid, -1, keepdims=True) + norm_eps)
    resid_hat = resid * inv_two
    gain_two = gain_f.astype(jnp.float32)
    normed_two = (resid_hat * gain_two).astype(jnp.bfloat16)
    pieces = (
        lax.all_gather(w_gate, "fsdp", axis=0, tiled=True),
        lax.all_gather(w_up, "fsdp", axis=0, tiled=True),
    )
    columns = normed_two
    gate = jnp.dot(columns, pieces[0], preferred_element_type=jnp.float32)
    upper = jnp.dot(columns, pieces[1], preferred_element_type=jnp.float32)
    gate_sig = jax.nn.sigmoid(gate)
    gate_act = gate * gate_sig
    hidden = (gate_act * upper).astype(jnp.bfloat16)
    columns = hidden
    branch_out = jnp.dot(
        columns,
        lax.all_gather(w_down, "fsdp", axis=0, tiled=True),
        preferred_element_type=jnp.float32,
    )
    layer_out = (resid + branch_out).astype(jnp.bfloat16).reshape(seq_count, tok_span, width)
    cot_rows = grad_out.reshape(tok_rows, width)
    grad_down = rows_of(hidden, cot_rows)
    d_hidden = times_transposed(cot_rows, lax.all_gather(w_down, "fsdp", axis=0, tiled=True))
    d_gate = (d_hidden * upper * (gate_sig + gate_act * (1.0 - gate_sig))).astype(jnp.bfloat16)
    d_up = (d_hidden * gate_act).astype(jnp.bfloat16)
    grad_gate = rows_of(normed_two, d_gate)
    grad_upper = rows_of(normed_two, d_up)
    pieces = lax.all_gather((w_gate, w_up), "fsdp", axis=0, tiled=True)
    d_normed_two = times_transposed(d_gate, pieces[0]) + times_transposed(d_up, pieces[1])
    d_hat_two = d_normed_two * gain_two
    grad_gain_two = jnp.sum(d_normed_two * resid_hat, 0)
    d_resid = cot_rows.astype(jnp.float32) + inv_two * (
        d_hat_two - resid_hat * jnp.mean(d_hat_two * resid_hat, -1, keepdims=True)
    )
    d_branch = d_resid.astype(jnp.bfloat16)
    grad_out_w = lax.dot_general(
        o_tokens, d_branch, (((0,), (0,)), ((), ())), preferred_element_type=jnp.float32
    )
    d_attended = (
        times_transposed(d_branch, wo_all)
        .astype(jnp.bfloat16)
        .reshape(seq_count, tok_span, HEADS * HEAD_DIM)
    )
    d_heads = lax.all_to_all(d_attended, "seq", split_axis=2, concat_axis=1, tiled=True)
    d_heads = d_heads.reshape(seq_count, full_len, kv_local, per_copy, HEAD_DIM)

    def backward_block(block_idx, state_three):
        d_query_h, d_key_h, d_value_h = state_three
        offset = block_idx * block_len
        q_block, logits = block_logits(offset)
        probs = jnp.exp(logits - lax.dynamic_slice_in_dim(log_sums, offset, block_len, 3))
        prob_low = probs.astype(jnp.bfloat16)
        grad_block = lax.dynamic_slice_in_dim(d_heads, offset, block_len, 1)
        d_probs = jnp.einsum(
            "sqcgd,skcd->scgqk", grad_block, v_heads, preferred_element_type=jnp.float32
        )
        inner = jnp.sum(probs * d_probs, -1, keepdims=True)
        d_logits = (probs * (d_probs - inner)).astype(jnp.bfloat16)
        dq_block = (
            jnp.einsum("scgqk,skcd->sqcgd", d_logits, k_heads, preferred_element_type=jnp.float32)
            * logit_scale
        )
        d_key_h = (
            d_key_h
            + jnp.einsum("scgqk,sqcgd->skcd", d_logits, q_block, preferred_element_type=jnp.float32)
            * logit_scale
        )
        d_value_h = d_value_h + jnp.einsum(
            "scgqk,sqcgd->skcd", prob_low, grad_block, preferred_element_type=jnp.float32
        )
        d_query_h = lax.dynamic_update_slice_in_dim(
            d_query_h, dq_block.astype(jnp.bfloat16), offset, 1
        )
        return (d_query_h, d_key_h, d_value_h)

    empty_dq = jnp.zeros((seq_count, full_len, kv_local, per_copy, HEAD_DIM), jnp.bfloat16)
    empty_dkv = jnp.zeros((seq_count, full_len, kv_local, HEAD_DIM), jnp.float32)
    d_query_h, d_key_h, d_value_h = lax.fori_loop(
        0, n_blocks, backward_block, (empty_dq, empty_dkv, empty_dkv)
    )
    d_kv_pair = (
        jnp.stack([d_key_h, d_value_h], 3)
        .astype(jnp.bfloat16)
        .reshape(seq_count, full_len, kv_local * 2 * HEAD_DIM)
    )
    d_q_pack = d_query_h.reshape(seq_count, full_len, q_local * HEAD_DIM)
    dq_tokens, dkv_tokens = (
        lax.all_to_all(d_q_pack, "seq", split_axis=1, concat_axis=2, tiled=True),
        lax.all_to_all(d_kv_pair, "seq", split_axis=1, concat_axis=2, tiled=True),
    )
    dq_rot = dq_tokens.reshape(tok_rows, HEADS, HEAD_DIM).astype(jnp.float32)
    dkv_sum = jnp.sum(
        dkv_tokens.reshape(tok_rows, KV_HEADS, repeats, 2, HEAD_DIM).astype(jnp.float32), 2
    )
    d_query = (
        unrotate(dq_rot, cos_tab, sin_tab).astype(jnp.bfloat16).reshape(tok_rows, HEADS * HEAD_DIM)
    )
    d_key = (
        unrotate(dkv_sum[:, :, 0], cos_tab, sin_tab)
        .astype(jnp.bfloat16)
        .reshape(tok_rows, KV_HEADS * HEAD_DIM)
    )
    d_value = dkv_sum[:, :, 1].astype(jnp.bfloat16).reshape(tok_rows, KV_HEADS * HEAD_DIM)
    d_qkv = jnp.concatenate([d_query, d_key, d_value], 1)
    grad_qkv = lax.dot_general(
        normed_one, d_qkv, (((0,), (0,)), ((), ())), preferred_element_type=jnp.float32
    )
    q_width = HEADS * HEAD_DIM
    kv_width = KV_HEADS * HEAD_DIM
    grad_query = grad_qkv[:, :q_width]
    grad_key = grad_qkv[:, q_width : q_width + kv_width]
    grad_value = grad_qkv[:, q_width + kv_width :]
    d_normed_one = (
        times_transposed(d_query, wq_all)
        + times_transposed(d_key, wk_all)
        + times_transposed(d_value, wv_all)
    )
    d_hat_one = d_normed_one * gain_one
    grad_gain_one = jnp.sum(d_normed_one * x_hat, 0)
    d_input = d_resid + inv_one * (
        d_hat_one - x_hat * jnp.mean(d_hat_one * x_hat, -1, keepdims=True)
    )
    grad_tokens = d_input.astype(jnp.bfloat16).reshape(seq_count, tok_span, width)
    sum_q, sum_k, sum_v, sum_o, sum_g1, sum_g2 = (
        lax.psum_scatter(
            grad_query.astype(jnp.bfloat16), "fsdp", scatter_dimension=0, tiled=True
        ).astype(jnp.float32),
        lax.psum_scatter(
            grad_key.astype(jnp.bfloat16), "fsdp", scatter_dimension=0, tiled=True
        ).astype(jnp.float32),
        lax.psum_scatter(
            grad_value.astype(jnp.bfloat16), "fsdp", scatter_dimension=0, tiled=True
        ).astype(jnp.float32),
        lax.psum_scatter(
            grad_out_w.astype(jnp.bfloat16), "fsdp", scatter_dimension=0, tiled=True
        ).astype(jnp.float32),
        lax.psum_scatter(
            grad_gain_one.astype(jnp.bfloat16), "fsdp", scatter_dimension=0, tiled=True
        ).astype(jnp.float32),
        lax.psum_scatter(
            grad_gain_two.astype(jnp.bfloat16), "fsdp", scatter_dimension=0, tiled=True
        ).astype(jnp.float32),
    )
    all_q, all_k, all_v, all_o, all_g1, all_g2, all_gate, all_up, all_down = (
        lax.psum(sum_q.astype(jnp.bfloat16), "seq").astype(jnp.float32),
        lax.psum(sum_k.astype(jnp.bfloat16), "seq").astype(jnp.float32),
        lax.psum(sum_v.astype(jnp.bfloat16), "seq").astype(jnp.float32),
        lax.psum(sum_o.astype(jnp.bfloat16), "seq").astype(jnp.float32),
        lax.psum(sum_g1.astype(jnp.bfloat16), "seq").astype(jnp.float32),
        lax.psum(sum_g2.astype(jnp.bfloat16), "seq").astype(jnp.float32),
        lax.psum(grad_gate.astype(jnp.bfloat16), "seq").astype(jnp.float32),
        lax.psum(grad_upper.astype(jnp.bfloat16), "seq").astype(jnp.float32),
        lax.psum(grad_down.astype(jnp.bfloat16), "seq").astype(jnp.float32),
    )
    return (
        layer_out,
        grad_tokens,
        all_g1,
        all_q,
        all_k,
        all_v,
        all_o,
        all_g2,
        all_gate,
        all_up,
        all_down,
    )


def solution(mesh):
    placed = (
        P("fsdp", "seq", None),
        P("fsdp", "seq"),
        P("fsdp"),
        P("fsdp", None),
        P("fsdp", None),
        P("fsdp", None),
        P("fsdp", None),
        P("fsdp"),
        P("fsdp", None),
        P("fsdp", None),
        P("fsdp", None),
        P("fsdp", "seq", None),
    )
    return jax.shard_map(
        body,
        mesh=mesh,
        in_specs=placed,
        out_specs=(
            P("fsdp", "seq", None),
            P("fsdp", "seq", None),
            P("fsdp"),
            P("fsdp", None),
            P("fsdp", None),
            P("fsdp", None),
            P("fsdp", None),
            P("fsdp"),
            P("fsdp", None),
            P("fsdp", None),
            P("fsdp", None),
        ),
        check_vma=False,
    )
```

profile of v0, /device:TPU:0, one launch (start us, length us, event | category | flops | bytes accessed | tf_op | source)
XLA Modules:
  0.0 3219.6 jit_solution(10981159727728233364)
XLA Ops:
  22.9 25.0 all-gather.14.cloned.1.call-done
  50.9 34.2 %all-gather.12.cloned.1.call-done = bf16[2048,512]{1,0:T(8,128)(2,1)} async-done(((bf16[512,512]{1,0:T(8,128)(2,1)}), bf16[2048,512]{1,0:T(8,128)(2,1)}) %all-gather.12.cloned.1.call-update) | async-done | bytes 2097168 | tf_op jit(solution)/shard_map/all_gather | solution.py:89
  97.8 76.8 %all-gather.10.cloned.1.call-done = bf16[2048,2048]{1,0:T(8,128)(2,1)} async-done(((bf16[512,2048]{1,0:T(8,128)(2,1)}), bf16[2048,2048]{1,0:T(8,128)(2,1)}) %all-gather.10.cloned.1.call-update) | async-done | bytes 8388624 | tf_op jit(solution)/shard_map/all_gather | solution.py:88
  200.6 25.9 all-to-all-done
  229.6 30.2 while.34
  272.6 18.4 all-to-all-done.2
  299.8 263.1 %all-gather.18.cloned.1.call-done = bf16[2048,8192]{1,0:T(8,128)(2,1)} async-done(((bf16[512,8192]{1,0:T(8,128)(2,1)}), bf16[2048,8192]{1,0:T(8,128)(2,1)}) %all-gather.18.cloned.1.call-update) | async-done | bytes 33554448 | tf_op jit(solution)/shard_map/all_gather | solution.py:168
  562.9 21.8 fusion.80
  584.7 277.1 %all-gather.20.cloned.1.call-done = bf16[2048,8192]{1,0:T(8,128)(2,1)} async-done(((bf16[512,8192]{1,0:T(8,128)(2,1)}), bf16[2048,8192]{1,0:T(8,128)(2,1)}) %all-gather.20.cloned.1.call-update) | async-done | bytes 33554448 | tf_op jit(solution)/shard_map/all_gather | solution.py:169
  861.8 21.2 fusion.81
  883.1 277.8 %all-gather.22.cloned.1.call-done = bf16[8192,2048]{1,0:T(8,128)(2,1)} async-done(((bf16[2048,2048]{1,0:T(8,128)(2,1)}), bf16[8192,2048]{1,0:T(8,128)(2,1)}) %all-gather.22.cloned.1.call-update) | async-done | bytes 33554448 | tf_op jit(solution)/shard_map/all_gather | solution.py:180
  1160.9 23.0 multiply_convert_fusion
  1183.9 17.2 fusion.82
  1201.0 18.7 multiply_reduce_fusion
  1235.3 26.6 all-to-all-done.3
  1264.9 98.3 %while.35 = (s32[]{:T(128)}, bf16[2,1024,1,4,64]{1,4,3,0,2:T(8,128)(2,1)}, f32[2,1024,1,64]{1,3,0,2:T(8,128)}, f32[2,1024,1,64]{1,3,0,2:T(8,128)}, bf16[2,1024,1...) while((s32[]{:T(128)}, ...), condition=%wide.region_9.10_spmd.clone, body=%wide.region_7.0_spmd.clone.sunk | while | flops 2748969472 | bytes 213307824 | solution.py:241
  1391.7 23.2 all-to-all-done.4
  1515.5 89.9 %reduce-scatter.20.cloned.1.call-done = bf16[512,2048]{1,0:T(8,128)(2,1)} async-done(((bf16[2048,2048]{1,0:T(8,128)(2,1)}), bf16[512,2048]{1,0:T(8,128)(2,1)}) %reduce-scatter.20.cloned.1.call-update) | async-done | bytes 2097168 | tf_op jit(solution)/shard_map/reduce_scatter | solution.py:297
  1605.4 90.4 %reduce-scatter.14.cloned.1.call-done = bf16[512,2048]{1,0:T(8,128)(2,1)} async-done(((bf16[2048,2048]{1,0:T(8,128)(2,1)}), bf16[512,2048]{1,0:T(8,128)(2,1)}) %reduce-scatter.14.cloned.1.call-update) | async-done | bytes 2097168 | tf_op jit(solution)/shard_map/reduce_scatter | solution.py:288
  1695.8 291.6 %reduce-scatter.22.cloned.1.call-done = bf16[512,8192]{1,0:T(8,128)(2,1)} async-done(((bf16[2048,8192]{1,0:T(8,128)(2,1)}), bf16[512,8192]{1,0:T(8,128)(2,1)}) %reduce-scatter.22.cloned.1.call-update) | async-done | bytes 8388624
  1987.4 292.0 %reduce-scatter.24.cloned.1.call-done = bf16[512,8192]{1,0:T(8,128)(2,1)} async-done(((bf16[2048,8192]{1,0:T(8,128)(2,1)}), bf16[512,8192]{1,0:T(8,128)(2,1)}) %reduce-scatter.24.cloned.1.call-update) | async-done | bytes 8388624
  2279.4 291.6 %reduce-scatter.26.cloned.1.call-done = bf16[2048,2048]{1,0:T(8,128)(2,1)} async-done(((bf16[8192,2048]{1,0:T(8,128)(2,1)}), bf16[2048,2048]{1,0:T(8,128)(2,1)}) %reduce-scatter.26.cloned.1.call-update) | async-done | bytes 8388624
  2573.0 19.2 fusion.62
  2621.5 546.9 %all-reduce.10.cloned.1.call-done = (bf16[512,2048]{1,0:T(8,128)(2,1)}, bf16[512,512]{1,0:T(8,128)(2,1)}, bf16[512,512]{1,0:T(8,128)(2,1)}, bf16[512,2048]{1,0:T...) async-done(((bf16[512,2048]{1,0:T(8,128)(2,1)}, bf16[512,512]{1,0:T(8,128)(2,1)}, bf16[512,512]{1,0:T(8,128)(2,1)}, ...) | async-done | bytes 30408720 | tf_op jit(solution)/shard_map/psum | solution.py:308
  (248 shorter events, 431.6 us)
Async XLA Ops:
  7.2 40.7 %all-gather.14.cloned.1.call-start = ((), (), s32[]{:S(2)}) async-start(), calls=%async_computation.15 | async-start | bytes 2621440 | tf_op jit(solution)/shard_map/all_gather | solution.py:90
  7.9 77.2 %all-gather.12.cloned.1.call-start = ((), (), s32[]{:S(2)}) async-start(), calls=%async_computation.14 | async-start | bytes 2621440 | tf_op jit(solution)/shard_map/all_gather | solution.py:89
  8.7 165.9 %all-gather.10.cloned.1.call-start = ((), (), s32[]{:S(2)}) async-start(), calls=%async_computation.13 | async-start | bytes 10485760 | tf_op jit(solution)/shard_map/all_gather | solution.py:88
  9.4 282.6 %all-gather.16.cloned.1.call-start = ((), (), s32[]{:S(2)}) async-start(), calls=%async_computation.16 | async-start | bytes 10485760 | tf_op jit(solution)/shard_map/all_gather | solution.py:91
  10.0 552.9 %all-gather.18.cloned.1.call-start = ((), (), s32[]{:S(2)}) async-start(), calls=%async_computation.17 | async-start | bytes 41943040 | tf_op jit(solution)/shard_map/all_gather | solution.py:168
  10.6 851.3 %all-gather.20.cloned.1.call-start = ((), (), s32[]{:S(2)}) async-start(), calls=%async_computation.18 | async-start | bytes 41943040 | tf_op jit(solution)/shard_map/all_gather | solution.py:169
  11.2 1149.7 %all-gather.22.cloned.1.call-start = ((), (), s32[]{:S(2)}) async-start(), calls=%async_computation.19 | async-start | bytes 41943040 | tf_op jit(solution)/shard_map/all_gather | solution.py:180
  22.6 170.5 %copy-start.20 = (f32[256,32]{0,1:T(8,128)}, f32[256,32]{0,1:T(8,128)S(1)}, u32[]{:S(2)}) copy-start(f32[256,32]{0,1:T(8,128)S(1)} %get-tuple-element.425) | copy-start | bytes 98308
  93.2 101.4 %all-to-all-start.1 = ((bf16[2,128,1024]{1,0,2:T(2,128)(2,1)}), bf16[2,128,1024]{1,0,2:T(2,128)(2,1)S(1)}, u32[]{:S(2)}, u32[]{:S(2)}) async-start(bf16[2,128,1024]{1,0,2:T(2,128)(2,1)} %reshape.420), calls=%async_computation.1 | async-start | bytes 1048576 | tf_op jit(solution)/shard_map/all_to_all | solution.py:122
  194.6 31.9 all-to-all-start
  260.8 30.2 all-to-all-start.2
  299.8 562.0 %copy-start.9 = (bf16[256,2048]{1,0:T(8,128)(2,1)}, bf16[256,2048]{1,0:T(8,128)(2,1)S(1)}, u32[]{:S(2)}) copy-start(bf16[256,2048]{1,0:T(8,128)(2,1)S(1)} %multiply_convert_fusion.4) | copy-start | bytes 3145732
  584.7 576.2 %copy-start.15 = (bf16[2,128,2048]{2,1,0:T(8,128)(2,1)S(1)}, bf16[2,128,2048]{2,1,0:T(8,128)(2,1)}, u32[]{:S(2)}) copy-start(bf16[2,128,2048]{2,1,0:T(8,128)(2,1)} %param.27) | copy-start | bytes 3145732
  1230.7 31.2 all-to-all-start.3
  1365.9 18.9 all-to-all-start.5
  1384.8 30.1 all-to-all-start.4
  1388.4 123.2 %reduce-scatter.16.cloned.1.call-start = ((), (), s32[]{:S(2)}) async-start(), calls=%async_computation.21 | async-start | bytes 2621440 | tf_op jit(solution)/shard_map/reduce_scatter | solution.py:291
  1443.8 71.7 %reduce-scatter.18.cloned.1.call-start = ((), (), s32[]{:S(2)}) async-start(), calls=%async_computation.22 | async-start | bytes 2621440 | tf_op jit(solution)/shard_map/reduce_scatter | solution.py:294
  1444.5 160.9 %reduce-scatter.20.cloned.1.call-start = ((), (), s32[]{:S(2)}) async-start(), calls=%async_computation.23 | async-start | bytes 10485760 | tf_op jit(solution)/shard_map/reduce_scatter | solution.py:297
  1452.4 243.4 %reduce-scatter.14.cloned.1.call-start = ((), (), s32[]{:S(2)}) async-start(), calls=%async_computation.20 | async-start | bytes 10485760 | tf_op jit(solution)/shard_map/reduce_scatter | solution.py:288
  1461.2 526.2 %reduce-scatter.22.cloned.1.call-start = ((), (), s32[]{:S(2)}) async-start(), calls=%async_computation.24 | async-start | bytes 41943040
  1477.8 801.6 %reduce-scatter.24.cloned.1.call-start = ((), (), s32[]{:S(2)}) async-start(), calls=%async_computation.25 | async-start | bytes 41943040
  1494.8 1076.2 %reduce-scatter.26.cloned.1.call-start = ((), (), s32[]{:S(2)}) async-start(), calls=%async_computation.26 | async-start | bytes 41943040
  1511.5 1656.9 %all-reduce.10.cloned.1.call-start = ((), (), s32[]{:S(2)}) async-start(), calls=%async_computation.27 | async-start | bytes 60817408 | tf_op jit(solution)/shard_map/psum | solution.py:308
  (40 other events, 515.3 us)
Sparse Core Ops, SparseCore 0:
  9.9 38.0 all-gather.13
  49.8 35.2 all-gather.11
  87.0 87.5 all-gather.9
  176.3 87.5 all-gather.15
  265.6 297.2 all-gather.17
  564.6 297.2 all-gather.19
  863.6 297.2 all-gather.21
  1443.9 33.0 reduce-scatter.15
  1480.3 35.1 reduce-scatter.17
  1519.0 86.3 reduce-scatter.19
  1609.4 86.3 reduce-scatter.13
  1698.7 288.6 reduce-scatter.21
  1990.8 288.6 reduce-scatter.23
  2282.4 288.6 reduce-scatter.25
  2574.7 593.6 all-reduce.9
where the time goes:
time: 3230 us; the launch traced here: 3220 us
  waiting for transfers between devices  2670 us (83%)
  matrix products  305 us (9%)
  other arithmetic  88.7 us (3%)
  local copies, waits for them, and re-layouts  69.3 us (2%)
  blocking collectives  42.5 us (1%)
    unnamed x18, waiting for transfers between devices  880 us
    psum x1, waiting for transfers between devices, body(): lax.psum(sum_q.astype(jnp.bfloat16), 'seq').astype(jnp.float32)  547 us
    all_gather x1, waiting for transfers between devices, body(): lax.all_gather(w_down, 'fsdp', axis=0, tiled=True)  278 us
    all_gather x1, waiting for transfers between devices, body(): lax.all_gather(w_up, 'fsdp', axis=0, tiled=True)  277 us
    all_gather x1, waiting for transfers between devices, body(): lax.all_gather(w_gate, 'fsdp', axis=0, tiled=True)  263 us
    reduce_scatter x1, waiting for transfers between devices, body(): lax.psum_scatter(grad_query.astype(jnp.bfloat16), 'fsdp', scatter_dimensi...  90.4 us
    reduce_scatter x1, waiting for transfers between devices, body(): lax.psum_scatter(grad_out_w.astype(jnp.bfloat16), 'fsdp', scatter_dimensi...  89.9 us
    all_gather x1, waiting for transfers between devices, body(): lax.all_gather(w_query, 'fsdp', axis=0, tiled=True)  76.8 us
  transfers between devices with their start and end apart: 21, of which 18 were waited for; matrix products, arithmetic and copies ran while one was open for 7% of the time, Pallas kernels for 0%

commit v1 on v0

v1 whole, which is shorter than its diff:
```python
import functools
import math

import jax
import jax.numpy as jnp
import numpy as np
from jax import lax
from jax.experimental import pallas as pl
from jax.experimental.pallas import tpu as pltpu
from jax.sharding import Mesh
from jax.sharding import PartitionSpec as P

HEADS = 32
KV_HEADS = 8
HEAD_DIM = 64
GROUP = HEADS // KV_HEADS
LANES = 128

norm_eps = 1e-05
theta_log = math.log(500000.0)
BF = jnp.bfloat16
F32 = jnp.float32


def xor_send(field, bit):
    count = lax.axis_size("fsdp")
    return lax.ppermute(field, "fsdp", [(i, i ^ bit) for i in range(count)])


def core_swap(field):
    return lax.ppermute(field, "core", [(0, 1), (1, 0)])


def gather_rel(own):
    count = lax.axis_size("fsdp")
    if count == 4:
        half = own.shape[0] // 2
        one = xor_send(own, 1)
        two = xor_send(own, 2)
        top = xor_send(one[:half], 2)
        low = xor_send(two[half:], 1)
        return [own, one, two, jnp.concatenate([top, low], 0)]
    chunks = [own]
    bit = 1
    while bit < count:
        chunks = chunks + [xor_send(chunk, bit) for chunk in chunks]
        bit *= 2
    return chunks


def reduce_rel(partials):
    count = lax.axis_size("fsdp")
    if count == 4:
        zero, one, two, three = partials
        half = three.shape[0] // 2
        top = xor_send(three[:half], 1)
        low = xor_send(three[half:], 2)
        two = jnp.concatenate([add_low(two[:half], top), two[half:]], 0)
        one = jnp.concatenate([one[:half], add_low(one[half:], low)], 0)
        one = xor_send(one, 1)
        two = xor_send(two, 2)
        return zero.astype(F32) + one.astype(F32) + two.astype(F32)
    chunks = list(partials)
    bit = count // 2
    while bit >= 1:
        sent = [xor_send(chunks[bit + i].astype(BF), bit) for i in range(bit)]
        chunks = [chunks[i].astype(F32) + sent[i].astype(F32) for i in range(bit)]
        bit //= 2
    return chunks[0]


def add_low(left, right):
    return (left.astype(F32) + right.astype(F32)).astype(BF)


def z_steps():
    count = lax.axis_size("zed")
    half = count // 2
    inwards = [[(i, i + 1), (count - 1 - i, count - 2 - i)] for i in range(half - 1)]
    outwards = [[(b, a) for a, b in pairs] for pairs in reversed(inwards)]
    middle = [(half - 1, half), (half, half - 1)]
    return [(pairs, True) for pairs in inwards + [middle]] + [(pairs, False) for pairs in outwards]


def z_move(field, stage):
    return lax.ppermute(field, "zed", z_steps()[stage][0])


def z_join(field, moved, stage):
    pairs, adds = z_steps()[stage]
    if adds:
        return add_low(field, moved)
    place = lax.axis_index("zed")
    return jnp.where((place == pairs[0][1]) | (place == pairs[1][1]), moved, field)


class Line:
    def __init__(self):
        self.last = len(z_steps())
        self.running = []
        self.ready = {}

    def round(self, tie, **fields):
        self.running += [(name, 0, field) for name, field in fields.items()]
        moved = [z_move(field, stage) for _, stage, field in self.running]
        tie, moved = lax.optimization_barrier((tie, moved))
        left = []
        for (name, stage, field), arrived in zip(self.running, moved):
            field = z_join(field, arrived, stage)
            if stage + 1 == self.last:
                self.ready[name] = field
            else:
                left.append((name, stage + 1, field))
        self.running = left
        return tie

    def take(self, *names):
        while not all(name in self.ready for name in names):
            self.round(())
        return [self.ready[name] for name in names]

    def hold(self, tie):
        held = [field for _, _, field in self.running]
        tie, held = lax.optimization_barrier((tie, held))
        self.running = [(name, stage, h) for (name, stage, _), h in zip(self.running, held)]
        return tie


def z_up(field):
    count = lax.axis_size("zed")
    return lax.ppermute(field, "zed", [(i, i + 1) for i in range(count - 1)])


def z_down(field):
    count = lax.axis_size("zed")
    return lax.ppermute(field, "zed", [(i + 1, i) for i in range(count - 1)])


def cost(flops, transcendentals, bytes_accessed):
    return pl.CostEstimate(
        flops=flops // 4, transcendentals=transcendentals // 4, bytes_accessed=bytes_accessed // 4
    )


def rotated(field, cos_tab, sin_tab):
    lane = lax.broadcasted_iota(jnp.int32, field.shape, 1)
    other = jnp.where(
        lane % HEAD_DIM < HEAD_DIM // 2,
        pltpu.roll(field, LANES - HEAD_DIM // 2, 1),
        pltpu.roll(field, HEAD_DIM // 2, 1),
    )
    return field * cos_tab + other * sin_tab


def kv_tables(cos_tab, sin_tab):
    lane = lax.broadcasted_iota(jnp.int32, cos_tab.shape, 1)
    return (
        jnp.where(lane < HEAD_DIM, cos_tab, 1.0),
        jnp.where(lane < HEAD_DIM, sin_tab, 0.0),
    )


def block_lanes(i, core, shard):
    half = shard // 2
    return pl.ds(pl.multiple_of(i * shard + core * half, half), half)


def project_kernel(
    place_ref, x_ref, gain_ref, own_ref, other_ref, cos_ref, sin_ref, h_ref, q_ref, kv_ref
):
    x = x_ref[...].astype(F32)
    inv = lax.rsqrt(jnp.mean(x * x, -1, keepdims=True) + norm_eps)
    h_ref[...] = (x * inv * gain_ref[...]).astype(BF)
    cos_tab = cos_ref[...]
    sin_tab = sin_ref[...]
    kv_cos, kv_sin = kv_tables(cos_tab, sin_tab)
    core = place_ref[1]
    raw = jnp.zeros((x.shape[0], own_ref.shape[2]), F32)
    for i in range(own_ref.shape[0]):
        for ref, side in ((own_ref, core), (other_ref, 1 - core)):
            cols = block_lanes(i, side, 2 * own_ref.shape[1])
            raw = raw + jnp.dot(h_ref[:, cols], ref[i], preferred_element_type=F32)
    q_width = q_ref.shape[1]
    for start in range(0, q_width, LANES):
        part = rotated(raw[:, start : start + LANES], cos_tab, sin_tab)
        q_ref[:, start : start + LANES] = (part * HEAD_DIM**-0.5).astype(BF)
    for start in range(0, kv_ref.shape[1], LANES):
        part = rotated(raw[:, q_width + start : q_width + start + LANES], kv_cos, kv_sin)
        kv_ref[:, start : start + LANES] = part.astype(BF)


def project(place, x, gain, w_own, w_other, cos_tab, sin_tab, kv_width):
    rows, width = x.shape
    all_width = w_own.shape[2]
    q_width = all_width - kv_width
    return pl.pallas_call(
        project_kernel,
        in_specs=[pl.BlockSpec(memory_space=pltpu.SMEM)]
        + [pl.BlockSpec(memory_space=pltpu.VMEM)] * 6,
        out_shape=(
            jax.ShapeDtypeStruct((rows, width), BF),
            jax.ShapeDtypeStruct((rows, q_width), BF),
            jax.ShapeDtypeStruct((rows, kv_width), BF),
        ),
        compiler_params=pltpu.CompilerParams(vmem_limit_bytes=40 << 20),
        cost_estimate=cost(
            flops=2 * rows * width * all_width,
            transcendentals=rows,
            bytes_accessed=4 * rows * width + 2 * width * all_width,
        ),
        name="project",
    )(place, x, gain, w_own, w_other, cos_tab, sin_tab)


def unrotate_kernel(dq_ref, cos_ref, sin_ref, d_ref):
    for start in range(0, dq_ref.shape[1], LANES):
        part = dq_ref[:, start : start + LANES].astype(F32)
        d_ref[:, start : start + LANES] = rotated(part, cos_ref[...], -sin_ref[...]).astype(BF)


def unrotate(dq, cos_tab, sin_tab, block):
    rows, wide = dq.shape
    tables = pl.BlockSpec((block, LANES), lambda i: (i, 0))
    field = pl.BlockSpec((block, wide), lambda i: (i, 0))
    return pl.pallas_call(
        unrotate_kernel,
        grid=(rows // block,),
        in_specs=[field, tables, tables],
        out_specs=field,
        out_shape=jax.ShapeDtypeStruct(dq.shape, BF),
        cost_estimate=cost(
            flops=6 * rows * wide, transcendentals=0, bytes_accessed=6 * rows * wide
        ),
        name="unrotate",
    )(dq, cos_tab, sin_tab)


def unproject_kernel(
    place_ref, dq_ref, dkv_ref, own_ref, other_ref, cos_ref, sin_ref, d_ref, dh_ref
):
    kv_cos, kv_sin = kv_tables(cos_ref[...], -sin_ref[...])
    q_width = dq_ref.shape[1]
    for start in range(0, dkv_ref.shape[1], LANES):
        part = rotated(dkv_ref[:, start : start + LANES].astype(F32), kv_cos, kv_sin)
        d_ref[:, start : start + LANES] = part.astype(BF)
    core = place_ref[1]
    across = (((1,), (1,)), ((), ()))
    for i in range(own_ref.shape[0]):
        for ref, side in ((own_ref, core), (other_ref, 1 - core)):
            cols = block_lanes(i, side, 2 * own_ref.shape[1])
            total = lax.dot_general(
                dq_ref[...], ref[i, :, :q_width], across, preferred_element_type=F32
            )
            total = total + lax.dot_general(
                d_ref[...], ref[i, :, q_width:], across, preferred_element_type=F32
            )
            dh_ref[:, cols] = total.astype(BF)


def unproject(place, dq, dkv, w_own, w_other, cos_tab, sin_tab):
    rows = dq.shape[0]
    count, half, cols = w_own.shape
    width = 2 * count * half
    block = rows // count

    def row_block(wide):
        return pl.BlockSpec((block, wide), lambda i, place: (i, 0))

    weights = pl.BlockSpec(w_own.shape, lambda i, place: (0, 0, 0))
    return pl.pallas_call(
        unproject_kernel,
        grid_spec=pltpu.PrefetchScalarGridSpec(
            num_scalar_prefetch=1,
            grid=(rows // block,),
            in_specs=[
                row_block(dq.shape[1]),
                row_block(dkv.shape[1]),
                weights,
                weights,
                row_block(LANES),
                row_block(LANES),
            ],
            out_specs=(row_block(dkv.shape[1]), row_block(width)),
        ),
        out_shape=(
            jax.ShapeDtypeStruct(dkv.shape, BF),
            jax.ShapeDtypeStruct((rows, width), BF),
        ),
        compiler_params=pltpu.CompilerParams(vmem_limit_bytes=40 << 20),
        cost_estimate=cost(
            flops=2 * rows * width * cols,
            transcendentals=0,
            bytes_accessed=2 * rows * width + 2 * width * cols + 4 * rows * cols,
        ),
        name="unproject",
    )(place, dq, dkv, w_own, w_other, cos_tab, sin_tab)


def pick_units(place, w_even, w_odd, count):
    high, wide = w_even.shape
    units = wide // count // 2

    def kernel(place_ref, even_ref, odd_ref, out_ref):
        even = place_ref[0] % 2 == 0

        @pl.when(even)
        def _():
            out_ref[0] = even_ref[...]

        @pl.when(jnp.logical_not(even))
        def _():
            out_ref[0] = odd_ref[...]

    def columns(parity):
        def index(i, place):
            here = place[0] % 2 == parity
            return (0, jnp.where(here, 2 * i + place[1], 0))

        return pl.BlockSpec((high, units), index)

    return pl.pallas_call(
        kernel,
        grid_spec=pltpu.PrefetchScalarGridSpec(
            num_scalar_prefetch=1,
            grid=(count,),
            in_specs=[columns(0), columns(1)],
            out_specs=pl.BlockSpec((1, high, units), lambda i, place: (i, 0, 0)),
        ),
        out_shape=jax.ShapeDtypeStruct((count, high, units), BF),
        cost_estimate=cost(
            flops=0, transcendentals=0, bytes_accessed=4 * count * high * units
        ),
        name="pick_units",
    )(place, w_even, w_odd)


def pick_heads(place, w_query, w_key, w_value, count):
    high = w_query.shape[0] // 2
    q_width = w_query.shape[1] // count
    k_width = w_key.shape[1] // count

    def kernel(place_ref, q_ref, k_ref, v_ref, out_ref):
        for i in range(count):
            out_ref[i, :, :q_width] = q_ref[:, i * q_width : (i + 1) * q_width]
            for head in range(k_width // HEAD_DIM):
                cols = slice(i * k_width + head * HEAD_DIM, i * k_width + (head + 1) * HEAD_DIM)
                start = q_width + head * LANES
                out_ref[i, :, start : start + LANES] = jnp.concatenate(
                    [k_ref[:, cols], v_ref[:, cols]], 1
                )

    def half(weight):
        return pl.BlockSpec((high, weight.shape[1]), lambda i, place: (place[1], 0))

    all_width = q_width + 2 * k_width
    return pl.pallas_call(
        kernel,
        grid_spec=pltpu.PrefetchScalarGridSpec(
            num_scalar_prefetch=1,
            grid=(1,),
            in_specs=[half(w_query), half(w_key), half(w_value)],
            out_specs=pl.BlockSpec((count, high, all_width), lambda i, place: (0, 0, 0)),
        ),
        out_shape=jax.ShapeDtypeStruct((count, high, all_width), BF),
        cost_estimate=cost(
            flops=0, transcendentals=0, bytes_accessed=4 * count * high * all_width
        ),
        name="pick_heads",
    )(place, w_query, w_key, w_value)


def feed_kernel(place_ref, h_ref, cot_ref, w0_ref, w1_ref, wd_ref, hidden_ref, dg_ref, du_ref):
    high = h_ref.shape[0] // 2

    def run(wg_ref, wu_ref):
        for start in (0, high):
            rows = slice(start, start + high)
            gate = jnp.dot(h_ref[rows], wg_ref[...], preferred_element_type=F32)
            upper = jnp.dot(h_ref[rows], wu_ref[...], preferred_element_type=F32)
            gate_sig = jax.nn.sigmoid(gate)
            gate_act = gate * gate_sig
            hidden_ref[rows] = (gate_act * upper).astype(BF)
            d_hidden = lax.dot_general(
                cot_ref[rows], wd_ref[...], (((1,), (1,)), ((), ())), preferred_element_type=F32
            )
            d_gate = d_hidden * upper * (gate_sig + gate_act * (1.0 - gate_sig))
            dg_ref[rows] = d_gate.astype(BF)
            du_ref[rows] = (d_hidden * gate_act).astype(BF)

    even = place_ref[0] % 2 == 0

    @pl.when(even)
    def _():
        run(w0_ref, w1_ref)

    @pl.when(jnp.logical_not(even))
    def _():
        run(w1_ref, w0_ref)


def feed(place, h_all, cot_all, w0, w1, w_down, side):
    rows, width = h_all.shape
    units = w0.shape[1]
    block = min(256, units)
    steps = units // block
    full = pl.BlockSpec((rows, width), lambda j, place: (0, 0))
    columns = pl.BlockSpec((width, block), lambda j, place: (0, j))
    out = pl.BlockSpec((rows, block), lambda j, place: (0, j))
    return pl.pallas_call(
        feed_kernel,
        grid_spec=pltpu.PrefetchScalarGridSpec(
            num_scalar_prefetch=1,
            grid=(steps,),
            in_specs=[
                full,
                full,
                columns,
                columns,
                pl.BlockSpec(
                    (block, width), lambda j, place: ((place[1] + side) % 2 * steps + j, 0)
                ),
            ],
            out_specs=[out] * 3,
        ),
        out_shape=[jax.ShapeDtypeStruct((rows, units), BF)] * 3,
        compiler_params=pltpu.CompilerParams(vmem_limit_bytes=56 << 20),
        cost_estimate=cost(
            flops=6 * rows * width * units,
            transcendentals=rows * units,
            bytes_accessed=4 * rows * width + 6 * width * units + 6 * rows * units,
        ),
        name="feed",
    )(place, h_all, cot_all, w0, w1, w_down)


def unfeed(place, dg, du, w0, w1, first, last):
    high = last - first
    units = dg[0].shape[1]
    width = w0[0].shape[0]
    block = min(512, width)
    across = (((1,), (1,)), ((), ()))

    def kernel(place_ref, dg0, dg1, du0, du1, w00, w01, w10, w11, out_ref):
        def run(*pairs):
            total = None
            for d_ref, w_ref in pairs:
                part = lax.dot_general(
                    d_ref[...], w_ref[...], across, preferred_element_type=F32
                )
                total = part if total is None else total + part
            out_ref[...] = total.astype(BF)

        even = place_ref[0] % 2 == 0

        @pl.when(even)
        def _():
            run((dg0, w00), (du0, w10), (dg1, w01), (du1, w11))

        @pl.when(jnp.logical_not(even))
        def _():
            run((du0, w00), (dg0, w10), (du1, w01), (dg1, w11))

    return pl.pallas_call(
        kernel,
        grid_spec=pltpu.PrefetchScalarGridSpec(
            num_scalar_prefetch=1,
            grid=(width // block,),
            in_specs=[pl.BlockSpec((high, units), lambda n, place: (first // high, 0))] * 4
            + [pl.BlockSpec((block, units), lambda n, place: (n, 0))] * 4,
            out_specs=pl.BlockSpec((high, block), lambda n, place: (0, n)),
        ),
        out_shape=jax.ShapeDtypeStruct((high, width), BF),
        compiler_params=pltpu.CompilerParams(vmem_limit_bytes=48 << 20),
        cost_estimate=cost(
            flops=8 * high * units * width,
            transcendentals=0,
            bytes_accessed=8 * width * units + 8 * high * units + 2 * high * width,
        ),
        name="unfeed",
    )(place, *dg, *du, *w0, *w1)


def lower(place, hidden, w_down):
    rows, units = hidden[0].shape
    width = w_down.shape[1]
    block = min(512, width)

    def kernel(place_ref, h0, h1, w0, w1, out_ref):
        total = jnp.dot(h0[...], w0[...], preferred_element_type=F32)
        total = total + jnp.dot(h1[...], w1[...], preferred_element_type=F32)
        out_ref[...] = total.astype(BF)

    return pl.pallas_call(
        kernel,
        grid_spec=pltpu.PrefetchScalarGridSpec(
            num_scalar_prefetch=1,
            grid=(width // block,),
            in_specs=[pl.BlockSpec((rows, units), lambda n, place: (0, 0))] * 2
            + [
                pl.BlockSpec((units, block), lambda n, place: (place[1], n)),
                pl.BlockSpec((units, block), lambda n, place: (1 - place[1], n)),
            ],
            out_specs=pl.BlockSpec((rows, block), lambda n, place: (0, n)),
        ),
        out_shape=jax.ShapeDtypeStruct((rows, width), BF),
        compiler_params=pltpu.CompilerParams(vmem_limit_bytes=48 << 20),
        cost_estimate=cost(
            flops=4 * rows * units * width,
            transcendentals=0,
            bytes_accessed=4 * width * units + 4 * rows * units + 2 * rows * width,
        ),
        name="lower",
    )(place, *hidden, w_down, w_down)


def low_lanes(shape):
    return lax.broadcasted_iota(jnp.int32, shape, 1) < HEAD_DIM


def stack_heads(ref, group, upper):
    rows = []
    for head in range(0, GROUP, 2):
        start = (group * GROUP + head) * HEAD_DIM
        pair = ref[:, start : start + LANES].astype(F32)
        turned = pltpu.roll(pair, HEAD_DIM, 1)
        keep = low_lanes(pair.shape)
        if upper:
            keep = jnp.logical_not(keep)
            rows += [jnp.where(keep, turned, 0.0), jnp.where(keep, pair, 0.0)]
        else:
            rows += [jnp.where(keep, pair, 0.0), jnp.where(keep, turned, 0.0)]
    return jnp.concatenate(rows, 0).astype(BF)


def unstack_heads(stacked, ref, group, upper):
    span = ref.shape[0]
    for head in range(0, GROUP, 2):
        even = stacked[head * span : (head + 1) * span]
        odd = stacked[(head + 1) * span : (head + 2) * span]
        keep = low_lanes(even.shape)
        if upper:
            pair = jnp.where(keep, pltpu.roll(even, HEAD_DIM, 1), odd)
        else:
            pair = jnp.where(keep, even, pltpu.roll(odd, HEAD_DIM, 1))
        start = (group * GROUP + head) * HEAD_DIM
        ref[:, start : start + LANES] = pair.astype(ref.dtype)


def logits_of(place_ref, q_all, kv_own, kv_rest, span):
    own = lax.dot_general(q_all, kv_own, (((1,), (1,)), ((), ())), preferred_element_type=F32)
    rest = lax.dot_general(q_all, kv_rest, (((1,), (1,)), ((), ())), preferred_element_type=F32)
    row = lax.broadcasted_iota(jnp.int32, own.shape, 0) % span
    col = lax.broadcasted_iota(jnp.int32, own.shape, 1)
    own = jnp.where(col <= row, own, -1e30)
    block = lax.broadcasted_iota(jnp.int32, (1, rest.shape[1]), 1) // span + 1
    have = jnp.where(block == 1, place_ref[1], place_ref[0])
    need = jnp.where(block == 1, 1, block // 2)
    rest = rest + jnp.where(have >= need, 0.0, -1e30)
    return own, rest


def attend_kernel(place_ref, q_ref, *refs):
    kv_refs = refs[:-2]
    out_ref, lse_ref = refs[-2:]
    span = q_ref.shape[0]
    for group in range(lse_ref.shape[1]):
        cols = slice(group * LANES, (group + 1) * LANES)
        q_all = stack_heads(q_ref, group, False)
        kv_own = kv_refs[0][:, cols]
        kv_rest = jnp.concatenate([ref[:, cols] for ref in kv_refs[1:]], 0)
        own, rest = logits_of(place_ref, q_all, kv_own, kv_rest, span)
        top = jnp.maximum(jnp.max(own, -1, keepdims=True), jnp.max(rest, -1, keepdims=True))
        own = jnp.exp(own - top)
        rest = jnp.exp(rest - top)
        total = jnp.sum(own, -1, keepdims=True) + jnp.sum(rest, -1, keepdims=True)
        out = jnp.dot(own.astype(BF), kv_own, preferred_element_type=F32)
        out = out + jnp.dot(rest.astype(BF), kv_rest, preferred_element_type=F32)
        unstack_heads(out / total, out_ref, group, True)
        lse_ref[0, group] = top + jnp.log(total)


def attend_back_kernel(place_ref, q_ref, do_ref, lse_ref, *refs):
    count = (len(refs) - 1) // 2
    kv_refs = refs[:count]
    dq_ref = refs[count]
    dkv_refs = refs[count + 1 :]
    span = q_ref.shape[0]
    flip = (((0,), (0,)), ((), ()))
    across = (((1,), (1,)), ((), ()))
    for group in range(lse_ref.shape[1]):
        cols = slice(group * LANES, (group + 1) * LANES)
        q_all = stack_heads(q_ref, group, False)
        do_all = stack_heads(do_ref, group, True)
        kv_own = kv_refs[0][:, cols]
        kv_rest = jnp.concatenate([ref[:, cols] for ref in kv_refs[1:]], 0)
        own, rest = logits_of(place_ref, q_all, kv_own, kv_rest, span)
        lse = lse_ref[0, group]
        own = jnp.exp(own - lse)
        rest = jnp.exp(rest - lse)
        d_own = lax.dot_general(do_all, kv_own, across, preferred_element_type=F32)
        d_rest = lax.dot_general(do_all, kv_rest, across, preferred_element_type=F32)
        inner = jnp.sum(own * d_own, -1, keepdims=True) + jnp.sum(rest * d_rest, -1, keepdims=True)
        d_own = (own * (d_own - inner)).astype(BF)
        d_rest = (rest * (d_rest - inner)).astype(BF)
        dq = jnp.dot(d_own, kv_own, preferred_element_type=F32)
        dq = dq + jnp.dot(d_rest, kv_rest, preferred_element_type=F32)
        unstack_heads(dq * HEAD_DIM**-0.5, dq_ref, group, False)
        dkv = lax.dot_general(d_own, q_all, flip, preferred_element_type=F32)
        dkv = dkv + lax.dot_general(own.astype(BF), do_all, flip, preferred_element_type=F32)
        dkv_refs[0][:, cols] = dkv.astype(BF)
        dkv = lax.dot_general(d_rest, q_all, flip, preferred_element_type=F32)
        dkv = dkv + lax.dot_general(rest.astype(BF), do_all, flip, preferred_element_type=F32)
        for i, ref in enumerate(dkv_refs[1:]):
            ref[:, cols] = dkv[i * span : (i + 1) * span].astype(BF)


def attend_specs(q_all, kv_all, span):
    kv_width = kv_all[0].shape[1]
    groups = kv_width // LANES
    return (
        pl.BlockSpec((span, q_all.shape[1]), lambda i, place: (i, 0)),
        pl.BlockSpec((span, kv_width), lambda i, place: (i, 0)),
        pl.BlockSpec((1, groups, GROUP * span, 1), lambda i, place: (i, 0, 0, 0)),
        groups,
    )


def attend(place, q_all, kv_all, span):
    rows = q_all.shape[0]
    q_spec, kv_spec, lse_spec, groups = attend_specs(q_all, kv_all, span)
    cells = rows * groups * GROUP * span * len(kv_all)
    return pl.pallas_call(
        attend_kernel,
        grid_spec=pltpu.PrefetchScalarGridSpec(
            num_scalar_prefetch=1,
            grid=(rows // span,),
            in_specs=[q_spec] + [kv_spec] * len(kv_all),
            out_specs=[q_spec, lse_spec],
        ),
        out_shape=(
            jax.ShapeDtypeStruct(q_all.shape, BF),
            jax.ShapeDtypeStruct((rows // span, groups, GROUP * span, 1), F32),
        ),
        compiler_params=pltpu.CompilerParams(vmem_limit_bytes=56 << 20),
        cost_estimate=cost(
            flops=2 * 4 * LANES * cells, transcendentals=cells, bytes_accessed=16 << 20
        ),
        name="attend",
    )(place, q_all, *kv_all)


def attend_back(place, q_all, do_all, lse, kv_all, span):
    rows = q_all.shape[0]
    q_spec, kv_spec, lse_spec, groups = attend_specs(q_all, kv_all, span)
    cells = rows * groups * GROUP * span * len(kv_all)
    outs = pl.pallas_call(
        attend_back_kernel,
        grid_spec=pltpu.PrefetchScalarGridSpec(
            num_scalar_prefetch=1,
            grid=(rows // span,),
            in_specs=[q_spec, q_spec, lse_spec] + [kv_spec] * len(kv_all),
            out_specs=[q_spec] + [kv_spec] * len(kv_all),
        ),
        out_shape=[jax.ShapeDtypeStruct(q_all.shape, BF)]
        + [jax.ShapeDtypeStruct(kv.shape, BF) for kv in kv_all],
        compiler_params=pltpu.CompilerParams(vmem_limit_bytes=60 << 20),
        cost_estimate=cost(
            flops=2 * 8 * LANES * cells, transcendentals=cells, bytes_accessed=24 << 20
        ),
        name="attend_back",
    )(place, q_all, do_all, lse, *kv_all)
    return outs[0], outs[1:]


def spread_kernel(place_ref, own_ref, other_ref, out_ref):
    @pl.when(pl.program_id(1) == 0)
    def _():
        out_ref[...] = own_ref[0].astype(F32)

    @pl.when(pl.program_id(1) == 1)
    def _():
        out_ref[...] = other_ref[0].astype(F32)


def spread(own, other, c, axis):
    count, high, wide = own.shape
    shape = {
        0: (high * 2 * count, wide),
        1: (high, wide * 2 * count),
        2: (high * 2, wide * count),
    }[axis]

    def out_place(i, side, place):
        core = (place[0] + side) % 2
        return [(2 * i + core, 0), (0, 2 * i + core), (core, i)][axis]

    return pl.pallas_call(
        spread_kernel,
        grid_spec=pltpu.PrefetchScalarGridSpec(
            num_scalar_prefetch=1,
            grid=(count, 2),
            in_specs=[pl.BlockSpec((1, high, wide), lambda i, side, place: (i, 0, 0))] * 2,
            out_specs=pl.BlockSpec((high, wide), out_place),
        ),
        out_shape=jax.ShapeDtypeStruct(shape, F32),
        compiler_params=pltpu.CompilerParams(vmem_limit_bytes=48 << 20),
        cost_estimate=cost(
            flops=own.size, transcendentals=0, bytes_accessed=12 * own.size
        ),
        name="spread",
    )(c.astype(jnp.int32)[None], own, other)


def dot(left, right):
    return jnp.dot(left, right, preferred_element_type=F32)


def dot_t(left, right):
    return lax.dot_general(left, right, (((1,), (1,)), ((), ())), preferred_element_type=F32)


def t_dot(left, right):
    return lax.dot_general(left, right, (((0,), (0,)), ((), ())), preferred_element_type=F32)


def exchange(field):
    return lax.all_to_all(field, "fsdp", split_axis=0, concat_axis=0, tiled=True)


def by_core(own, other, axis):
    first = lax.axis_index("core") == 0
    return jnp.stack([jnp.where(first, own, other), jnp.where(first, other, own)], axis)


def take(field, index, size, axis):
    return lax.dynamic_slice_in_dim(field, index * size, size, axis)


def body(
    tokens,
    positions,
    gain_attn,
    w_query,
    w_key,
    w_value,
    w_out,
    gain_ffn,
    w_gate,
    w_up,
    w_down,
    grad_out,
):
    seq_count, span, width = tokens.shape
    rows = seq_count * span
    count = lax.axis_size("fsdp")
    depth = lax.axis_size("zed")
    f = lax.axis_index("fsdp")
    z = lax.axis_index("zed")
    c = lax.axis_index("core")
    shard = width // count
    half_shard = shard // 2
    q_width = HEADS * HEAD_DIM // count
    k_width = KV_HEADS * HEAD_DIM // count
    kv_local = KV_HEADS // count
    ff = w_gate.shape[1]
    ff_half = ff // count // 2
    place = jnp.stack([z, c]).astype(jnp.int32)

    x_own = tokens.reshape(rows, width)
    x_list = gather_rel(x_own)
    small = jnp.concatenate(
        [gain_attn.astype(F32), gain_ffn.astype(F32), positions.reshape(rows).astype(F32)]
    ).reshape(-1, LANES)
    small_list = [small] + [xor_send(small, r) for r in range(1, count)]
    gain_rows = shard // LANES

    def by_index(pieces):
        bit = 1
        while bit < count:
            odd = (f // bit) % 2 == 1
            pieces = [jnp.where(odd, pieces[i ^ bit], pieces[i]) for i in range(count)]
            bit *= 2
        return jnp.concatenate(pieces, 0)

    gain_one = by_index([piece[:gain_rows] for piece in small_list]).reshape(1, width)
    gain_two = by_index([piece[gain_rows : 2 * gain_rows] for piece in small_list]).reshape(
        1, width
    )
    places = jnp.concatenate([piece[2 * gain_rows :].reshape(rows) for piece in small_list])
    half_dim = HEAD_DIM // 2
    lane = jnp.arange(LANES, dtype=jnp.int32)
    freqs = jnp.exp((lane % half_dim).astype(F32) * (-2.0 * theta_log / (2 * half_dim)))
    angles = places[:, None] * freqs
    cos_tab = jnp.cos(angles)
    sin_tab = jnp.sin(angles) * jnp.where(lane % HEAD_DIM < half_dim, -1.0, 1.0)

    all_width = q_width + 2 * k_width
    w_own = exchange(pick_heads(place, w_query, w_key, w_value, count))
    w_other = core_swap(w_own)

    w0, x_list, cos_tab, sin_tab, gain_one = lax.optimization_barrier(
        (pick_units(place, w_gate, w_up, count), x_list, cos_tab, sin_tab, gain_one)
    )
    w0 = exchange(w0).reshape(width, ff_half)

    kv_width = 2 * k_width
    h_list, q_list, kv_list = [], [], []
    for r in range(count):
        piece = slice(r * rows, (r + 1) * rows)
        h, q, kv = project(
            place, x_list[r], gain_one, w_own, w_other, cos_tab[piece], sin_tab[piece], kv_width
        )
        h_list.append(h)
        q_list.append(q)
        kv_list.append(kv)
    h_all = jnp.concatenate(h_list, 0)
    q_all = jnp.concatenate(q_list, 0)
    stream = jnp.concatenate(kv_list, 0)
    kv_all = []
    for step in range(depth):
        if step == 0:
            stream, w0 = lax.optimization_barrier((stream, w0))
        if step:
            stream = z_up(stream)
        kv_all += [stream, core_swap(stream)]
    w1, _ = lax.optimization_barrier((w0, stream))
    w1 = lax.ppermute(w1, "zed", [(i, i ^ 1) for i in range(depth)])
    cot_own = grad_out.reshape(rows, width)
    cot_abs, _ = lax.optimization_barrier((cot_own, w0))
    cot_abs = lax.all_gather(cot_abs, "fsdp", axis=0, tiled=True)
    q_all, cot_abs = lax.optimization_barrier((q_all, cot_abs))
    attended, lse = attend(place, q_all, kv_all, span)

    w0 = [w0, core_swap(w0)]

    def chunk(field, r):
        return field[r * rows : (r + 1) * rows]

    branch = [dot(chunk(attended, r), w_out) for r in range(count)]
    branch = reduce_rel([branch[0]] + [part.astype(BF) for part in branch[1:]])
    x_float = x_own.astype(F32)
    resid = x_float + branch
    inv_two = lax.rsqrt(jnp.mean(resid * resid, -1, keepdims=True) + norm_eps)
    resid_hat = resid * inv_two
    h2_list = gather_rel((resid_hat * gain_two).astype(BF))
    h2_list, w1 = lax.optimization_barrier((h2_list, w1))
    h2_all = jnp.concatenate(h2_list, 0)
    w1 = [w1, core_swap(w1)]

    cot_all = jnp.concatenate([take(cot_abs, f ^ r, rows, 0) for r in range(count)], 0)
    hidden, d_gate, d_up = zip(
        *[feed(place, h2_all, cot_all, w0[side], w1[side], w_down, side) for side in range(2)]
    )
    middle = count // 2 * rows
    far = unfeed(place, d_gate, d_up, w0, w1, middle, count * rows)
    near = unfeed(place, d_gate, d_up, w0, w1, 0, middle)
    d_h2 = reduce_rel([chunk(part, r) for part in (near, far) for r in range(count // 2)])
    down = lower(place, hidden, w_down)

    def core_sum(own, other):
        return add_low(own, core_swap(other))

    def halves(left, right):
        cut = left.shape[1] // 2
        return [
            core_sum(*[t_dot(left[:, cols], right[side]).astype(BF) for side in range(2)])
            for cols in (slice(0, cut), slice(cut, 2 * cut))
        ]

    line = Line()
    gate_parts = halves(h2_all, d_gate)
    d_h2, down = line.round((d_h2, down), gate0=gate_parts[0])
    up_parts = halves(h2_all, d_up)
    down_part = core_sum(*[t_dot(hidden[side], cot_all).astype(BF) for side in range(2)])

    d_hat_two = d_h2 * gain_two
    part_gain_two = jnp.sum(d_h2 * resid_hat, 0)
    d_resid = cot_own.astype(F32) + inv_two * (
        d_hat_two - resid_hat * jnp.mean(d_hat_two * resid_hat, -1, keepdims=True)
    )
    d_branch = gather_rel(d_resid.astype(BF))
    d_branch = line.round(d_branch, gate1=gate_parts[1])
    d_branch = jnp.concatenate(d_branch, 0)
    d_attended = dot_t(d_branch, w_out).astype(BF)
    dq, dkv_all = attend_back(place, q_all, d_attended, lse, kv_all, span)
    dq, dkv_all = line.round((dq, dkv_all), up0=up_parts[0])
    d_q = unrotate(dq, cos_tab, sin_tab, rows)
    tail = None
    for step in reversed(range(depth)):
        here = dkv_all[2 * step].astype(F32) + core_swap(dkv_all[2 * step + 1]).astype(F32)
        if tail is not None:
            here = here + z_down(tail).astype(F32)
        tail = here.astype(BF)
    down = reduce_rel([chunk(down, r) for r in range(count)])
    layer_out = (resid + down).astype(BF).reshape(seq_count, span, width)
    tail, up_last, layer_out = line.hold((tail, up_parts[1], layer_out))
    d_kv, d_h1_all = unproject(place, d_q, tail, w_own, w_other, cos_tab, sin_tab)
    d_h1 = reduce_rel([chunk(d_h1_all, r) for r in range(count)])
    d_h1 = line.round(d_h1, up1=up_last)

    def row_halves(field):
        field = field.astype(BF).reshape(count, 2, half_shard, -1)
        own = lax.dynamic_index_in_dim(field, c, 1, keepdims=False)
        other = lax.dynamic_index_in_dim(field, 1 - c, 1, keepdims=False)
        return core_sum(own, other)

    g_q = row_halves(t_dot(h_all, d_q))
    g_kv = t_dot(h_all, d_kv)
    g_out = t_dot(attended, d_branch).astype(BF)
    out_half = q_width // 2
    g_out = core_sum(take(g_out, c, out_half, 0), take(g_out, 1 - c, out_half, 0))

    inv_one = lax.rsqrt(jnp.mean(x_float * x_float, -1, keepdims=True) + norm_eps)
    x_hat = x_float * inv_one
    d_hat_one = d_h1 * gain_one
    part_gain_one = jnp.sum(d_h1 * x_hat, 0)
    d_input = d_resid + inv_one * (
        d_hat_one - x_hat * jnp.mean(d_hat_one * x_hat, -1, keepdims=True)
    )
    grad_tokens = d_input.astype(BF).reshape(seq_count, span, width)
    gains = jnp.stack([part_gain_one, part_gain_two], 1)
    gains = jnp.pad(gains, ((0, 0), (0, LANES - 2)))
    g_kv = row_halves(jnp.concatenate([g_kv, gains], 1))

    def pair_rows(own):
        return spread(own[None], core_swap(own)[None], c, 0)

    def to_rows(own):
        own = exchange(own.reshape(count, shard, ff_half))
        return spread(own, core_swap(own), c, 1)

    cut = ff_half // 2
    d_h1 = line.round(d_h1, down0=down_part[:cut])
    d_h1 = line.round(d_h1, down1=down_part[cut:])

    def whole(name):
        return jnp.concatenate(line.take(name + "0", name + "1"), 0)

    grad_gate = to_rows(whole("gate"))
    grad_gate = line.round(grad_gate, q=g_q, out=g_out, kv=g_kv)
    grad_up = to_rows(whole("up"))
    grad_gate, grad_up = line.round((grad_gate, grad_up))
    grad_gate, grad_up = line.round((grad_gate, grad_up))
    g_q, g_out, g_kv = line.take("q", "out", "kv")
    grad_down = pair_rows(whole("down"))
    grad_out_w = pair_rows(g_out)
    g_q = exchange(g_q)
    grad_q = spread(g_q, core_swap(g_q), c, 2)
    g_kv = exchange(g_kv)
    g_kv = by_core(g_kv, core_swap(g_kv), 0).astype(F32)
    g_kv = jnp.transpose(g_kv, (0, 2, 1, 3)).reshape(shard, count, -1)
    gains = jnp.sum(g_kv[:, :, 2 * k_width : 2 * k_width + 2], 1)
    g_kv = g_kv[:, :, : 2 * k_width].reshape(shard, count * kv_local, 2, HEAD_DIM)
    grad_k = g_kv[:, :, 0].reshape(shard, count * k_width)
    grad_v = g_kv[:, :, 1].reshape(shard, count * k_width)
    return (
        layer_out,
        grad_tokens,
        gains[:, 0],
        grad_q,
        grad_k,
        grad_v,
        grad_out_w,
        gains[:, 1],
        grad_gate,
        grad_up,
        grad_down,
    )


def solution(mesh):
    fsdp, seq = mesh.devices.shape
    split = Mesh(mesh.devices.reshape(fsdp, seq // 2, 2), ("fsdp", "zed", "core"))
    field = P("fsdp", ("zed", "core"), None)
    vector = P("fsdp")
    matrix = P("fsdp", None)
    return jax.shard_map(
        body,
        mesh=split,
        in_specs=(
            field,
            P("fsdp", ("zed", "core")),
            vector,
            matrix,
            matrix,
            matrix,
            matrix,
            vector,
            matrix,
            matrix,
            matrix,
            field,
        ),
        out_specs=(
            field,
            field,
            vector,
            matrix,
            matrix,
            matrix,
            matrix,
            vector,
            matrix,
            matrix,
            matrix,
        ),
        check_vma=False,
    )
```

time: 3230 us -> 1110 us (0.34)
  waiting for transfers between devices: 2670 us -> 456 us
  matrix products: 305 us -> 57.2 us
  Pallas kernels: 0 us -> 217 us
  starting transfers between devices: 26.5 us -> 171 us
  other arithmetic: 88.7 us -> 134 us
  blocking collectives: 42.5 us -> 0 us
    all_gather x7 -> x1, waiting for transfers between devices: 954 us -> 7.07 us  [body(): cot_abs = lax.all_gather(cot_abs, 'fsdp', axis=0, tiled=True)]
    unnamed x18 -> x1, waiting for transfers between devices: 880 us -> 0.02 us
    psum x1 -> x0, waiting for transfers between devices: 547 us -> none  [body(): lax.psum(sum_q.astype(jnp.bfloat16), 'seq').astype(jnp.float32)]
    ppermute x0 -> x90, waiting for transfers between devices: none -> 398 us  [the longest x27 194 us: z_move(): return lax.ppermute(field, 'zed', z_steps()[stage][0])]
    dot_general x33 -> x18, matrix products: 305 us -> 57.2 us  [the longest x13 49.4 us: t_dot(): lax.dot_general(left, right, (((0,), (0,)), ((), ())), preferred_element_...]
    pallas_call x0 -> x20, Pallas kernels: none -> 217 us  [the longest x5 42.8 us: spread(): pl.pallas_call(spread_kernel, grid_spec=pltpu.PrefetchScalarGridSpec(num_...]
    reduce_scatter x4 -> x0, waiting for transfers between devices: 184 us -> none  [the longest x1 90.4 us: body(): lax.psum_scatter(grad_query.astype(jnp.bfloat16), 'fsdp', scatter_dimensi...]
    ppermute x0 -> x90, starting transfers between devices: none -> 145 us  [the longest x27 83.6 us: z_move(): return lax.ppermute(field, 'zed', z_steps()[stage][0])]
  transfers between devices with their start and end apart: 21 -> 97, of which waited for: 18 -> 43; matrix products, arithmetic and copies ran while one was open for 7% -> 19% of each run, Pallas kernels for 0% -> 17%
where the time goes in v1:
time: 1110 us; the launch traced here: 1100 us
  waiting for transfers between devices  456 us (41%)
  Pallas kernels  217 us (20%)
  starting transfers between devices  171 us (15%)
  other arithmetic  134 us (12%)
  matrix products  57.2 us (5%)
  local copies, waits for them, and re-layouts  46 us (4%)
  between operations  16.4 us (1%)
    ppermute x27, waiting for transfers between devices, z_move(): return lax.ppermute(field, 'zed', z_steps()[stage][0])  194 us
    ppermute x31, waiting for transfers between devices, xor_send(): return lax.ppermute(field, 'fsdp', [(i, i ^ bit) for i in range(count)])  147 us
    ppermute x27, starting transfers between devices, z_move(): return lax.ppermute(field, 'zed', z_steps()[stage][0])  83.6 us
    convert_element_type x32, other arithmetic, add_low(): return (left.astype(F32) + right.astype(F32)).astype(BF)  69.3 us
    all_to_all x6, waiting for transfers between devices, exchange(): lax.all_to_all(field, 'fsdp', split_axis=0, concat_axis=0, tiled=True)  51 us
    dot_general x13, matrix products, t_dot(): lax.dot_general(left, right, (((0,), (0,)), ((), ())), preferred_element_...  49.4 us
    pallas_call x5, Pallas kernels, spread(): pl.pallas_call(spread_kernel, grid_spec=pltpu.PrefetchScalarGridSpec(num_...  42.8 us
    pallas_call x2, Pallas kernels, feed(): pl.pallas_call(feed_kernel, grid_spec=pltpu.PrefetchScalarGridSpec(num_sc...  42.4 us
  transfers between devices with their start and end apart: 97, of which 43 were waited for; matrix products, arithmetic and copies ran while one was open for 19% of the time, Pallas kernels for 17%

profile of v1, /device:TPU:0, one launch (start us, length us, event | category | flops | bytes accessed | tf_op | source)
XLA Modules:
  0.0 1098.9 jit_solution(9307684513219614054)
XLA Ops:
  50.1 11.9 %collective-permute-done.3 = bf16[128,2048]{1,0:T(8,128)(2,1)S(1)} collective-permute-done((bf16[128,2048]{1,0:T(8,128)(2,1)S(1)}, bf16[128,2048]{1,0:T(8,128)(2,1)S(1)}, u32[]{:S(2)}, u32[]{:S(2)}) %collective-permute-start.3) | collective-permute-done | bytes 524320 | tf_op jit(solution)/shard_map/ppermute | solution.py:27
  93.9 22.0 %all-to-all-done.1 = bf16[4,512,1024]{2,1,0:T(8,128)(2,1)} async-done(((bf16[4,512,1024]{2,1,0:T(8,128)(2,1)}), bf16[4,512,1024]{2,1,0:T(8,128)(2,1)}, u32[]{:S(2)}, u32[]{:S(2)}) %all-to-all-start.1) | async-done | bytes 4194336 | tf_op jit(solution)/shard_map/all_to_all | solution.py:727
  169.1 19.1 %attend.1 = (bf16[1024,512]{1,0:T(8,128)(2,1)}, f32[8,2,512,1]{3,2,1,0:T(8,128)}) custom-call(s32[2]{0:T(128)} %pad_add_fusion.place_ref, bf16[1024,512]{1,0:T(8,128)(2,1)} %pad_maximum_fusion.5.q_ref, bf16[1024,256]{1,0:T(8,128)(2,1)} %pad_maximum_fusion.16.refs_0_, bf16[1024,256]{1,0:T(8,128)(2,1)} %collective-permute-done.8.refs_1_, ...), custom_call_target="tpu_custom_call" | custom-call | flops 2147483648 | bytes 4194304 | tf_op jit(solution)/shard_map/attend/pallas_call | solution.py:632
  206.8 21.6 %collective-permute-done.18 = bf16[256,2048]{1,0:T(8,128)(2,1)S(1)} collective-permute-done((bf16[256,2048]{1,0:T(8,128)(2,1)S(1)}, bf16[256,2048]{1,0:T(8,128)(2,1)S(1)}, u32[]{:S(2)}, u32[]{:S(2)}) %collective-permute-start.18) | collective-permute-done | bytes 1048608 | tf_op jit(solution)/shard_map/ppermute | solution.py:27
  233.6 21.0 %collective-permute-done.20 = bf16[256,2048]{1,0:T(8,128)(2,1)S(1)} collective-permute-done((bf16[256,2048]{1,0:T(8,128)(2,1)S(1)}, bf16[256,2048]{1,0:T(8,128)(2,1)S(1)}, u32[]{:S(2)}, u32[]{:S(2)}) %collective-permute-start.20) | collective-permute-done | bytes 1048608 | tf_op jit(solution)/shard_map/ppermute | solution.py:27
  279.2 20.9 %feed.2 = (bf16[1024,1024]{1,0:T(8,128)(2,1)}, bf16[1024,1024]{1,0:T(8,128)(2,1)}, bf16[1024,1024]{1,0:T(8,128)(2,1)}) custom-call(s32[2]{0:T(128)} %pad_add_fusion.place_ref, bf16[1024,2048]{1,0:T(8,128)(2,1)} %copy-done.41, bf16[1024,2048]{1,0:T(8,128)(2,1)} %pad_maximum_fusion.cot_ref, bf16[2048,1024]{1,0:T(8,128)(2,1)} %bitcast.11.w0_ref.w00, ...), custom_call_target="tpu_custom_call" | custom-call | flops 3221225472 | bytes 6815744 | tf_op jit(solution)/shard_map/feed/pallas_call | solution.py:409
  300.1 21.5 %feed.3 = (bf16[1024,1024]{1,0:T(8,128)(2,1)}, bf16[1024,1024]{1,0:T(8,128)(2,1)}, bf16[1024,1024]{1,0:T(8,128)(2,1)}) custom-call(s32[2]{0:T(128)} %pad_add_fusion.place_ref, bf16[1024,2048]{1,0:T(8,128)(2,1)} %copy-done.41, bf16[1024,2048]{1,0:T(8,128)(2,1)} %pad_maximum_fusion.cot_ref, bf16[2048,1024]{1,0:T(8,128)(2,1)} %collective-permute-done.24.w0_ref.w01, ...), custom_call_target="tpu_custom_call" | custom-call | flops 3221225472 | bytes 6815744 | tf_op jit(solution)/shard_map/feed/pallas_call | solution.py:409
  327.6 13.7 %unfeed.3 = bf16[512,2048]{1,0:T(8,128)(2,1)S(1)} custom-call(s32[2]{0:T(128)S(1)} %copy-done.31, bf16[1024,1024]{1,0:T(8,128)(2,1)S(1)} %copy-done.7, bf16[1024,1024]{1,0:T(8,128)(2,1)} %get-tuple-element.143.dg1, bf16[1024,1024]{1,0:T(8,128)(2,1)} %get-tuple-element.144.du0, bf16[1024,1024]{1,0:T(8,128)(2,1)} %get-tuple-element.145.du1, ...), custom_call_target="tpu_custom_call" | custom-call | flops 2147483648 | bytes 5767168 | tf_op jit(solution)/shard_map/unfeed/pallas_call | solution.py:463
  347.9 14.1 %unfeed.2 = bf16[512,2048]{1,0:T(8,128)(2,1)S(1)} custom-call(s32[2]{0:T(128)S(1)} %copy-done.31, bf16[1024,1024]{1,0:T(8,128)(2,1)S(1)} %copy-done.7, bf16[1024,1024]{1,0:T(8,128)(2,1)} %get-tuple-element.143.dg1, bf16[1024,1024]{1,0:T(8,128)(2,1)} %get-tuple-element.144.du0, bf16[1024,1024]{1,0:T(8,128)(2,1)} %get-tuple-element.145.du1, ...), custom_call_target="tpu_custom_call" | custom-call | flops 2147483648 | bytes 5767168 | tf_op jit(solution)/shard_map/unfeed/pallas_call | solution.py:463
  378.8 12.5 %lower.1 = bf16[1024,2048]{1,0:T(8,128)(2,1)} custom-call(s32[2]{0:T(128)S(1)} %copy-done.31, bf16[1024,1024]{1,0:T(8,128)(2,1)S(1)} %copy-done.16, bf16[1024,1024]{1,0:T(8,128)(2,1)S(1)} %copy-done.18, bf16[2048,2048]{1,0:T(8,128)(2,1)} %w1.1, bf16[2048,2048]{1,0:T(8,128)(2,1)} %w1.1), custom_call_target="tpu_custom_call" | custom-call | flops 2147483648 | bytes 4194304 | tf_op jit(solution)/shard_map/lower/pallas_call | solution.py:493
  399.9 14.9 %collective-permute-done.31 = bf16[1024,1024]{1,0:T(8,128)(2,1)} collective-permute-done((bf16[1024,1024]{1,0:T(8,128)(2,1)}, bf16[1024,1024]{1,0:T(8,128)(2,1)}, u32[]{:S(2)}, u32[]{:S(2)}) %collective-permute-start.31) | collective-permute-done | bytes 2097184 | tf_op jit(solution)/shard_map/ppermute | solution.py:86
  460.4 17.0 %collective-permute-done.33 = bf16[256,2048]{1,0:T(8,128)(2,1)S(1)} collective-permute-done((bf16[256,2048]{1,0:T(8,128)(2,1)S(1)}, bf16[256,2048]{1,0:T(8,128)(2,1)S(1)}, u32[]{:S(2)}, u32[]{:S(2)}) %collective-permute-start.33) | collective-permute-done | bytes 1048608 | tf_op jit(solution)/shard_map/ppermute | solution.py:27
  505.4 38.5 %attend_back.1 = (bf16[1024,512]{1,0:T(8,128)(2,1)}, bf16[1024,256]{1,0:T(8,128)(2,1)}, bf16[1024,256]{1,0:T(8,128)(2,1)}, bf16[1024,256]{1,0:T(8,128)(2,1)}, bf...) custom-call(s32[2]{0:T(128)} %pad_add_fusion.place_ref, ...), custom_call_target="tpu_custom_call" | custom-call | flops 4294967296 | bytes 6291456 | tf_op jit(solution)/shard_map/attend_back/pallas_call | solution.py:656
  561.5 20.9 %collective-permute-done.47 = bf16[1024,256]{1,0:T(8,128)(2,1)S(1)} collective-permute-done((bf16[1024,256]{1,0:T(8,128)(2,1)S(1)}, bf16[1024,256]{1,0:T(8,128)(2,1)S(1)}, u32[]{:S(2)}, u32[]{:S(2)}) %collective-permute-start.47) | collective-permute-done | bytes 524320 | tf_op jit(solution)/shard_map/ppermute | solution.py:136
  653.9 12.2 %collective-permute-done.58 = bf16[256,2048]{1,0:T(8,128)(2,1)S(1)} collective-permute-done((bf16[256,2048]{1,0:T(8,128)(2,1)}, bf16[256,2048]{1,0:T(8,128)(2,1)S(1)}, u32[]{:S(2)}, u32[]{:S(2)}) %collective-permute-start.58) | collective-permute-done | bytes 1048608 | tf_op jit(solution)/shard_map/ppermute | solution.py:27
  751.7 13.1 %collective-permute-start.75 = (bf16[256,2048]{1,0:T(8,128)(2,1)S(1)}, bf16[256,2048]{1,0:T(8,128)(2,1)}, u32[]{:S(2)}, u32[]{:S(2)}) collective-permute-start(bf16[256,2048]{1,0:T(8,128)(2,1)S(1)} %add_convert_fusion.21), channel_id=1, source_target_pairs={{0,2},{6,4},{1,3},{7,5},{8,10},{14,12},{9,11},{15,13},{16,18},{22,... | collective-permute-start | bytes 3145736 | tf_op jit(solution)/shard_map/ppermute | solution.py:86
  776.7 10.5 collective-permute-done.67
  819.6 16.6 %all-to-all-done.3.own_ref = bf16[4,512,1024]{2,1,0:T(8,128)(2,1)} async-done(((bf16[4,512,1024]{2,1,0:T(8,128)(2,1)}), bf16[4,512,1024]{2,1,0:T(8,128)(2,1)}, u32[]{:S(2)}, u32[]{:S(2)}) %all-to-all-start.3) | async-done | bytes 4194336 | tf_op jit(solution)/shard_map/all_to_all | solution.py:727
  838.2 10.6 collective-permute-start.73
  851.5 13.4 %spread.5 = f32[512,8192]{1,0:T(8,128)} custom-call(s32[1]{0:T(128)} %bitcast.1.place_ref, bf16[4,512,1024]{2,1,0:T(8,128)(2,1)} %all-to-all-done.2.own_ref, bf16[4,512,1024]{2,1,0:T(8,128)(2,1)} %collective-permute-done.62.other_ref), custom_call_target="tpu_custom_call" | custom-call | flops 524288 | bytes 6291456 | tf_op jit(solution)/shard_map/spread/pallas_call | solution.py:697
  872.2 16.5 %collective-permute-done.77 = bf16[4,256,384]{2,1,0:T(8,128)(2,1)S(1)} collective-permute-done((bf16[4,256,384]{2,1,0:T(8,128)(2,1)S(1)}, bf16[4,256,384]{2,1,0:T(8,128)(2,1)S(1)}, u32[]{:S(2)}, u32[]{:S(2)}) %collective-permute-start.77) | collective-permute-done | bytes 786464 | tf_op jit(solution)/shard_map/ppermute | solution.py:86
  900.2 13.4 %spread.6 = f32[512,8192]{1,0:T(8,128)} custom-call(s32[1]{0:T(128)} %bitcast.1.place_ref, bf16[4,512,1024]{2,1,0:T(8,128)(2,1)} %all-to-all-done.3.own_ref, bf16[4,512,1024]{2,1,0:T(8,128)(2,1)} %collective-permute-done.78.other_ref), custom_call_target="tpu_custom_call" | custom-call | flops 524288 | bytes 6291456 | tf_op jit(solution)/shard_map/spread/pallas_call | solution.py:697
  913.6 27.6 %collective-permute-done.79 = bf16[512,2048]{1,0:T(8,128)(2,1)} collective-permute-done((bf16[512,2048]{1,0:T(8,128)(2,1)S(1)}, bf16[512,2048]{1,0:T(8,128)(2,1)}, u32[]{:S(2)}, u32[]{:S(2)}) %collective-permute-start.79) | collective-permute-done | bytes 2097184 | tf_op jit(solution)/shard_map/ppermute | solution.py:86
  954.3 73.2 %collective-permute-done.85 = bf16[4,256,384]{2,1,0:T(8,128)(2,1)} collective-permute-done((bf16[4,256,384]{2,1,0:T(8,128)(2,1)}, bf16[4,256,384]{2,1,0:T(8,128)(2,1)}, u32[]{:S(2)}, u32[]{:S(2)}) %collective-permute-start.85) | collective-permute-done | bytes 786464 | tf_op jit(solution)/shard_map/ppermute | solution.py:86
  (536 shorter events, 605.9 us)
Async XLA Ops:
  64.6 51.4 %all-to-all-start.1 = ((bf16[4,512,1024]{2,1,0:T(8,128)(2,1)}), bf16[4,512,1024]{2,1,0:T(8,128)(2,1)}, u32[]{:S(2)}, u32[]{:S(2)}) async-start(bf16[4,512,1024]{2,1,0:T(8,128)(2,1)} %pick_units.1), calls=%async_computation.1 | async-start | bytes 8388608 | tf_op jit(solution)/shard_map/all_to_all | solution.py:727
  69.4 99.6 %all-gather.2.cloned.1.call-start = ((), (), s32[]{:S(2)}) async-start(), calls=%async_computation.6 | async-start | bytes 5242880 | tf_op jit(solution)/shard_map/all_gather | solution.py:830
  159.5 109.0 %collective-permute-start.23 = (bf16[2048,1024]{1,0:T(8,128)(2,1)}, bf16[2048,1024]{1,0:T(8,128)(2,1)}, u32[]{:S(2)}, u32[]{:S(2)}) collective-permute-start(bf16[2048,1024]{1,0:T(8,128)(2,1)} %bitcast.11.w0_ref.w00), channel_id=1, source_target_pairs={{0,2},{2,0},{4,6},{6,4},{1,3},{3,1},{5,7},{7,5},{8,10},{10,8},{12,... | collective-permute-start | bytes 12582920 | tf_op jit(solution)/shard_map/ppermute | solution.py:827
  378.8 54.4 %collective-permute-start.37 = (bf16[1024,1024]{1,0:T(8,128)(2,1)}, bf16[1024,1024]{1,0:T(8,128)(2,1)}, u32[]{:S(2)}, u32[]{:S(2)}) collective-permute-start(bf16[1024,1024]{1,0:T(8,128)(2,1)} %convolution_convert_fusion.9), channel_id=1, source_target_pairs={{0,1},{1,0},{2,3},{3,2},{4,5},{5,4},{6,7},{7,6},{8,9},{9,8},{10,11... | collective-permute-start | bytes 6291464 | tf_op jit(solution)/shard_map/ppermute | solution.py:31
  433.1 49.0 %collective-permute-start.41 = (bf16[1024,1024]{1,0:T(8,128)(2,1)S(1)}, bf16[1024,1024]{1,0:T(8,128)(2,1)S(1)}, u32[]{:S(2)}, u32[]{:S(2)}) collective-permute-start(bf16[1024,1024]{1,0:T(8,128)(2,1)S(1)} %convolution_convert_fusion.8), channel_id=1, source_target_pairs={{0,1},{1,0},{2,3},{3,2},{4,5},{5,4},{6,7},{7,6},{8,9},{9,8},{10,11... | collective-permute-start | bytes 6291464 | tf_op jit(solution)/shard_map/ppermute | solution.py:31
  435.6 55.7 %collective-permute-start.38 = (bf16[1024,1024]{1,0:T(8,128)(2,1)S(1)}, bf16[1024,1024]{1,0:T(8,128)(2,1)S(1)}, u32[]{:S(2)}, u32[]{:S(2)}) collective-permute-start(bf16[1024,1024]{1,0:T(8,128)(2,1)S(1)} %add_convert_fusion.14), channel_id=1, source_target_pairs={{0,2},{6,4},{1,3},{7,5},{8,10},{14,12},{9,11},{15,13},{16,18},{22,... | collective-permute-start | bytes 6291464 | tf_op jit(solution)/shard_map/ppermute | solution.py:86
  484.5 59.4 %collective-permute-start.42 = (bf16[1024,1024]{1,0:T(8,128)(2,1)}, bf16[1024,1024]{1,0:T(8,128)(2,1)}, u32[]{:S(2)}, u32[]{:S(2)}) collective-permute-start(bf16[1024,1024]{1,0:T(8,128)(2,1)} %add_convert_fusion.11), channel_id=1, source_target_pairs={{0,2},{6,4},{1,3},{7,5},{8,10},{14,12},{9,11},{15,13},{16,18},{22,... | collective-permute-start | bytes 6291464 | tf_op jit(solution)/shard_map/ppermute | solution.py:86
  493.7 57.9 %collective-permute-start.39 = (bf16[1024,1024]{1,0:T(8,128)(2,1)}, bf16[1024,1024]{1,0:T(8,128)(2,1)}, u32[]{:S(2)}, u32[]{:S(2)}) collective-permute-start(bf16[1024,1024]{1,0:T(8,128)(2,1)} %add_convert_fusion.13), channel_id=1, source_target_pairs={{2,0},{4,6},{3,1},{5,7},{10,8},{12,14},{11,9},{13,15},{18,16},{20,... | collective-permute-start | bytes 6291464 | tf_op jit(solution)/shard_map/ppermute | solution.py:86
  497.3 54.3 %collective-permute-start.40 = (bf16[1024,1024]{1,0:T(8,128)(2,1)}, bf16[1024,1024]{1,0:T(8,128)(2,1)}, u32[]{:S(2)}, u32[]{:S(2)}) collective-permute-start(bf16[1024,1024]{1,0:T(8,128)(2,1)} %add_convert_fusion.12), channel_id=1, source_target_pairs={{2,4},{4,2},{3,5},{5,3},{10,12},{12,10},{11,13},{13,11},{18,20},{2... | collective-permute-start | bytes 6291464 | tf_op jit(solution)/shard_map/ppermute | solution.py:86
  590.6 54.5 %collective-permute-start.63 = (bf16[1024,2048]{1,0:T(8,128)(2,1)}, bf16[1024,2048]{1,0:T(8,128)(2,1)}, u32[]{:S(2)}, u32[]{:S(2)}) collective-permute-start(bf16[1024,2048]{1,0:T(8,128)(2,1)} %convolution_convert_fusion), channel_id=1, source_target_pairs={{0,1},{1,0},{2,3},{3,2},{4,5},{5,4},{6,7},{7,6},{8,9},{9,8},{10,11... | collective-permute-start | bytes 12582920 | tf_op jit(solution)/shard_map/ppermute | solution.py:31
  635.0 51.7 %collective-permute-start.61 = (bf16[1024,1024]{1,0:T(8,128)(2,1)S(1)}, bf16[1024,1024]{1,0:T(8,128)(2,1)}, u32[]{:S(2)}, u32[]{:S(2)}) collective-permute-start(bf16[1024,1024]{1,0:T(8,128)(2,1)S(1)} %copy-done.51), channel_id=1, source_target_pairs={{0,2},{6,4},{1,3},{7,5},{8,10},{14,12},{9,11},{15,13},{16,18},{22,... | collective-permute-start | bytes 6291464 | tf_op jit(solution)/shard_map/ppermute | solution.py:86
  666.1 65.6 %collective-permute-start.66 = (bf16[512,2048]{1,0:T(8,128)(2,1)}, bf16[512,2048]{1,0:T(8,128)(2,1)}, u32[]{:S(2)}, u32[]{:S(2)}) collective-permute-start(bf16[512,2048]{1,0:T(8,128)(2,1)} %get-tuple-element.248), channel_id=1, source_target_pairs={{0,2},{6,4},{1,3},{7,5},{8,10},{14,12},{9,11},{15,13},{16,18},{22,... | collective-permute-start | bytes 6291464 | tf_op jit(solution)/shard_map/ppermute | solution.py:86
  698.0 78.7 %collective-permute-start.69 = (bf16[512,2048]{1,0:T(8,128)(2,1)}, bf16[512,2048]{1,0:T(8,128)(2,1)}, u32[]{:S(2)}, u32[]{:S(2)}) collective-permute-start(bf16[512,2048]{1,0:T(8,128)(2,1)} %get-tuple-element.247), channel_id=1, source_target_pairs={{0,2},{6,4},{1,3},{7,5},{8,10},{14,12},{9,11},{15,13},{16,18},{22,... | collective-permute-start | bytes 6291464 | tf_op jit(solution)/shard_map/ppermute | solution.py:86
  714.9 53.1 %all-to-all-start.2 = ((bf16[4,512,1024]{2,1,0:T(8,128)(2,1)}), bf16[4,512,1024]{2,1,0:T(8,128)(2,1)}, u32[]{:S(2)}, u32[]{:S(2)}) async-start(bf16[4,512,1024]{2,1,0:T(8,128)(2,1)} %bitcast.123), calls=%async_computation.2 | async-start | bytes 8388608 | tf_op jit(solution)/shard_map/all_to_all | solution.py:727
  751.7 67.8 %collective-permute-start.75 = (bf16[256,2048]{1,0:T(8,128)(2,1)S(1)}, bf16[256,2048]{1,0:T(8,128)(2,1)}, u32[]{:S(2)}, u32[]{:S(2)}) collective-permute-start(bf16[256,2048]{1,0:T(8,128)(2,1)S(1)} %add_convert_fusion.21), channel_id=1, source_target_pairs={{0,2},{6,4},{1,3},{7,5},{8,10},{14,12},{9,11},{15,13},{16,18},{22,... | collective-permute-start | bytes 3145736 | tf_op jit(solution)/shard_map/ppermute | solution.py:86
  768.0 82.2 %collective-permute-start.62 = (bf16[4,512,1024]{2,1,0:T(8,128)(2,1)}, bf16[4,512,1024]{2,1,0:T(8,128)(2,1)}, u32[]{:S(2)}, u32[]{:S(2)}) collective-permute-start(bf16[4,512,1024]{2,1,0:T(8,128)(2,1)} %all-to-all-done.2.own_ref), channel_id=1, source_target_pairs={{0,1},{1,0},{2,3},{3,2},{4,5},{5,4},{6,7},{7,6},{8,9},{9,8},{10,11... | collective-permute-start | bytes 12582920 | tf_op jit(solution)/shard_map/ppermute | solution.py:31
  811.4 77.2 %collective-permute-start.70 = (bf16[512,2048]{1,0:T(8,128)(2,1)}, bf16[512,2048]{1,0:T(8,128)(2,1)}, u32[]{:S(2)}, u32[]{:S(2)}) collective-permute-start(bf16[512,2048]{1,0:T(8,128)(2,1)} %add_convert_fusion.3), channel_id=1, source_target_pairs={{2,0},{4,6},{3,1},{5,7},{10,8},{12,14},{11,9},{13,15},{18,16},{20,... | collective-permute-start | bytes 6291464 | tf_op jit(solution)/shard_map/ppermute | solution.py:86
  816.6 72.1 %collective-permute-start.71 = (bf16[512,2048]{1,0:T(8,128)(2,1)}, bf16[512,2048]{1,0:T(8,128)(2,1)}, u32[]{:S(2)}, u32[]{:S(2)}) collective-permute-start(bf16[512,2048]{1,0:T(8,128)(2,1)} %add_convert_fusion.2), channel_id=1, source_target_pairs={{2,4},{4,2},{3,5},{5,3},{10,12},{12,10},{11,13},{13,11},{18,20},{2... | collective-permute-start | bytes 6291464 | tf_op jit(solution)/shard_map/ppermute | solution.py:86
  836.3 63.9 %collective-permute-start.78 = (bf16[4,512,1024]{2,1,0:T(8,128)(2,1)}, bf16[4,512,1024]{2,1,0:T(8,128)(2,1)}, u32[]{:S(2)}, u32[]{:S(2)}) collective-permute-start(bf16[4,512,1024]{2,1,0:T(8,128)(2,1)} %all-to-all-done.3.own_ref), channel_id=1, source_target_pairs={{0,1},{1,0},{2,3},{3,2},{4,5},{5,4},{6,7},{7,6},{8,9},{9,8},{10,11... | collective-permute-start | bytes 12582920 | tf_op jit(solution)/shard_map/ppermute | solution.py:31
  891.8 49.4 %collective-permute-start.79 = (bf16[512,2048]{1,0:T(8,128)(2,1)S(1)}, bf16[512,2048]{1,0:T(8,128)(2,1)}, u32[]{:S(2)}, u32[]{:S(2)}) collective-permute-start(bf16[512,2048]{1,0:T(8,128)(2,1)S(1)} %add_convert_fusion.1), channel_id=1, source_target_pairs={{2,0},{4,6},{3,1},{5,7},{10,8},{12,14},{11,9},{13,15},{18,16},{20,... | collective-permute-start | bytes 6291464 | tf_op jit(solution)/shard_map/ppermute | solution.py:86
  942.7 84.8 %collective-permute-start.83 = (bf16[4,256,512]{2,1,0:T(8,128)(2,1)S(1)}, bf16[4,256,512]{2,1,0:T(8,128)(2,1)}, u32[]{:S(2)}, u32[]{:S(2)}) collective-permute-start(bf16[4,256,512]{2,1,0:T(8,128)(2,1)S(1)} %add_convert_fusion.18), channel_id=1, source_target_pairs={{2,0},{4,6},{3,1},{5,7},{10,8},{12,14},{11,9},{13,15},{18,16},{20,... | collective-permute-start | bytes 3145736 | tf_op jit(solution)/shard_map/ppermute | solution.py:86
  950.2 132.3 %collective-permute-start.89 = (bf16[1024,2048]{1,0:T(8,128)(2,1)}, bf16[1024,2048]{1,0:T(8,128)(2,1)}, u32[]{:S(2)}, u32[]{:S(2)}) collective-permute-start(bf16[1024,2048]{1,0:T(8,128)(2,1)} %get-tuple-element.245), channel_id=1, source_target_pairs={{0,1},{1,0},{2,3},{3,2},{4,5},{5,4},{6,7},{7,6},{8,9},{9,8},{10,11... | collective-permute-start | bytes 12582920 | tf_op jit(solution)/shard_map/ppermute | solution.py:31
  950.6 76.8 %collective-permute-start.84 = (bf16[256,2048]{1,0:T(8,128)(2,1)S(1)}, bf16[256,2048]{1,0:T(8,128)(2,1)}, u32[]{:S(2)}, u32[]{:S(2)}) collective-permute-start(bf16[256,2048]{1,0:T(8,128)(2,1)S(1)} %add_convert_fusion.17), channel_id=1, source_target_pairs={{2,0},{4,6},{3,1},{5,7},{10,8},{12,14},{11,9},{13,15},{18,16},{20,... | collective-permute-start | bytes 3145736 | tf_op jit(solution)/shard_map/ppermute | solution.py:86
  953.0 74.5 %collective-permute-start.85 = (bf16[4,256,384]{2,1,0:T(8,128)(2,1)}, bf16[4,256,384]{2,1,0:T(8,128)(2,1)}, u32[]{:S(2)}, u32[]{:S(2)}) collective-permute-start(bf16[4,256,384]{2,1,0:T(8,128)(2,1)} %add_convert_fusion.23), channel_id=1, source_target_pairs={{2,0},{4,6},{3,1},{5,7},{10,8},{12,14},{11,9},{13,15},{18,16},{20,... | collective-permute-start | bytes 2359304 | tf_op jit(solution)/shard_map/ppermute | solution.py:86
  (169 other events, 2735.0 us)
Sparse Core Ops, SparseCore 0:
  116.1 52.9 all-gather.1

commit v2 on v1

--- a/solution.py
+++ b/solution.py
@@ -31,21 +31,22 @@
     return lax.ppermute(field, "core", [(0, 1), (1, 0)])
 
 
-def gather_rel(own):
+def gather_rel(own, tie=()):
     count = lax.axis_size("fsdp")
+    chunks = [own, xor_send(own, 1)]
+    if count == 4:
+        chunks.append(xor_send(own, 2))
+    chunks, tie = lax.optimization_barrier((chunks, tie))
     if count == 4:
         half = own.shape[0] // 2
-        one = xor_send(own, 1)
-        two = xor_send(own, 2)
-        top = xor_send(one[:half], 2)
-        low = xor_send(two[half:], 1)
-        return [own, one, two, jnp.concatenate([top, low], 0)]
-    chunks = [own]
-    bit = 1
+        top = xor_send(chunks[1][:half], 2)
+        low = xor_send(chunks[2][half:], 1)
+        return chunks + [jnp.concatenate([top, low], 0)], tie
+    bit = 2
     while bit < count:
         chunks = chunks + [xor_send(chunk, bit) for chunk in chunks]
         bit *= 2
-    return chunks
+    return chunks, tie
 
 
 def reduce_rel(partials):
@@ -138,7 +139,7 @@
 
 def cost(flops, transcendentals, bytes_accessed):
     return pl.CostEstimate(
-        flops=flops // 4, transcendentals=transcendentals // 4, bytes_accessed=bytes_accessed // 4
+        flops=flops // 32, transcendentals=transcendentals // 32, bytes_accessed=bytes_accessed // 32
     )
 
 
@@ -552,11 +553,19 @@
     row = lax.broadcasted_iota(jnp.int32, own.shape, 0) % span
     col = lax.broadcasted_iota(jnp.int32, own.shape, 1)
     own = jnp.where(col <= row, own, -1e30)
+    depth = rest.shape[1] // span // 2 + 1
     block = lax.broadcasted_iota(jnp.int32, (1, rest.shape[1]), 1) // span + 1
-    have = jnp.where(block == 1, place_ref[1], place_ref[0])
-    need = jnp.where(block == 1, 1, block // 2)
+    have = jnp.where(block == depth, place_ref[1], place_ref[0])
+    need = jnp.where(block == depth, 1, block % depth)
     rest = rest + jnp.where(have >= need, 0.0, -1e30)
     return own, rest
+
+
+def rest_of(kv_refs, cols):
+    sibling = kv_refs[-1]
+    parts = [ref[:, cols] for ref in kv_refs[1:-1]]
+    parts += [sibling[i, :, cols] for i in range(sibling.shape[0])]
+    return jnp.concatenate(parts, 0)
 
 
 def attend_kernel(place_ref, q_ref, *refs):
@@ -567,7 +576,7 @@
         cols = slice(group * LANES, (group + 1) * LANES)
         q_all = stack_heads(q_ref, group, False)
         kv_own = kv_refs[0][:, cols]
-        kv_rest = jnp.concatenate([ref[:, cols] for ref in kv_refs[1:]], 0)
+        kv_rest = rest_of(kv_refs, cols)
         own, rest = logits_of(place_ref, q_all, kv_own, kv_rest, span)
         top = jnp.maximum(jnp.max(own, -1, keepdims=True), jnp.max(rest, -1, keepdims=True))
         own = jnp.exp(own - top)
@@ -592,7 +601,7 @@
         q_all = stack_heads(q_ref, group, False)
         do_all = stack_heads(do_ref, group, True)
         kv_own = kv_refs[0][:, cols]
-        kv_rest = jnp.concatenate([ref[:, cols] for ref in kv_refs[1:]], 0)
+        kv_rest = rest_of(kv_refs, cols)
         own, rest = logits_of(place_ref, q_all, kv_own, kv_rest, span)
         lse = lse_ref[0, group]
         own = jnp.exp(own - lse)
@@ -610,16 +619,21 @@
         dkv_refs[0][:, cols] = dkv.astype(BF)
         dkv = lax.dot_general(d_rest, q_all, flip, preferred_element_type=F32)
         dkv = dkv + lax.dot_general(rest.astype(BF), do_all, flip, preferred_element_type=F32)
-        for i, ref in enumerate(dkv_refs[1:]):
-            ref[:, cols] = dkv[i * span : (i + 1) * span].astype(BF)
+        for i in range(count - 2):
+            dkv_refs[i + 1][:, cols] = dkv[i * span : (i + 1) * span].astype(BF)
+        for i in range(count - 1):
+            start = (count - 2 + i) * span
+            dkv_refs[-1][i, :, cols] = dkv[start : start + span].astype(BF)
 
 
 def attend_specs(q_all, kv_all, span):
-    kv_width = kv_all[0].shape[1]
+    depth, _, kv_width = kv_all[-1].shape
     groups = kv_width // LANES
+    kv_spec = pl.BlockSpec((span, kv_width), lambda i, place: (i, 0))
+    sibling = pl.BlockSpec((depth, span, kv_width), lambda i, place: (0, i, 0))
     return (
         pl.BlockSpec((span, q_all.shape[1]), lambda i, place: (i, 0)),
-        pl.BlockSpec((span, kv_width), lambda i, place: (i, 0)),
+        [kv_spec] * depth + [sibling],
         pl.BlockSpec((1, groups, GROUP * span, 1), lambda i, place: (i, 0, 0, 0)),
         groups,
     )
@@ -627,14 +641,14 @@
 
 def attend(place, q_all, kv_all, span):
     rows = q_all.shape[0]
-    q_spec, kv_spec, lse_spec, groups = attend_specs(q_all, kv_all, span)
-    cells = rows * groups * GROUP * span * len(kv_all)
+    q_spec, kv_specs, lse_spec, groups = attend_specs(q_all, kv_all, span)
+    cells = rows * groups * GROUP * span * (2 * len(kv_all) - 2)
     return pl.pallas_call(
         attend_kernel,
         grid_spec=pltpu.PrefetchScalarGridSpec(
             num_scalar_prefetch=1,
             grid=(rows // span,),
-            in_specs=[q_spec] + [kv_spec] * len(kv_all),
+            in_specs=[q_spec] + kv_specs,
             out_specs=[q_spec, lse_spec],
         ),
         out_shape=(
@@ -651,15 +665,15 @@
 
 def attend_back(place, q_all, do_all, lse, kv_all, span):
     rows = q_all.shape[0]
-    q_spec, kv_spec, lse_spec, groups = attend_specs(q_all, kv_all, span)
-    cells = rows * groups * GROUP * span * len(kv_all)
+    q_spec, kv_specs, lse_spec, groups = attend_specs(q_all, kv_all, span)
+    cells = rows * groups * GROUP * span * (2 * len(kv_all) - 2)
     outs = pl.pallas_call(
         attend_back_kernel,
         grid_spec=pltpu.PrefetchScalarGridSpec(
             num_scalar_prefetch=1,
             grid=(rows // span,),
-            in_specs=[q_spec, q_spec, lse_spec] + [kv_spec] * len(kv_all),
-            out_specs=[q_spec] + [kv_spec] * len(kv_all),
+            in_specs=[q_spec, q_spec, lse_spec] + kv_specs,
+            out_specs=[q_spec] + kv_specs,
         ),
         out_shape=[jax.ShapeDtypeStruct(q_all.shape, BF)]
         + [jax.ShapeDtypeStruct(kv.shape, BF) for kv in kv_all],
@@ -767,7 +781,7 @@
     place = jnp.stack([z, c]).astype(jnp.int32)
 
     x_own = tokens.reshape(rows, width)
-    x_list = gather_rel(x_own)
+    x_list, _ = gather_rel(x_own)
     small = jnp.concatenate(
         [gain_attn.astype(F32), gain_ffn.astype(F32), positions.reshape(rows).astype(F32)]
     ).reshape(-1, LANES)
@@ -816,22 +830,24 @@
     h_all = jnp.concatenate(h_list, 0)
     q_all = jnp.concatenate(q_list, 0)
     stream = jnp.concatenate(kv_list, 0)
-    kv_all = []
-    for step in range(depth):
-        if step == 0:
+    kv_all = [stream]
+    sibling = core_swap(stream)
+    for step in range(1, depth):
+        stream = z_up(stream)
+        if step == 1:
             stream, w0 = lax.optimization_barrier((stream, w0))
-        if step:
-            stream = z_up(stream)
-        kv_all += [stream, core_swap(stream)]
+        kv_all.append(stream)
+    others = core_swap(jnp.stack(kv_all[1:]))
+    kv_all = kv_all + [jnp.concatenate([sibling[None], others], 0)]
     w1, _ = lax.optimization_barrier((w0, stream))
     w1 = lax.ppermute(w1, "zed", [(i, i ^ 1) for i in range(depth)])
     cot_own = grad_out.reshape(rows, width)
     cot_abs, _ = lax.optimization_barrier((cot_own, w0))
     cot_abs = lax.all_gather(cot_abs, "fsdp", axis=0, tiled=True)
-    q_all, cot_abs = lax.optimization_barrier((q_all, cot_abs))
     attended, lse = attend(place, q_all, kv_all, span)
-
     w0 = [w0, core_swap(w0)]
+    attended, cot_abs, w0 = lax.optimization_barrier((attended, cot_abs, w0))
+
 
     def chunk(field, r):
         return field[r * rows : (r + 1) * rows]
@@ -842,8 +858,7 @@
     resid = x_float + branch
     inv_two = lax.rsqrt(jnp.mean(resid * resid, -1, keepdims=True) + norm_eps)
     resid_hat = resid * inv_two
-    h2_list = gather_rel((resid_hat * gain_two).astype(BF))
-    h2_list, w1 = lax.optimization_barrier((h2_list, w1))
+    h2_list, w1 = gather_rel((resid_hat * gain_two).astype(BF), w1)
     h2_all = jnp.concatenate(h2_list, 0)
     w1 = [w1, core_swap(w1)]
 
@@ -854,61 +869,73 @@
     middle = count // 2 * rows
     far = unfeed(place, d_gate, d_up, w0, w1, middle, count * rows)
     near = unfeed(place, d_gate, d_up, w0, w1, 0, middle)
+    def core_sum(own, other):
+        return add_low(own, core_swap(other))
+
+    def halves(left, right):
+        cut = left.shape[1] // 2
+        other = core_swap(t_dot(left, right[1]).astype(BF))
+        return [
+            (t_dot(left[:, rows], right[0]) + other[rows].astype(F32)).astype(BF)
+            for rows in (slice(0, cut), slice(cut, 2 * cut))
+        ]
+
+    near, late = lax.optimization_barrier((near, (h2_all, hidden, cot_all, d_up)))
     d_h2 = reduce_rel([chunk(part, r) for part in (near, far) for r in range(count // 2)])
     down = lower(place, hidden, w_down)
-
-    def core_sum(own, other):
-        return add_low(own, core_swap(other))
-
-    def halves(left, right):
-        cut = left.shape[1] // 2
-        return [
-            core_sum(*[t_dot(left[:, cols], right[side]).astype(BF) for side in range(2)])
-            for cols in (slice(0, cut), slice(cut, 2 * cut))
-        ]
-
     line = Line()
     gate_parts = halves(h2_all, d_gate)
     d_h2, down = line.round((d_h2, down), gate0=gate_parts[0])
-    up_parts = halves(h2_all, d_up)
-    down_part = core_sum(*[t_dot(hidden[side], cot_all).astype(BF) for side in range(2)])
+    h2_late, hidden_late, cot_late, d_up_late = late
+    up_parts = halves(h2_late, d_up_late)
+    down_part = core_sum(*[t_dot(hidden_late[side], cot_late).astype(BF) for side in range(2)])
 
     d_hat_two = d_h2 * gain_two
     part_gain_two = jnp.sum(d_h2 * resid_hat, 0)
     d_resid = cot_own.astype(F32) + inv_two * (
         d_hat_two - resid_hat * jnp.mean(d_hat_two * resid_hat, -1, keepdims=True)
     )
-    d_branch = gather_rel(d_resid.astype(BF))
+    d_branch, _ = gather_rel(d_resid.astype(BF))
     d_branch = line.round(d_branch, gate1=gate_parts[1])
     d_branch = jnp.concatenate(d_branch, 0)
     d_attended = dot_t(d_branch, w_out).astype(BF)
     dq, dkv_all = attend_back(place, q_all, d_attended, lse, kv_all, span)
-    dq, dkv_all = line.round((dq, dkv_all), up0=up_parts[0])
+    dq, dkv_all, down = line.round((dq, dkv_all, down), up0=up_parts[0])
     d_q = unrotate(dq, cos_tab, sin_tab, rows)
+    up_last = up_parts[1]
     tail = None
+    from_sibling = core_swap(dkv_all[-1])
     for step in reversed(range(depth)):
-        here = dkv_all[2 * step].astype(F32) + core_swap(dkv_all[2 * step + 1]).astype(F32)
+        here = dkv_all[step].astype(F32) + from_sibling[step].astype(F32)
         if tail is not None:
-            here = here + z_down(tail).astype(F32)
+            moved = z_down(tail)
+            if step == depth - 2:
+                moved, up_last = line.hold((moved, up_last))
+            here = here + moved.astype(F32)
         tail = here.astype(BF)
     down = reduce_rel([chunk(down, r) for r in range(count)])
     layer_out = (resid + down).astype(BF).reshape(seq_count, span, width)
-    tail, up_last, layer_out = line.hold((tail, up_parts[1], layer_out))
-    d_kv, d_h1_all = unproject(place, d_q, tail, w_own, w_other, cos_tab, sin_tab)
-    d_h1 = reduce_rel([chunk(d_h1_all, r) for r in range(count)])
-    d_h1 = line.round(d_h1, up1=up_last)
-
-    def row_halves(field):
+    tail, layer_out = line.round((tail, layer_out), up1=up_last)
+    def row_pair(field):
         field = field.astype(BF).reshape(count, 2, half_shard, -1)
         own = lax.dynamic_index_in_dim(field, c, 1, keepdims=False)
         other = lax.dynamic_index_in_dim(field, 1 - c, 1, keepdims=False)
-        return core_sum(own, other)
-
-    g_q = row_halves(t_dot(h_all, d_q))
-    g_kv = t_dot(h_all, d_kv)
+        return own, other
+
+    g_q = row_pair(t_dot(h_all, d_q))
     g_out = t_dot(attended, d_branch).astype(BF)
     out_half = q_width // 2
-    g_out = core_sum(take(g_out, c, out_half, 0), take(g_out, 1 - c, out_half, 0))
+    g_out = (take(g_out, c, out_half, 0), take(g_out, 1 - c, out_half, 0))
+    g_qo = core_sum(
+        *[
+            jnp.concatenate([q.reshape(-1, q_width), out.reshape(-1, q_width)], 0)
+            for q, out in zip(g_q, g_out)
+        ]
+    )
+    d_kv, d_h1_all = unproject(place, d_q, tail, w_own, w_other, cos_tab, sin_tab)
+    d_h1 = reduce_rel([chunk(d_h1_all, r) for r in range(count)])
+    g_kv = core_sum(*row_pair(t_dot(h_all, d_kv)))
+    d_h1, g_kv = line.round((d_h1, g_kv), qo=g_qo)
 
     inv_one = lax.rsqrt(jnp.mean(x_float * x_float, -1, keepdims=True) + norm_eps)
     x_hat = x_float * inv_one
@@ -920,7 +947,7 @@
     grad_tokens = d_input.astype(BF).reshape(seq_count, span, width)
     gains = jnp.stack([part_gain_one, part_gain_two], 1)
     gains = jnp.pad(gains, ((0, 0), (0, LANES - 2)))
-    g_kv = row_halves(jnp.concatenate([g_kv, gains], 1))
+    gains = core_sum(*row_pair(gains))
 
     def pair_rows(own):
         return spread(own[None], core_swap(own)[None], c, 0)
@@ -930,29 +957,32 @@
         return spread(own, core_swap(own), c, 1)
 
     cut = ff_half // 2
-    d_h1 = line.round(d_h1, down0=down_part[:cut])
-    d_h1 = line.round(d_h1, down1=down_part[cut:])
+    gains = line.round(gains, kv=g_kv, down0=down_part[:cut])
 
     def whole(name):
         return jnp.concatenate(line.take(name + "0", name + "1"), 0)
 
     grad_gate = to_rows(whole("gate"))
-    grad_gate = line.round(grad_gate, q=g_q, out=g_out, kv=g_kv)
+    grad_gate = line.round(grad_gate, gains=gains, down1=down_part[cut:])
     grad_up = to_rows(whole("up"))
-    grad_gate, grad_up = line.round((grad_gate, grad_up))
-    grad_gate, grad_up = line.round((grad_gate, grad_up))
-    g_q, g_out, g_kv = line.take("q", "out", "kv")
-    grad_down = pair_rows(whole("down"))
-    grad_out_w = pair_rows(g_out)
-    g_q = exchange(g_q)
+    (g_qo,) = line.take("qo")
+    high = count * half_shard
+    grad_out_w = pair_rows(g_qo[high:].reshape(out_half, width))
+    g_q = exchange(g_qo[:high].reshape(count, half_shard, q_width))
     grad_q = spread(g_q, core_swap(g_q), c, 2)
+    grad_up, grad_out_w, grad_q = line.round((grad_up, grad_out_w, grad_q))
+    (g_kv,) = line.take("kv")
     g_kv = exchange(g_kv)
     g_kv = by_core(g_kv, core_swap(g_kv), 0).astype(F32)
-    g_kv = jnp.transpose(g_kv, (0, 2, 1, 3)).reshape(shard, count, -1)
-    gains = jnp.sum(g_kv[:, :, 2 * k_width : 2 * k_width + 2], 1)
-    g_kv = g_kv[:, :, : 2 * k_width].reshape(shard, count * kv_local, 2, HEAD_DIM)
+    g_kv = jnp.transpose(g_kv, (0, 2, 1, 3)).reshape(shard, count * kv_local, 2, HEAD_DIM)
     grad_k = g_kv[:, :, 0].reshape(shard, count * k_width)
     grad_v = g_kv[:, :, 1].reshape(shard, count * k_width)
+    grad_k, grad_v = line.round((grad_k, grad_v))
+    (gains,) = line.take("gains")
+    gains = exchange(gains)[:, :, :2].astype(F32)
+    gains = jnp.sum(gains, 0)
+    gains = by_core(gains, core_swap(gains), 0).reshape(shard, 2)
+    grad_down = pair_rows(whole("down"))
     return (
         layer_out,
         grad_tokens,

time: 1110 us -> 1070 us (0.964)
  waiting for transfers between devices: 456 us -> 384 us
  local copies, waits for them, and re-layouts: 46 us -> 62 us
  matrix products: 57.2 us -> 72.4 us
  starting transfers between devices: 171 us -> 186 us
    ppermute x27, waiting for transfers between devices: 194 us -> 132 us  [z_move(): return lax.ppermute(field, 'zed', z_steps()[stage][0])]
    ppermute x31, waiting for transfers between devices: 147 us -> 111 us  [xor_send(): return lax.ppermute(field, 'fsdp', [(i, i ^ bit) for i in range(count)])]
    ppermute x3, waiting for transfers between devices: 27.5 us -> 62.1 us  [z_down(): return lax.ppermute(field, 'zed', [(i + 1, i) for i in range(count - 1)])]
    all_to_all x6 -> x7, waiting for transfers between devices: 51 us -> 20.5 us  [exchange(): lax.all_to_all(field, 'fsdp', split_axis=0, concat_axis=0, tiled=True)]
    ppermute x1, waiting for transfers between devices: 0.01 us -> 21.2 us  [body(): w1 = lax.ppermute(w1, 'zed', [(i, i ^ 1) for i in range(depth)])]
    ppermute x27, starting transfers between devices: 83.6 us -> 99 us  [z_move(): return lax.ppermute(field, 'zed', z_steps()[stage][0])]
    reshape x0 -> x5, local copies, waits for them, and re-layouts: none -> 13.7 us  [the longest x2 8.01 us: body(): jnp.transpose(g_kv, (0, 2, 1, 3))]
    dot_general x13 -> x11, matrix products: 49.4 us -> 62.4 us  [t_dot(): lax.dot_general(left, right, (((0,), (0,)), ((), ())), preferred_element_...]
  transfers between devices with their start and end apart: 97 -> 92, of which waited for: 43 -> 40; matrix products, arithmetic and copies ran while one was open for 19% -> 20% of each run, Pallas kernels for 17% -> 17%
where the time goes in v2:
time: 1070 us; the launch traced here: 1060 us
  waiting for transfers between devices  384 us (36%)
  Pallas kernels  216 us (20%)
  starting transfers between devices  186 us (17%)
  other arithmetic  126 us (12%)
  matrix products  72.4 us (7%)
  local copies, waits for them, and re-layouts  62 us (6%)
  between operations  16.4 us (2%)
    ppermute x27, waiting for transfers between devices, z_move(): return lax.ppermute(field, 'zed', z_steps()[stage][0])  132 us
    ppermute x31, waiting for transfers between devices, xor_send(): return lax.ppermute(field, 'fsdp', [(i, i ^ bit) for i in range(count)])  111 us
    ppermute x27, starting transfers between devices, z_move(): return lax.ppermute(field, 'zed', z_steps()[stage][0])  99 us
    convert_element_type x27, other arithmetic, add_low(): return (left.astype(F32) + right.astype(F32)).astype(BF)  62.8 us
    dot_general x11, matrix products, t_dot(): lax.dot_general(left, right, (((0,), (0,)), ((), ())), preferred_element_...  62.4 us
    ppermute x3, waiting for transfers between devices, z_down(): return lax.ppermute(field, 'zed', [(i + 1, i) for i in range(count - 1)])  62.1 us
    pallas_call x2, Pallas kernels, feed(): pl.pallas_call(feed_kernel, grid_spec=pltpu.PrefetchScalarGridSpec(num_sc...  42.1 us
    pallas_call x5, Pallas kernels, spread(): pl.pallas_call(spread_kernel, grid_spec=pltpu.PrefetchScalarGridSpec(num_...  41.5 us
  transfers between devices with their start and end apart: 92, of which 40 were waited for; matrix products, arithmetic and copies ran while one was open for 20% of the time, Pallas kernels for 17%

profile of v2, /device:TPU:0, one launch (start us, length us, event | category | flops | bytes accessed | tf_op | source)
XLA Modules:
  0.0 1062.7 jit_solution(10443537361750266479)
XLA Ops:
  43.2 20.3 %collective-permute-done.3 = bf16[128,2048]{1,0:T(8,128)(2,1)S(1)} collective-permute-done((bf16[128,2048]{1,0:T(8,128)(2,1)S(1)}, bf16[128,2048]{1,0:T(8,128)(2,1)S(1)}, u32[]{:S(2)}, u32[]{:S(2)}) %collective-permute-start.3) | collective-permute-done | bytes 524320 | tf_op jit(solution)/shard_map/ppermute | solution.py:27
  119.7 12.0 %collective-permute-done.9.refs_2_ = bf16[1024,256]{1,0:T(8,128)(2,1)S(1)} collective-permute-done((bf16[1024,256]{1,0:T(8,128)(2,1)}, bf16[1024,256]{1,0:T(8,128)(2,1)S(1)}, u32[]{:S(2)}, u32[]{:S(2)}) %collective-permute-start.9) | collective-permute-done | bytes 524320 | tf_op jit(solution)/shard_map/ppermute | solution.py:132
  154.2 19.1 %attend.1 = (bf16[1024,512]{1,0:T(8,128)(2,1)}, f32[8,2,512,1]{3,2,1,0:T(8,128)}) custom-call(s32[2]{0:T(128)} %pad_add_fusion.place_ref, bf16[1024,512]{1,0:T(8,128)(2,1)} %copy-done.62, bf16[1024,256]{1,0:T(8,128)(2,1)} %copy-done.71, bf16[1024,256]{1,0:T(8,128)(2,1)} %collective-permute-done.8.refs_1_, bf16[1024,256]{1,0:T(8,128)(2,1)} %copy-done.63, ...), custom_call_target="tpu_custom_call" | custom-call | flops 268435456 | bytes 524288 | tf_op jit(solution)/shard_map/attend/pallas_call | solution.py:646
  193.0 21.5 %collective-permute-done.17 = bf16[256,2048]{1,0:T(8,128)(2,1)S(1)} collective-permute-done((bf16[256,2048]{1,0:T(8,128)(2,1)S(1)}, bf16[256,2048]{1,0:T(8,128)(2,1)S(1)}, u32[]{:S(2)}, u32[]{:S(2)}) %collective-permute-start.17) | collective-permute-done | bytes 1048608 | tf_op jit(solution)/shard_map/ppermute | solution.py:27
  221.6 21.2 %collective-permute-done.20.w1_ref.w10 = bf16[2048,1024]{1,0:T(8,128)(2,1)} collective-permute-done((bf16[2048,1024]{1,0:T(8,128)(2,1)}, bf16[2048,1024]{1,0:T(8,128)(2,1)}, u32[]{:S(2)}, u32[]{:S(2)}) %collective-permute-start.20) | collective-permute-done | bytes 4194336 | tf_op jit(solution)/shard_map/ppermute | solution.py:843
  253.6 13.2 %collective-permute-done.21 = bf16[128,2048]{1,0:T(8,128)(2,1)S(1)} collective-permute-done((bf16[128,2048]{1,0:T(8,128)(2,1)S(1)}, bf16[128,2048]{1,0:T(8,128)(2,1)S(1)}, u32[]{:S(2)}, u32[]{:S(2)}) %collective-permute-start.21) | collective-permute-done | bytes 524320 | tf_op jit(solution)/shard_map/ppermute | solution.py:27
  268.9 20.9 %feed.3 = (bf16[1024,1024]{1,0:T(8,128)(2,1)}, bf16[1024,1024]{1,0:T(8,128)(2,1)}, bf16[1024,1024]{1,0:T(8,128)(2,1)}) custom-call(s32[2]{0:T(128)} %pad_add_fusion.place_ref, bf16[1024,2048]{1,0:T(8,128)(2,1)} %copy-done.45, bf16[1024,2048]{1,0:T(8,128)(2,1)} %pad_maximum_fusion.cot_ref, bf16[2048,1024]{1,0:T(8,128)(2,1)} %collective-permute-done.13.w0_ref.w01, ...), custom_call_target="tpu_custom_call" | custom-call | flops 402653184 | bytes 851968 | tf_op jit(solution)/shard_map/feed/pallas_call | solution.py:410
  300.4 21.1 %feed.2 = (bf16[1024,1024]{1,0:T(8,128)(2,1)}, bf16[1024,1024]{1,0:T(8,128)(2,1)}, bf16[1024,1024]{1,0:T(8,128)(2,1)}) custom-call(s32[2]{0:T(128)} %pad_add_fusion.place_ref, bf16[1024,2048]{1,0:T(8,128)(2,1)} %copy-done.45, bf16[1024,2048]{1,0:T(8,128)(2,1)} %pad_maximum_fusion.cot_ref, bf16[2048,1024]{1,0:T(8,128)(2,1)} %bitcast.11.w0_ref.w00, ...), custom_call_target="tpu_custom_call" | custom-call | flops 402653184 | bytes 851968 | tf_op jit(solution)/shard_map/feed/pallas_call | solution.py:410
  323.1 13.7 %unfeed.2 = bf16[512,2048]{1,0:T(8,128)(2,1)S(1)} custom-call(s32[2]{0:T(128)S(1)} %copy-done.38, bf16[1024,1024]{1,0:T(8,128)(2,1)S(1)} %copy-done.7, bf16[1024,1024]{1,0:T(8,128)(2,1)} %get-tuple-element.160.dg1, bf16[1024,1024]{1,0:T(8,128)(2,1)} %get-tuple-element.186.du0, bf16[1024,1024]{1,0:T(8,128)(2,1)} %get-tuple-element.187.du1, ...), custom_call_target="tpu_custom_call" | custom-call | flops 268435456 | bytes 720896 | tf_op jit(solution)/shard_map/unfeed/pallas_call | solution.py:464
  336.9 14.4 %unfeed.3 = bf16[512,2048]{1,0:T(8,128)(2,1)S(1)} custom-call(s32[2]{0:T(128)S(1)} %copy-done.38, bf16[1024,1024]{1,0:T(8,128)(2,1)S(1)} %copy-done.7, bf16[1024,1024]{1,0:T(8,128)(2,1)} %get-tuple-element.160.dg1, bf16[1024,1024]{1,0:T(8,128)(2,1)} %get-tuple-element.186.du0, bf16[1024,1024]{1,0:T(8,128)(2,1)} %get-tuple-element.187.du1, ...), custom_call_target="tpu_custom_call" | custom-call | flops 268435456 | bytes 720896 | tf_op jit(solution)/shard_map/unfeed/pallas_call | solution.py:464
  387.6 12.7 %lower.1 = bf16[1024,2048]{1,0:T(8,128)(2,1)} custom-call(s32[2]{0:T(128)S(1)} %copy-done.38, bf16[1024,1024]{1,0:T(8,128)(2,1)S(1)} %copy-done.18, bf16[1024,1024]{1,0:T(8,128)(2,1)S(1)} %copy-done.19, bf16[2048,2048]{1,0:T(8,128)(2,1)} %w1.1, bf16[2048,2048]{1,0:T(8,128)(2,1)} %w1.1), custom_call_target="tpu_custom_call" | custom-call | flops 268435456 | bytes 524288 | tf_op jit(solution)/shard_map/lower/pallas_call | solution.py:494
  417.3 13.8 %collective-permute-done.29 = bf16[1024,1024]{1,0:T(8,128)(2,1)} collective-permute-done((bf16[1024,1024]{1,0:T(8,128)(2,1)S(1)}, bf16[1024,1024]{1,0:T(8,128)(2,1)}, u32[]{:S(2)}, u32[]{:S(2)}) %collective-permute-start.29) | collective-permute-done | bytes 2097184 | tf_op jit(solution)/shard_map/ppermute | solution.py:87
  497.5 38.6 %attend_back.1 = (bf16[1024,512]{1,0:T(8,128)(2,1)}, bf16[1024,256]{1,0:T(8,128)(2,1)}, bf16[1024,256]{1,0:T(8,128)(2,1)}, bf16[1024,256]{1,0:T(8,128)(2,1)}, bf...) custom-call(s32[2]{0:T(128)} %pad_add_fusion.place_ref, bf16[1024,512]{1,0:T(8,128)(2,1)} %copy-done.62, ...), custom_call_target="tpu_custom_call" | custom-call | flops 536870912 | bytes 786432 | tf_op jit(solution)/shard_map/attend_back/pallas_call | solution.py:670
  567.8 19.8 %collective-permute-done.41 = bf16[1024,256]{1,0:T(8,128)(2,1)S(1)} collective-permute-done((bf16[1024,256]{1,0:T(8,128)(2,1)S(1)}, bf16[1024,256]{1,0:T(8,128)(2,1)S(1)}, u32[]{:S(2)}, u32[]{:S(2)}) %collective-permute-start.41) | collective-permute-done | bytes 524320 | tf_op jit(solution)/shard_map/ppermute | solution.py:137
  610.0 38.5 %collective-permute-done.42 = bf16[1024,256]{1,0:T(8,128)(2,1)S(1)} collective-permute-done((bf16[1024,256]{1,0:T(8,128)(2,1)S(1)}, bf16[1024,256]{1,0:T(8,128)(2,1)S(1)}, u32[]{:S(2)}, u32[]{:S(2)}) %collective-permute-start.42) | collective-permute-done | bytes 524320 | tf_op jit(solution)/shard_map/ppermute | solution.py:137
  709.1 11.8 %collective-permute-done.54 = bf16[256,2048]{1,0:T(8,128)(2,1)} collective-permute-done((bf16[256,2048]{1,0:T(8,128)(2,1)}, bf16[256,2048]{1,0:T(8,128)(2,1)}, u32[]{:S(2)}, u32[]{:S(2)}) %collective-permute-start.54) | collective-permute-done | bytes 1048608 | tf_op jit(solution)/shard_map/ppermute | solution.py:27
  748.8 17.1 %collective-permute-start.63 = (bf16[4,256,256]{2,1,0:T(8,128)(2,1)S(1)}, bf16[4,256,256]{2,1,0:T(8,128)(2,1)S(1)}, u32[]{:S(2)}, u32[]{:S(2)}) collective-permute-start(bf16[4,256,256]{2,1,0:T(8,128)(2,1)S(1)} %fusion.27), channel_id=1, source_target_pairs={{0,2},{6,4},{1,3},{7,5},{8,10},{14,12},{9,11},{15,13},{16,18},{22,... | collective-permute-start | bytes 1572872 | tf_op jit(solution)/shard_map/ppermute | solution.py:87
  788.0 15.1 %collective-permute-done.61 = bf16[1024,1024]{1,0:T(8,128)(2,1)} collective-permute-done((bf16[1024,1024]{1,0:T(8,128)(2,1)}, bf16[1024,1024]{1,0:T(8,128)(2,1)}, u32[]{:S(2)}, u32[]{:S(2)}) %collective-permute-start.61) | collective-permute-done | bytes 2097184 | tf_op jit(solution)/shard_map/ppermute | solution.py:87
  822.0 12.6 %collective-permute-start.71 = (bf16[4,256,128]{2,1,0:T(8,128)(2,1)S(1)}, bf16[4,256,128]{2,1,0:T(8,128)(2,1)S(1)}, u32[]{:S(2)}, u32[]{:S(2)}) collective-permute-start(bf16[4,256,128]{2,1,0:T(8,128)(2,1)S(1)} %fusion.36), channel_id=1, source_target_pairs={{0,2},{6,4},{1,3},{7,5},{8,10},{14,12},{9,11},{15,13},{16,18},{22,... | collective-permute-start | bytes 786440 | tf_op jit(solution)/shard_map/ppermute | solution.py:87
  834.6 13.4 %spread.6 = f32[512,8192]{1,0:T(8,128)} custom-call(s32[1]{0:T(128)} %bitcast.1.place_ref, bf16[4,512,1024]{2,1,0:T(8,128)(2,1)} %all-to-all-done.3.own_ref, bf16[4,512,1024]{2,1,0:T(8,128)(2,1)} %collective-permute-done.67.other_ref), custom_call_target="tpu_custom_call" | custom-call | flops 65536 | bytes 786432 | tf_op jit(solution)/shard_map/spread/pallas_call | solution.py:711
  850.2 22.7 %collective-permute-done.68 = bf16[2048,512]{1,0:T(8,128)(2,1)} collective-permute-done((bf16[2048,512]{1,0:T(8,128)(2,1)S(1)}, bf16[2048,512]{1,0:T(8,128)(2,1)}, u32[]{:S(2)}, u32[]{:S(2)}) %collective-permute-start.68) | collective-permute-done | bytes 2097184 | tf_op jit(solution)/shard_map/ppermute | solution.py:87
  910.6 13.4 %spread.5 = f32[512,8192]{1,0:T(8,128)} custom-call(s32[1]{0:T(128)} %bitcast.1.place_ref, bf16[4,512,1024]{2,1,0:T(8,128)(2,1)} %all-to-all-done.2.own_ref, bf16[4,512,1024]{2,1,0:T(8,128)(2,1)} %collective-permute-done.66.other_ref), custom_call_target="tpu_custom_call" | custom-call | flops 65536 | bytes 786432 | tf_op jit(solution)/shard_map/spread/pallas_call | solution.py:711
  924.0 34.2 %collective-permute-done.75 = bf16[4,256,256]{2,1,0:T(8,128)(2,1)} collective-permute-done((bf16[4,256,256]{2,1,0:T(8,128)(2,1)}, bf16[4,256,256]{2,1,0:T(8,128)(2,1)}, u32[]{:S(2)}, u32[]{:S(2)}) %collective-permute-start.75) | collective-permute-done | bytes 524320 | tf_op jit(solution)/shard_map/ppermute | solution.py:87
  993.0 24.7 %collective-permute-done.80 = bf16[4,256,128]{2,1,0:T(8,128)(2,1)S(1)} collective-permute-done((bf16[4,256,128]{2,1,0:T(8,128)(2,1)}, bf16[4,256,128]{2,1,0:T(8,128)(2,1)S(1)}, u32[]{:S(2)}, u32[]{:S(2)}) %collective-permute-start.80) | collective-permute-done | bytes 262176 | tf_op jit(solution)/shard_map/ppermute | solution.py:87
  (547 shorter events, 580.4 us)
Async XLA Ops:
  69.4 103.9 %all-gather.2.cloned.1.call-start = ((), (), s32[]{:S(2)}) async-start(), calls=%async_computation.7 | async-start | bytes 5242880 | tf_op jit(solution)/shard_map/all_gather | solution.py:846
  116.0 57.3 %collective-permute-start.13 = (bf16[2048,1024]{1,0:T(8,128)(2,1)}, bf16[2048,1024]{1,0:T(8,128)(2,1)}, u32[]{:S(2)}, u32[]{:S(2)}) collective-permute-start(bf16[2048,1024]{1,0:T(8,128)(2,1)} %bitcast.11.w0_ref.w00), channel_id=1, source_target_pairs={{0,1},{1,0},{2,3},{3,2},{4,5},{5,4},{6,7},{7,6},{8,9},{9,8},{10,11... | collective-permute-start | bytes 12582920 | tf_op jit(solution)/shard_map/ppermute | solution.py:31
  149.1 93.7 %collective-permute-start.20 = (bf16[2048,1024]{1,0:T(8,128)(2,1)}, bf16[2048,1024]{1,0:T(8,128)(2,1)}, u32[]{:S(2)}, u32[]{:S(2)}) collective-permute-start(bf16[2048,1024]{1,0:T(8,128)(2,1)} %bitcast.11.w0_ref.w00), channel_id=1, source_target_pairs={{0,2},{2,0},{4,6},{6,4},{1,3},{3,1},{5,7},{7,5},{8,10},{10,8},{12,... | collective-permute-start | bytes 12582920 | tf_op jit(solution)/shard_map/ppermute | solution.py:843
  299.4 77.6 %collective-permute-start.28 = (bf16[2048,1024]{1,0:T(8,128)(2,1)}, bf16[2048,1024]{1,0:T(8,128)(2,1)}, u32[]{:S(2)}, u32[]{:S(2)}) collective-permute-start(bf16[2048,1024]{1,0:T(8,128)(2,1)} %convolution_convert_fusion.2), channel_id=1, source_target_pairs={{0,1},{1,0},{2,3},{3,2},{4,5},{5,4},{6,7},{7,6},{8,9},{9,8},{10,11... | collective-permute-start | bytes 12582920 | tf_op jit(solution)/shard_map/ppermute | solution.py:31
  376.9 60.1 %collective-permute-start.64 = (bf16[1024,2048]{1,0:T(8,128)(2,1)}, bf16[1024,2048]{1,0:T(8,128)(2,1)}, u32[]{:S(2)}, u32[]{:S(2)}) collective-permute-start(bf16[1024,2048]{1,0:T(8,128)(2,1)} %convolution_convert_fusion), channel_id=1, source_target_pairs={{0,1},{1,0},{2,3},{3,2},{4,5},{5,4},{6,7},{7,6},{8,9},{9,8},{10,11... | collective-permute-start | bytes 12582920 | tf_op jit(solution)/shard_map/ppermute | solution.py:31
  407.7 68.5 %collective-permute-start.35 = (bf16[1024,1024]{1,0:T(8,128)(2,1)S(1)}, bf16[1024,1024]{1,0:T(8,128)(2,1)S(1)}, u32[]{:S(2)}, u32[]{:S(2)}) collective-permute-start(bf16[1024,1024]{1,0:T(8,128)(2,1)S(1)} %add_convert_fusion.17), channel_id=1, source_target_pairs={{0,2},{6,4},{1,3},{7,5},{8,10},{14,12},{9,11},{15,13},{16,18},{22,... | collective-permute-start | bytes 6291464 | tf_op jit(solution)/shard_map/ppermute | solution.py:87
  414.6 121.5 %collective-permute-start.39 = (bf16[1024,1024]{1,0:T(8,128)(2,1)}, bf16[1024,1024]{1,0:T(8,128)(2,1)}, u32[]{:S(2)}, u32[]{:S(2)}) collective-permute-start(bf16[1024,1024]{1,0:T(8,128)(2,1)} %add_convert_fusion.14), channel_id=1, source_target_pairs={{0,2},{6,4},{1,3},{7,5},{8,10},{14,12},{9,11},{15,13},{16,18},{22,... | collective-permute-start | bytes 6291464 | tf_op jit(solution)/shard_map/ppermute | solution.py:87
  480.8 56.7 %collective-permute-start.36 = (bf16[1024,1024]{1,0:T(8,128)(2,1)}, bf16[1024,1024]{1,0:T(8,128)(2,1)}, u32[]{:S(2)}, u32[]{:S(2)}) collective-permute-start(bf16[1024,1024]{1,0:T(8,128)(2,1)} %add_convert_fusion.16), channel_id=1, source_target_pairs={{2,0},{4,6},{3,1},{5,7},{10,8},{12,14},{11,9},{13,15},{18,16},{20,... | collective-permute-start | bytes 6291464 | tf_op jit(solution)/shard_map/ppermute | solution.py:87
  482.1 55.4 %collective-permute-start.37 = (bf16[1024,1024]{1,0:T(8,128)(2,1)}, bf16[1024,1024]{1,0:T(8,128)(2,1)}, u32[]{:S(2)}, u32[]{:S(2)}) collective-permute-start(bf16[1024,1024]{1,0:T(8,128)(2,1)} %add_convert_fusion.15), channel_id=1, source_target_pairs={{2,4},{4,2},{3,5},{5,3},{10,12},{12,10},{11,13},{13,11},{18,20},{2... | collective-permute-start | bytes 6291464 | tf_op jit(solution)/shard_map/ppermute | solution.py:87
  560.1 89.9 %collective-permute-start.58 = (bf16[2048,512]{1,0:T(8,128)(2,1)}, bf16[2048,512]{1,0:T(8,128)(2,1)}, u32[]{:S(2)}, u32[]{:S(2)}) collective-permute-start(bf16[2048,512]{1,0:T(8,128)(2,1)} %pad_maximum_fusion.5), channel_id=1, source_target_pairs={{0,1},{1,0},{2,3},{3,2},{4,5},{5,4},{6,7},{7,6},{8,9},{9,8},{10,11... | collective-permute-start | bytes 6291464 | tf_op jit(solution)/shard_map/ppermute | solution.py:31
  587.7 79.0 %collective-permute-start.48 = (bf16[1024,1024]{1,0:T(8,128)(2,1)}, bf16[1024,1024]{1,0:T(8,128)(2,1)}, u32[]{:S(2)}, u32[]{:S(2)}) collective-permute-start(bf16[1024,1024]{1,0:T(8,128)(2,1)} %add_convert_fusion.12), channel_id=1, source_target_pairs={{2,0},{4,6},{3,1},{5,7},{10,8},{12,14},{11,9},{13,15},{18,16},{20,... | collective-permute-start | bytes 6291464 | tf_op jit(solution)/shard_map/ppermute | solution.py:87
  589.0 77.8 %collective-permute-start.49 = (bf16[1024,1024]{1,0:T(8,128)(2,1)}, bf16[1024,1024]{1,0:T(8,128)(2,1)}, u32[]{:S(2)}, u32[]{:S(2)}) collective-permute-start(bf16[1024,1024]{1,0:T(8,128)(2,1)} %add_convert_fusion.11), channel_id=1, source_target_pairs={{2,4},{4,2},{3,5},{5,3},{10,12},{12,10},{11,13},{13,11},{18,20},{2... | collective-permute-start | bytes 6291464 | tf_op jit(solution)/shard_map/ppermute | solution.py:87
  591.0 75.7 %collective-permute-start.50 = (bf16[1024,1024]{1,0:T(8,128)(2,1)}, bf16[1024,1024]{1,0:T(8,128)(2,1)}, u32[]{:S(2)}, u32[]{:S(2)}) collective-permute-start(bf16[1024,1024]{1,0:T(8,128)(2,1)} %add_convert_fusion.13), channel_id=1, source_target_pairs={{0,2},{6,4},{1,3},{7,5},{8,10},{14,12},{9,11},{15,13},{16,18},{22,... | collective-permute-start | bytes 6291464 | tf_op jit(solution)/shard_map/ppermute | solution.py:87
  653.6 80.8 %collective-permute-start.59 = (bf16[2048,512]{1,0:T(8,128)(2,1)}, bf16[2048,512]{1,0:T(8,128)(2,1)}, u32[]{:S(2)}, u32[]{:S(2)}) collective-permute-start(bf16[2048,512]{1,0:T(8,128)(2,1)} %add_convert_fusion.8), channel_id=1, source_target_pairs={{0,2},{6,4},{1,3},{7,5},{8,10},{14,12},{9,11},{15,13},{16,18},{22,... | collective-permute-start | bytes 6291464 | tf_op jit(solution)/shard_map/ppermute | solution.py:87
  703.0 62.9 %all-to-all-start.3 = ((bf16[4,512,1024]{2,1,0:T(8,128)(2,1)}), bf16[4,512,1024]{2,1,0:T(8,128)(2,1)}, u32[]{:S(2)}, u32[]{:S(2)}) async-start(bf16[4,512,1024]{2,1,0:T(8,128)(2,1)} %bitcast.153), calls=%async_computation.3 | async-start | bytes 8388608 | tf_op jit(solution)/shard_map/all_to_all | solution.py:741
  721.0 55.9 %collective-permute-start.65 = (bf16[512,2048]{1,0:T(8,128)(2,1)}, bf16[512,2048]{1,0:T(8,128)(2,1)}, u32[]{:S(2)}, u32[]{:S(2)}) collective-permute-start(bf16[512,2048]{1,0:T(8,128)(2,1)} %get-tuple-element.294), channel_id=1, source_target_pairs={{0,2},{6,4},{1,3},{7,5},{8,10},{14,12},{9,11},{15,13},{16,18},{22,... | collective-permute-start | bytes 6291464 | tf_op jit(solution)/shard_map/ppermute | solution.py:87
  743.9 59.3 %collective-permute-start.61 = (bf16[1024,1024]{1,0:T(8,128)(2,1)}, bf16[1024,1024]{1,0:T(8,128)(2,1)}, u32[]{:S(2)}, u32[]{:S(2)}) collective-permute-start(bf16[1024,1024]{1,0:T(8,128)(2,1)} %add_convert_fusion.7), channel_id=1, source_target_pairs={{2,0},{4,6},{3,1},{5,7},{10,8},{12,14},{11,9},{13,15},{18,16},{20,... | collective-permute-start | bytes 6291464 | tf_op jit(solution)/shard_map/ppermute | solution.py:87
  745.1 58.0 %collective-permute-start.62 = (bf16[2048,512]{1,0:T(8,128)(2,1)}, bf16[2048,512]{1,0:T(8,128)(2,1)}, u32[]{:S(2)}, u32[]{:S(2)}) collective-permute-start(bf16[2048,512]{1,0:T(8,128)(2,1)} %add_convert_fusion.6), channel_id=1, source_target_pairs={{2,4},{4,2},{3,5},{5,3},{10,12},{12,10},{11,13},{13,11},{18,20},{2... | collective-permute-start | bytes 6291464 | tf_op jit(solution)/shard_map/ppermute | solution.py:87
  765.9 56.0 %collective-permute-start.67 = (bf16[4,512,1024]{2,1,0:T(8,128)(2,1)}, bf16[4,512,1024]{2,1,0:T(8,128)(2,1)}, u32[]{:S(2)}, u32[]{:S(2)}) collective-permute-start(bf16[4,512,1024]{2,1,0:T(8,128)(2,1)} %all-to-all-done.3.own_ref), channel_id=1, source_target_pairs={{0,1},{1,0},{2,3},{3,2},{4,5},{5,4},{6,7},{7,6},{8,9},{9,8},{10,11... | collective-permute-start | bytes 12582920 | tf_op jit(solution)/shard_map/ppermute | solution.py:31
  776.9 71.1 %collective-permute-start.72 = (bf16[512,2048]{1,0:T(8,128)(2,1)}, bf16[512,2048]{1,0:T(8,128)(2,1)}, u32[]{:S(2)}, u32[]{:S(2)}) collective-permute-start(bf16[512,2048]{1,0:T(8,128)(2,1)} %get-tuple-element.293), channel_id=1, source_target_pairs={{0,2},{6,4},{1,3},{7,5},{8,10},{14,12},{9,11},{15,13},{16,18},{22,... | collective-permute-start | bytes 6291464 | tf_op jit(solution)/shard_map/ppermute | solution.py:87
  807.4 65.4 %all-to-all-start.2 = ((bf16[4,512,1024]{2,1,0:T(8,128)(2,1)}), bf16[4,512,1024]{2,1,0:T(8,128)(2,1)}, u32[]{:S(2)}, u32[]{:S(2)}) async-start(bf16[4,512,1024]{2,1,0:T(8,128)(2,1)} %bitcast.154), calls=%async_computation.2 | async-start | bytes 8388608 | tf_op jit(solution)/shard_map/all_to_all | solution.py:741
  886.5 71.7 %collective-permute-start.76 = (bf16[512,2048]{1,0:T(8,128)(2,1)}, bf16[512,2048]{1,0:T(8,128)(2,1)}, u32[]{:S(2)}, u32[]{:S(2)}) collective-permute-start(bf16[512,2048]{1,0:T(8,128)(2,1)} %add_convert_fusion.3), channel_id=1, source_target_pairs={{2,0},{4,6},{3,1},{5,7},{10,8},{12,14},{11,9},{13,15},{18,16},{20,... | collective-permute-start | bytes 6291464 | tf_op jit(solution)/shard_map/ppermute | solution.py:87
  887.8 70.5 %collective-permute-start.78 = (bf16[512,2048]{1,0:T(8,128)(2,1)}, bf16[512,2048]{1,0:T(8,128)(2,1)}, u32[]{:S(2)}, u32[]{:S(2)}) collective-permute-start(bf16[512,2048]{1,0:T(8,128)(2,1)} %add_convert_fusion.2), channel_id=1, source_target_pairs={{2,4},{4,2},{3,5},{5,3},{10,12},{12,10},{11,13},{13,11},{18,20},{2... | collective-permute-start | bytes 6291464 | tf_op jit(solution)/shard_map/ppermute | solution.py:87
  897.1 61.2 %collective-permute-start.75 = (bf16[4,256,256]{2,1,0:T(8,128)(2,1)}, bf16[4,256,256]{2,1,0:T(8,128)(2,1)}, u32[]{:S(2)}, u32[]{:S(2)}) collective-permute-start(bf16[4,256,256]{2,1,0:T(8,128)(2,1)} %add_convert_fusion.21), channel_id=1, source_target_pairs={{2,0},{4,6},{3,1},{5,7},{10,8},{12,14},{11,9},{13,15},{18,16},{20,... | collective-permute-start | bytes 1572872 | tf_op jit(solution)/shard_map/ppermute | solution.py:87
  (168 other events, 3045.8 us)
Sparse Core Ops, SparseCore 0:
  116.1 52.9 all-gather.1

commit v3 on v2

--- a/solution.py
+++ b/solution.py
@@ -741,6 +741,11 @@
     return lax.all_to_all(field, "fsdp", split_axis=0, concat_axis=0, tiled=True)
 
 
+def by_chunk(field, f):
+    count = field.shape[0]
+    return [lax.dynamic_index_in_dim(field, f ^ r, 0, keepdims=False) for r in range(count)]
+
+
 def by_core(own, other, axis):
     first = lax.axis_index("core") == 0
     return jnp.stack([jnp.where(first, own, other), jnp.where(first, other, own)], axis)
@@ -854,6 +859,8 @@
 
     branch = [dot(chunk(attended, r), w_out) for r in range(count)]
     branch = reduce_rel([branch[0]] + [part.astype(BF) for part in branch[1:]])
+    cot_all = jnp.concatenate([take(cot_abs, f ^ r, rows, 0) for r in range(count)], 0)
+    branch, cot_all = lax.optimization_barrier((branch, cot_all))
     x_float = x_own.astype(F32)
     resid = x_float + branch
     inv_two = lax.rsqrt(jnp.mean(resid * resid, -1, keepdims=True) + norm_eps)
@@ -862,32 +869,33 @@
     h2_all = jnp.concatenate(h2_list, 0)
     w1 = [w1, core_swap(w1)]
 
-    cot_all = jnp.concatenate([take(cot_abs, f ^ r, rows, 0) for r in range(count)], 0)
-    hidden, d_gate, d_up = zip(
-        *[feed(place, h2_all, cot_all, w0[side], w1[side], w_down, side) for side in range(2)]
-    )
+    def summed(left, right):
+        other = core_swap(t_dot(left, right[1]).astype(BF))
+        return (t_dot(left, right[0]) + other.astype(F32)).astype(BF)
+
+    cut = width // 2
+    fed = [None, feed(place, h2_all, cot_all, w0[1], w1[1], w_down, 1)]
+    h2_late, fed[1] = lax.optimization_barrier((h2_all, fed[1]))
+    fed[0] = feed(place, h2_late, cot_all, w0[0], w1[0], w_down, 0)
+    hidden, d_gate, d_up = zip(*fed)
+    gate0 = summed(h2_all[:, :cut], d_gate)
+    gate0, d_gate, d_up = lax.optimization_barrier((gate0, d_gate, d_up))
     middle = count // 2 * rows
     far = unfeed(place, d_gate, d_up, w0, w1, middle, count * rows)
     near = unfeed(place, d_gate, d_up, w0, w1, 0, middle)
+
     def core_sum(own, other):
         return add_low(own, core_swap(other))
 
-    def halves(left, right):
-        cut = left.shape[1] // 2
-        other = core_swap(t_dot(left, right[1]).astype(BF))
-        return [
-            (t_dot(left[:, rows], right[0]) + other[rows].astype(F32)).astype(BF)
-            for rows in (slice(0, cut), slice(cut, 2 * cut))
-        ]
-
-    near, late = lax.optimization_barrier((near, (h2_all, hidden, cot_all, d_up)))
+    near, late = lax.optimization_barrier((near, (h2_all, hidden, cot_all)))
     d_h2 = reduce_rel([chunk(part, r) for part in (near, far) for r in range(count // 2)])
     down = lower(place, hidden, w_down)
     line = Line()
-    gate_parts = halves(h2_all, d_gate)
-    d_h2, down = line.round((d_h2, down), gate0=gate_parts[0])
-    h2_late, hidden_late, cot_late, d_up_late = late
-    up_parts = halves(h2_late, d_up_late)
+    h2_late, hidden_late, cot_late = late
+    gate1 = summed(h2_late[:, cut:], d_gate)
+    d_h2, down = line.round((d_h2, down), gate0=gate0)
+    up_sum = summed(h2_late, d_up)
+    up_parts = [up_sum[:cut], up_sum[cut:]]
     down_part = core_sum(*[t_dot(hidden_late[side], cot_late).astype(BF) for side in range(2)])
 
     d_hat_two = d_h2 * gain_two
@@ -896,7 +904,7 @@
         d_hat_two - resid_hat * jnp.mean(d_hat_two * resid_hat, -1, keepdims=True)
     )
     d_branch, _ = gather_rel(d_resid.astype(BF))
-    d_branch = line.round(d_branch, gate1=gate_parts[1])
+    d_branch = line.round(d_branch, gate1=gate1)
     d_branch = jnp.concatenate(d_branch, 0)
     d_attended = dot_t(d_branch, w_out).astype(BF)
     dq, dkv_all = attend_back(place, q_all, d_attended, lse, kv_all, span)
@@ -923,6 +931,7 @@
         return own, other
 
     g_q = row_pair(t_dot(h_all, d_q))
+    d_branch, _ = lax.optimization_barrier((d_branch, d_q))
     g_out = t_dot(attended, d_branch).astype(BF)
     out_half = q_width // 2
     g_out = (take(g_out, c, out_half, 0), take(g_out, 1 - c, out_half, 0))
@@ -947,7 +956,9 @@
     grad_tokens = d_input.astype(BF).reshape(seq_count, span, width)
     gains = jnp.stack([part_gain_one, part_gain_two], 1)
     gains = jnp.pad(gains, ((0, 0), (0, LANES - 2)))
-    gains = core_sum(*row_pair(gains))
+    gains = reduce_rel(by_chunk(gains.astype(BF).reshape(count, shard, LANES), f))
+    gains = gains.astype(BF)
+    gains = core_sum(take(gains, c, half_shard, 0), take(gains, 1 - c, half_shard, 0))
 
     def pair_rows(own):
         return spread(own[None], core_swap(own)[None], c, 0)
@@ -979,9 +990,7 @@
     grad_v = g_kv[:, :, 1].reshape(shard, count * k_width)
     grad_k, grad_v = line.round((grad_k, grad_v))
     (gains,) = line.take("gains")
-    gains = exchange(gains)[:, :, :2].astype(F32)
-    gains = jnp.sum(gains, 0)
-    gains = by_core(gains, core_swap(gains), 0).reshape(shard, 2)
+    gains = by_core(gains, core_swap(gains), 0).astype(F32).reshape(shard, LANES)
     grad_down = pair_rows(whole("down"))
     return (
         layer_out,

time: 1070 us -> 1060 us (level)
  waiting for transfers between devices: 384 us -> 359 us
    ppermute x27, waiting for transfers between devices: 132 us -> 96 us  [z_move(): return lax.ppermute(field, 'zed', z_steps()[stage][0])]
    ppermute x31 -> x35, waiting for transfers between devices: 111 us -> 131 us  [xor_send(): return lax.ppermute(field, 'fsdp', [(i, i ^ bit) for i in range(count)])]
    ppermute x3, waiting for transfers between devices: 62.1 us -> 48.6 us  [z_down(): return lax.ppermute(field, 'zed', [(i + 1, i) for i in range(count - 1)])]
    ppermute x31 -> x35, starting transfers between devices: 35.1 us -> 40.3 us  [xor_send(): return lax.ppermute(field, 'fsdp', [(i, i ^ bit) for i in range(count)])]
    all_to_all x7 -> x6, waiting for transfers between devices: 20.5 us -> 25.4 us  [exchange(): lax.all_to_all(field, 'fsdp', split_axis=0, concat_axis=0, tiled=True)]
    all_to_all x7 -> x6, starting transfers between devices: 30.4 us -> 27.2 us  [exchange(): lax.all_to_all(field, 'fsdp', split_axis=0, concat_axis=0, tiled=True)]
    unnamed x219 -> x231, local copies, waits for them, and re-layouts: 31 us -> 33.1 us
    convert_element_type x27 -> x28, other arithmetic: 62.8 us -> 62.9 us  [add_low(): return (left.astype(F32) + right.astype(F32)).astype(BF)]
  transfers between devices with their start and end apart: 92 -> 96, of which waited for: 40 -> 43; matrix products, arithmetic and copies ran while one was open for 20% -> 20% of each run, Pallas kernels for 17% -> 16%
where the time goes in v3:
time: 1060 us; the launch traced here: 1040 us
  waiting for transfers between devices  359 us (34%)
  Pallas kernels  217 us (20%)
  starting transfers between devices  191 us (18%)
  other arithmetic  123 us (12%)
  matrix products  69.3 us (7%)
  local copies, waits for them, and re-layouts  68.7 us (6%)
  between operations  16.3 us (2%)
    ppermute x35, waiting for transfers between devices, xor_send(): return lax.ppermute(field, 'fsdp', [(i, i ^ bit) for i in range(count)])  131 us
    ppermute x27, starting transfers between devices, z_move(): return lax.ppermute(field, 'zed', z_steps()[stage][0])  102 us
    ppermute x27, waiting for transfers between devices, z_move(): return lax.ppermute(field, 'zed', z_steps()[stage][0])  96 us
    convert_element_type x28, other arithmetic, add_low(): return (left.astype(F32) + right.astype(F32)).astype(BF)  62.9 us
    dot_general x11, matrix products, t_dot(): lax.dot_general(left, right, (((0,), (0,)), ((), ())), preferred_element_...  60.4 us
    ppermute x3, waiting for transfers between devices, z_down(): return lax.ppermute(field, 'zed', [(i + 1, i) for i in range(count - 1)])  48.6 us
    pallas_call x2, Pallas kernels, feed(): pl.pallas_call(feed_kernel, grid_spec=pltpu.PrefetchScalarGridSpec(num_sc...  41.8 us
    pallas_call x5, Pallas kernels, spread(): pl.pallas_call(spread_kernel, grid_spec=pltpu.PrefetchScalarGridSpec(num_...  41.5 us
  transfers between devices with their start and end apart: 96, of which 43 were waited for; matrix products, arithmetic and copies ran while one was open for 20% of the time, Pallas kernels for 16%

profile of v3, /device:TPU:0, one launch (start us, length us, event | category | flops | bytes accessed | tf_op | source)
XLA Modules:
  0.0 1044.3 jit_solution(12065989061779220106)
XLA Ops:
  43.2 20.3 %collective-permute-done.3 = bf16[128,2048]{1,0:T(8,128)(2,1)S(1)} collective-permute-done((bf16[128,2048]{1,0:T(8,128)(2,1)S(1)}, bf16[128,2048]{1,0:T(8,128)(2,1)S(1)}, u32[]{:S(2)}, u32[]{:S(2)}) %collective-permute-start.3) | collective-permute-done | bytes 524320 | tf_op jit(solution)/shard_map/ppermute | solution.py:27
  119.7 12.0 %collective-permute-done.9.refs_2_ = bf16[1024,256]{1,0:T(8,128)(2,1)S(1)} collective-permute-done((bf16[1024,256]{1,0:T(8,128)(2,1)}, bf16[1024,256]{1,0:T(8,128)(2,1)S(1)}, u32[]{:S(2)}, u32[]{:S(2)}) %collective-permute-start.9) | collective-permute-done | bytes 524320 | tf_op jit(solution)/shard_map/ppermute | solution.py:132
  154.1 19.1 %attend.1 = (bf16[1024,512]{1,0:T(8,128)(2,1)}, f32[8,2,512,1]{3,2,1,0:T(8,128)}) custom-call(s32[2]{0:T(128)} %pad_add_fusion.place_ref, bf16[1024,512]{1,0:T(8,128)(2,1)} %copy-done.66, bf16[1024,256]{1,0:T(8,128)(2,1)} %copy-done.72, bf16[1024,256]{1,0:T(8,128)(2,1)} %collective-permute-done.8.refs_1_, bf16[1024,256]{1,0:T(8,128)(2,1)} %copy-done.67, ...), custom_call_target="tpu_custom_call" | custom-call | flops 268435456 | bytes 524288 | tf_op jit(solution)/shard_map/attend/pallas_call | solution.py:646
  198.9 16.3 %collective-permute-done.17 = bf16[256,2048]{1,0:T(8,128)(2,1)} collective-permute-done((bf16[256,2048]{1,0:T(8,128)(2,1)}, bf16[256,2048]{1,0:T(8,128)(2,1)}, u32[]{:S(2)}, u32[]{:S(2)}) %collective-permute-start.17) | collective-permute-done | bytes 1048608 | tf_op jit(solution)/shard_map/ppermute | solution.py:27
  222.8 20.0 %collective-permute-done.20.w1_ref.w10 = bf16[2048,1024]{1,0:T(8,128)(2,1)} collective-permute-done((bf16[2048,1024]{1,0:T(8,128)(2,1)}, bf16[2048,1024]{1,0:T(8,128)(2,1)}, u32[]{:S(2)}, u32[]{:S(2)}) %collective-permute-start.20) | collective-permute-done | bytes 4194336 | tf_op jit(solution)/shard_map/ppermute | solution.py:848
  263.7 20.8 %feed.2 = (bf16[1024,1024]{1,0:T(8,128)(2,1)}, bf16[1024,1024]{1,0:T(8,128)(2,1)}, bf16[1024,1024]{1,0:T(8,128)(2,1)}) custom-call(s32[2]{0:T(128)} %pad_add_fusion.place_ref, bf16[1024,2048]{1,0:T(8,128)(2,1)} %constant_dynamic-update-slice_fusion.8.h_ref, bf16[1024,2048]{1,0:T(8,128)(2,1)} %pad_maximum_fusion.cot_ref, ...), custom_call_target="tpu_custom_call" | custom-call | flops 402653184 | bytes 851968 | tf_op jit(solution)/shard_map/feed/pallas_call | solution.py:410
  289.2 21.0 %feed.3 = (bf16[1024,1024]{1,0:T(8,128)(2,1)}, bf16[1024,1024]{1,0:T(8,128)(2,1)}, bf16[1024,1024]{1,0:T(8,128)(2,1)}) custom-call(s32[2]{0:T(128)} %pad_add_fusion.place_ref, bf16[1024,2048]{1,0:T(8,128)(2,1)} %constant_dynamic-update-slice_fusion.8.h_ref, bf16[1024,2048]{1,0:T(8,128)(2,1)} %pad_maximum_fusion.cot_ref, ...), custom_call_target="tpu_custom_call" | custom-call | flops 402653184 | bytes 851968 | tf_op jit(solution)/shard_map/feed/pallas_call | solution.py:410
  316.3 13.7 %unfeed.3 = bf16[512,2048]{1,0:T(8,128)(2,1)S(1)} custom-call(s32[2]{0:T(128)S(1)} %copy-done.42, bf16[1024,1024]{1,0:T(8,128)(2,1)S(1)} %copy-done.6, bf16[1024,1024]{1,0:T(8,128)(2,1)} %get-tuple-element.180.dg1, bf16[1024,1024]{1,0:T(8,128)(2,1)} %get-tuple-element.181.du0, bf16[1024,1024]{1,0:T(8,128)(2,1)} %get-tuple-element.182.du1, ...), custom_call_target="tpu_custom_call" | custom-call | flops 268435456 | bytes 720896 | tf_op jit(solution)/shard_map/unfeed/pallas_call | solution.py:464
  336.5 12.7 %lower.1 = bf16[1024,2048]{1,0:T(8,128)(2,1)} custom-call(s32[2]{0:T(128)S(1)} %copy-done.42, bf16[1024,1024]{1,0:T(8,128)(2,1)S(1)} %copy-done.21, bf16[1024,1024]{1,0:T(8,128)(2,1)S(1)} %copy-done.23, bf16[2048,2048]{1,0:T(8,128)(2,1)} %w1.1, bf16[2048,2048]{1,0:T(8,128)(2,1)} %w1.1), custom_call_target="tpu_custom_call" | custom-call | flops 268435456 | bytes 524288 | tf_op jit(solution)/shard_map/lower/pallas_call | solution.py:494
  349.2 13.9 %unfeed.2 = bf16[512,2048]{1,0:T(8,128)(2,1)S(1)} custom-call(s32[2]{0:T(128)S(1)} %copy-done.42, bf16[1024,1024]{1,0:T(8,128)(2,1)S(1)} %copy-done.7, bf16[1024,1024]{1,0:T(8,128)(2,1)} %get-tuple-element.180.dg1, bf16[1024,1024]{1,0:T(8,128)(2,1)} %get-tuple-element.181.du0, bf16[1024,1024]{1,0:T(8,128)(2,1)} %get-tuple-element.182.du1, ...), custom_call_target="tpu_custom_call" | custom-call | flops 268435456 | bytes 720896 | tf_op jit(solution)/shard_map/unfeed/pallas_call | solution.py:464
  402.7 11.5 %collective-permute-done.29 = bf16[1024,1024]{1,0:T(8,128)(2,1)S(1)} collective-permute-done((bf16[1024,1024]{1,0:T(8,128)(2,1)S(1)}, bf16[1024,1024]{1,0:T(8,128)(2,1)S(1)}, u32[]{:S(2)}, u32[]{:S(2)}) %collective-permute-start.29) | collective-permute-done | bytes 2097184 | tf_op jit(solution)/shard_map/ppermute | solution.py:87
  453.2 16.7 %collective-permute-done.36 = bf16[1024,1024]{1,0:T(8,128)(2,1)S(1)} collective-permute-done((bf16[1024,1024]{1,0:T(8,128)(2,1)S(1)}, bf16[1024,1024]{1,0:T(8,128)(2,1)S(1)}, u32[]{:S(2)}, u32[]{:S(2)}) %collective-permute-start.36) | collective-permute-done | bytes 2097184 | tf_op jit(solution)/shard_map/ppermute | solution.py:87
  504.2 38.7 %attend_back.1 = (bf16[1024,512]{1,0:T(8,128)(2,1)}, bf16[1024,256]{1,0:T(8,128)(2,1)}, bf16[1024,256]{1,0:T(8,128)(2,1)}, bf16[1024,256]{1,0:T(8,128)(2,1)}, bf...) custom-call(s32[2]{0:T(128)} %pad_add_fusion.place_ref, bf16[1024,512]{1,0:T(8,128)(2,1)} %copy-done.66, ...), custom_call_target="tpu_custom_call" | custom-call | flops 536870912 | bytes 786432 | tf_op jit(solution)/shard_map/attend_back/pallas_call | solution.py:670
  620.8 37.6 %collective-permute-done.43 = bf16[1024,256]{1,0:T(8,128)(2,1)S(1)} collective-permute-done((bf16[1024,256]{1,0:T(8,128)(2,1)S(1)}, bf16[1024,256]{1,0:T(8,128)(2,1)S(1)}, u32[]{:S(2)}, u32[]{:S(2)}) %collective-permute-start.43) | collective-permute-done | bytes 524320 | tf_op jit(solution)/shard_map/ppermute | solution.py:137
  716.1 11.1 %collective-permute-done.55 = bf16[256,2048]{1,0:T(8,128)(2,1)} collective-permute-done((bf16[256,2048]{1,0:T(8,128)(2,1)}, bf16[256,2048]{1,0:T(8,128)(2,1)}, u32[]{:S(2)}, u32[]{:S(2)}) %collective-permute-start.55) | collective-permute-done | bytes 1048608 | tf_op jit(solution)/shard_map/ppermute | solution.py:27
  727.2 13.7 %collective-permute-start.70 = (bf16[512,2048]{1,0:T(8,128)(2,1)}, bf16[512,2048]{1,0:T(8,128)(2,1)}, u32[]{:S(2)}, u32[]{:S(2)}) collective-permute-start(bf16[512,2048]{1,0:T(8,128)(2,1)} %get-tuple-element.294), channel_id=1, source_target_pairs={{0,2},{6,4},{1,3},{7,5},{8,10},{14,12},{9,11},{15,13},{16,18},{22,... | collective-permute-start | bytes 6291464 | tf_op jit(solution)/shard_map/ppermute | solution.py:87
  759.2 13.8 %collective-permute-done.61 = bf16[256,128]{1,0:T(8,128)(2,1)S(1)} collective-permute-done((bf16[256,128]{1,0:T(8,128)(2,1)S(1)}, bf16[256,128]{1,0:T(8,128)(2,1)S(1)}, u32[]{:S(2)}, u32[]{:S(2)}) %collective-permute-start.61) | collective-permute-done | bytes 65568 | tf_op jit(solution)/shard_map/ppermute | solution.py:27
  781.2 12.9 %collective-permute-start.68 = (bf16[4,256,256]{2,1,0:T(8,128)(2,1)}, bf16[4,256,256]{2,1,0:T(8,128)(2,1)}, u32[]{:S(2)}, u32[]{:S(2)}) collective-permute-start(bf16[4,256,256]{2,1,0:T(8,128)(2,1)} %fusion.17), channel_id=1, source_target_pairs={{0,2},{6,4},{1,3},{7,5},{8,10},{14,12},{9,11},{15,13},{16,18},{22,... | collective-permute-start | bytes 1572872 | tf_op jit(solution)/shard_map/ppermute | solution.py:87
  817.3 12.6 %collective-permute-start.77 = (bf16[512,2048]{1,0:T(8,128)(2,1)}, bf16[512,2048]{1,0:T(8,128)(2,1)}, u32[]{:S(2)}, u32[]{:S(2)}) collective-permute-start(bf16[512,2048]{1,0:T(8,128)(2,1)} %get-tuple-element.293), channel_id=1, source_target_pairs={{0,2},{6,4},{1,3},{7,5},{8,10},{14,12},{9,11},{15,13},{16,18},{22,... | collective-permute-start | bytes 6291464 | tf_op jit(solution)/shard_map/ppermute | solution.py:87
  843.0 29.9 %collective-permute-done.77 = bf16[512,2048]{1,0:T(8,128)(2,1)} collective-permute-done((bf16[512,2048]{1,0:T(8,128)(2,1)}, bf16[512,2048]{1,0:T(8,128)(2,1)}, u32[]{:S(2)}, u32[]{:S(2)}) %collective-permute-start.77) | collective-permute-done | bytes 2097184 | tf_op jit(solution)/shard_map/ppermute | solution.py:87
  877.3 13.4 %spread.6 = f32[512,8192]{1,0:T(8,128)} custom-call(s32[1]{0:T(128)} %bitcast.1.place_ref, bf16[4,512,1024]{2,1,0:T(8,128)(2,1)} %all-to-all-done.3.own_ref, bf16[4,512,1024]{2,1,0:T(8,128)(2,1)} %collective-permute-done.72.other_ref), custom_call_target="tpu_custom_call" | custom-call | flops 65536 | bytes 786432 | tf_op jit(solution)/shard_map/spread/pallas_call | solution.py:711
  910.7 12.6 %all-to-all-done.4.own_ref = bf16[4,256,512]{2,1,0:T(8,128)(2,1)S(1)} async-done(((bf16[4,256,512]{2,1,0:T(8,128)(2,1)}), bf16[4,256,512]{2,1,0:T(8,128)(2,1)S(1)}, u32[]{:S(2)}, u32[]{:S(2)}) %all-to-all-start.4) | async-done | bytes 1048608 | tf_op jit(solution)/shard_map/all_to_all | solution.py:741
  937.1 13.4 %spread.5 = f32[512,8192]{1,0:T(8,128)} custom-call(s32[1]{0:T(128)} %bitcast.1.place_ref, bf16[4,512,1024]{2,1,0:T(8,128)(2,1)} %all-to-all-done.2.own_ref, bf16[4,512,1024]{2,1,0:T(8,128)(2,1)} %collective-permute-done.71.other_ref), custom_call_target="tpu_custom_call" | custom-call | flops 65536 | bytes 786432 | tf_op jit(solution)/shard_map/spread/pallas_call | solution.py:711
  991.0 19.0 %collective-permute-done.85 = bf16[256,128]{1,0:T(8,128)(2,1)S(1)} collective-permute-done((bf16[256,128]{1,0:T(8,128)(2,1)S(1)}, bf16[256,128]{1,0:T(8,128)(2,1)S(1)}, u32[]{:S(2)}, u32[]{:S(2)}) %collective-permute-start.85) | collective-permute-done | bytes 65568 | tf_op jit(solution)/shard_map/ppermute | solution.py:87
  (572 shorter events, 601.5 us)
Async XLA Ops:
  69.4 103.8 %all-gather.2.cloned.1.call-start = ((), (), s32[]{:S(2)}) async-start(), calls=%async_computation.6 | async-start | bytes 5242880 | tf_op jit(solution)/shard_map/all_gather | solution.py:851
  116.0 57.3 %collective-permute-start.13 = (bf16[2048,1024]{1,0:T(8,128)(2,1)}, bf16[2048,1024]{1,0:T(8,128)(2,1)}, u32[]{:S(2)}, u32[]{:S(2)}) collective-permute-start(bf16[2048,1024]{1,0:T(8,128)(2,1)} %bitcast.11.w0_ref.w00), channel_id=1, source_target_pairs={{0,1},{1,0},{2,3},{3,2},{4,5},{5,4},{6,7},{7,6},{8,9},{9,8},{10,11... | collective-permute-start | bytes 12582920 | tf_op jit(solution)/shard_map/ppermute | solution.py:31
  149.1 93.7 %collective-permute-start.20 = (bf16[2048,1024]{1,0:T(8,128)(2,1)}, bf16[2048,1024]{1,0:T(8,128)(2,1)}, u32[]{:S(2)}, u32[]{:S(2)}) collective-permute-start(bf16[2048,1024]{1,0:T(8,128)(2,1)} %bitcast.11.w0_ref.w00), channel_id=1, source_target_pairs={{0,2},{2,0},{4,6},{6,4},{1,3},{3,1},{5,7},{7,5},{8,10},{10,8},{12,... | collective-permute-start | bytes 12582920 | tf_op jit(solution)/shard_map/ppermute | solution.py:848
  392.8 85.4 %collective-permute-start.39 = (bf16[2048,1024]{1,0:T(8,128)(2,1)}, bf16[2048,1024]{1,0:T(8,128)(2,1)S(1)}, u32[]{:S(2)}, u32[]{:S(2)}) collective-permute-start(bf16[2048,1024]{1,0:T(8,128)(2,1)} %convolution_convert_fusion.1), channel_id=1, source_target_pairs={{0,1},{1,0},{2,3},{3,2},{4,5},{5,4},{6,7},{7,6},{8,9},{9,8},{10,11... | collective-permute-start | bytes 12582920 | tf_op jit(solution)/shard_map/ppermute | solution.py:31
  451.9 91.0 %collective-permute-start.69 = (bf16[1024,2048]{1,0:T(8,128)(2,1)}, bf16[1024,2048]{1,0:T(8,128)(2,1)}, u32[]{:S(2)}, u32[]{:S(2)}) collective-permute-start(bf16[1024,2048]{1,0:T(8,128)(2,1)} %convolution_convert_fusion), channel_id=1, source_target_pairs={{0,1},{1,0},{2,3},{3,2},{4,5},{5,4},{6,7},{7,6},{8,9},{9,8},{10,11... | collective-permute-start | bytes 12582920 | tf_op jit(solution)/shard_map/ppermute | solution.py:31
  472.2 79.7 %collective-permute-start.37 = (bf16[1024,1024]{1,0:T(8,128)(2,1)}, bf16[1024,1024]{1,0:T(8,128)(2,1)}, u32[]{:S(2)}, u32[]{:S(2)}) collective-permute-start(bf16[1024,1024]{1,0:T(8,128)(2,1)} %add_convert_fusion.15), channel_id=1, source_target_pairs={{2,0},{4,6},{3,1},{5,7},{10,8},{12,14},{11,9},{13,15},{18,16},{20,... | collective-permute-start | bytes 6291464 | tf_op jit(solution)/shard_map/ppermute | solution.py:87
  475.9 76.0 %collective-permute-start.38 = (bf16[1024,1024]{1,0:T(8,128)(2,1)}, bf16[1024,1024]{1,0:T(8,128)(2,1)}, u32[]{:S(2)}, u32[]{:S(2)}) collective-permute-start(bf16[1024,1024]{1,0:T(8,128)(2,1)} %add_convert_fusion.14), channel_id=1, source_target_pairs={{2,4},{4,2},{3,5},{5,3},{10,12},{12,10},{11,13},{13,11},{18,20},{2... | collective-permute-start | bytes 6291464 | tf_op jit(solution)/shard_map/ppermute | solution.py:87
  489.9 62.1 %collective-permute-start.40 = (bf16[1024,1024]{1,0:T(8,128)(2,1)}, bf16[1024,1024]{1,0:T(8,128)(2,1)}, u32[]{:S(2)}, u32[]{:S(2)}) collective-permute-start(bf16[1024,1024]{1,0:T(8,128)(2,1)} %get-tuple-element.308), channel_id=1, source_target_pairs={{0,2},{6,4},{1,3},{7,5},{8,10},{14,12},{9,11},{15,13},{16,18},{22,... | collective-permute-start | bytes 6291464 | tf_op jit(solution)/shard_map/ppermute | solution.py:87
  581.5 78.4 %collective-permute-start.59 = (bf16[2048,512]{1,0:T(8,128)(2,1)}, bf16[2048,512]{1,0:T(8,128)(2,1)}, u32[]{:S(2)}, u32[]{:S(2)}) collective-permute-start(bf16[2048,512]{1,0:T(8,128)(2,1)} %pad_maximum_fusion.5), channel_id=1, source_target_pairs={{0,1},{1,0},{2,3},{3,2},{4,5},{5,4},{6,7},{7,6},{8,9},{9,8},{10,11... | collective-permute-start | bytes 6291464 | tf_op jit(solution)/shard_map/ppermute | solution.py:31
  597.9 78.2 %collective-permute-start.49 = (bf16[1024,1024]{1,0:T(8,128)(2,1)}, bf16[1024,1024]{1,0:T(8,128)(2,1)}, u32[]{:S(2)}, u32[]{:S(2)}) collective-permute-start(bf16[1024,1024]{1,0:T(8,128)(2,1)} %add_convert_fusion.13), channel_id=1, source_target_pairs={{2,0},{4,6},{3,1},{5,7},{10,8},{12,14},{11,9},{13,15},{18,16},{20,... | collective-permute-start | bytes 6291464 | tf_op jit(solution)/shard_map/ppermute | solution.py:87
  599.2 77.0 %collective-permute-start.50 = (bf16[1024,1024]{1,0:T(8,128)(2,1)}, bf16[1024,1024]{1,0:T(8,128)(2,1)}, u32[]{:S(2)}, u32[]{:S(2)}) collective-permute-start(bf16[1024,1024]{1,0:T(8,128)(2,1)} %add_convert_fusion.12), channel_id=1, source_target_pairs={{2,4},{4,2},{3,5},{5,3},{10,12},{12,10},{11,13},{13,11},{18,20},{2... | collective-permute-start | bytes 6291464 | tf_op jit(solution)/shard_map/ppermute | solution.py:87
  606.0 70.1 %collective-permute-start.51 = (bf16[1024,1024]{1,0:T(8,128)(2,1)}, bf16[1024,1024]{1,0:T(8,128)(2,1)}, u32[]{:S(2)}, u32[]{:S(2)}) collective-permute-start(bf16[1024,1024]{1,0:T(8,128)(2,1)} %get-tuple-element.218), channel_id=1, source_target_pairs={{0,2},{6,4},{1,3},{7,5},{8,10},{14,12},{9,11},{15,13},{16,18},{22,... | collective-permute-start | bytes 6291464 | tf_op jit(solution)/shard_map/ppermute | solution.py:87
  663.6 79.8 %collective-permute-start.60 = (bf16[2048,512]{1,0:T(8,128)(2,1)}, bf16[2048,512]{1,0:T(8,128)(2,1)}, u32[]{:S(2)}, u32[]{:S(2)}) collective-permute-start(bf16[2048,512]{1,0:T(8,128)(2,1)} %add_convert_fusion.9), channel_id=1, source_target_pairs={{0,2},{6,4},{1,3},{7,5},{8,10},{14,12},{9,11},{15,13},{16,18},{22,... | collective-permute-start | bytes 6291464 | tf_op jit(solution)/shard_map/ppermute | solution.py:87
  710.1 84.0 %all-to-all-start.3 = ((bf16[4,512,1024]{2,1,0:T(8,128)(2,1)}), bf16[4,512,1024]{2,1,0:T(8,128)(2,1)}, u32[]{:S(2)}, u32[]{:S(2)}) async-start(bf16[4,512,1024]{2,1,0:T(8,128)(2,1)} %bitcast.172), calls=%async_computation.3 | async-start | bytes 8388608 | tf_op jit(solution)/shard_map/all_to_all | solution.py:741
  727.2 69.0 %collective-permute-start.70 = (bf16[512,2048]{1,0:T(8,128)(2,1)}, bf16[512,2048]{1,0:T(8,128)(2,1)}, u32[]{:S(2)}, u32[]{:S(2)}) collective-permute-start(bf16[512,2048]{1,0:T(8,128)(2,1)} %get-tuple-element.294), channel_id=1, source_target_pairs={{0,2},{6,4},{1,3},{7,5},{8,10},{14,12},{9,11},{15,13},{16,18},{22,... | collective-permute-start | bytes 6291464 | tf_op jit(solution)/shard_map/ppermute | solution.py:87
  748.6 59.5 %collective-permute-start.66 = (bf16[1024,1024]{1,0:T(8,128)(2,1)}, bf16[1024,1024]{1,0:T(8,128)(2,1)}, u32[]{:S(2)}, u32[]{:S(2)}) collective-permute-start(bf16[1024,1024]{1,0:T(8,128)(2,1)} %add_convert_fusion.8), channel_id=1, source_target_pairs={{2,0},{4,6},{3,1},{5,7},{10,8},{12,14},{11,9},{13,15},{18,16},{20,... | collective-permute-start | bytes 6291464 | tf_op jit(solution)/shard_map/ppermute | solution.py:87
  754.0 54.1 %collective-permute-start.67 = (bf16[2048,512]{1,0:T(8,128)(2,1)}, bf16[2048,512]{1,0:T(8,128)(2,1)}, u32[]{:S(2)}, u32[]{:S(2)}) collective-permute-start(bf16[2048,512]{1,0:T(8,128)(2,1)} %add_convert_fusion.7), channel_id=1, source_target_pairs={{2,4},{4,2},{3,5},{5,3},{10,12},{12,10},{11,13},{13,11},{18,20},{2... | collective-permute-start | bytes 6291464 | tf_op jit(solution)/shard_map/ppermute | solution.py:87
  794.1 78.7 %collective-permute-start.72 = (bf16[4,512,1024]{2,1,0:T(8,128)(2,1)}, bf16[4,512,1024]{2,1,0:T(8,128)(2,1)}, u32[]{:S(2)}, u32[]{:S(2)}) collective-permute-start(bf16[4,512,1024]{2,1,0:T(8,128)(2,1)} %all-to-all-done.3.own_ref), channel_id=1, source_target_pairs={{0,1},{1,0},{2,3},{3,2},{4,5},{5,4},{6,7},{7,6},{8,9},{9,8},{10,11... | collective-permute-start | bytes 12582920 | tf_op jit(solution)/shard_map/ppermute | solution.py:31
  812.4 60.5 %all-to-all-start.2 = ((bf16[4,512,1024]{2,1,0:T(8,128)(2,1)}), bf16[4,512,1024]{2,1,0:T(8,128)(2,1)}, u32[]{:S(2)}, u32[]{:S(2)}) async-start(bf16[4,512,1024]{2,1,0:T(8,128)(2,1)} %bitcast.173), calls=%async_computation.2 | async-start | bytes 8388608 | tf_op jit(solution)/shard_map/all_to_all | solution.py:741
  817.3 55.6 %collective-permute-start.77 = (bf16[512,2048]{1,0:T(8,128)(2,1)}, bf16[512,2048]{1,0:T(8,128)(2,1)}, u32[]{:S(2)}, u32[]{:S(2)}) collective-permute-start(bf16[512,2048]{1,0:T(8,128)(2,1)} %get-tuple-element.293), channel_id=1, source_target_pairs={{0,2},{6,4},{1,3},{7,5},{8,10},{14,12},{9,11},{15,13},{16,18},{22,... | collective-permute-start | bytes 6291464 | tf_op jit(solution)/shard_map/ppermute | solution.py:87
  837.7 53.0 %collective-permute-start.75 = (bf16[512,2048]{1,0:T(8,128)(2,1)}, bf16[512,2048]{1,0:T(8,128)(2,1)}, u32[]{:S(2)}, u32[]{:S(2)}) collective-permute-start(bf16[512,2048]{1,0:T(8,128)(2,1)} %add_convert_fusion.5), channel_id=1, source_target_pairs={{2,4},{4,2},{3,5},{5,3},{10,12},{12,10},{11,13},{13,11},{18,20},{2... | collective-permute-start | bytes 6291464 | tf_op jit(solution)/shard_map/ppermute | solution.py:87
  872.9 64.3 %collective-permute-start.71 = (bf16[4,512,1024]{2,1,0:T(8,128)(2,1)}, bf16[4,512,1024]{2,1,0:T(8,128)(2,1)}, u32[]{:S(2)}, u32[]{:S(2)}) collective-permute-start(bf16[4,512,1024]{2,1,0:T(8,128)(2,1)} %all-to-all-done.2.own_ref), channel_id=1, source_target_pairs={{0,1},{1,0},{2,3},{3,2},{4,5},{5,4},{6,7},{7,6},{8,9},{9,8},{10,11... | collective-permute-start | bytes 12582920 | tf_op jit(solution)/shard_map/ppermute | solution.py:31
  895.5 61.5 %collective-permute-start.81 = (bf16[512,2048]{1,0:T(8,128)(2,1)}, bf16[512,2048]{1,0:T(8,128)(2,1)}, u32[]{:S(2)}, u32[]{:S(2)}) collective-permute-start(bf16[512,2048]{1,0:T(8,128)(2,1)} %add_convert_fusion.4), channel_id=1, source_target_pairs={{2,0},{4,6},{3,1},{5,7},{10,8},{12,14},{11,9},{13,15},{18,16},{20,... | collective-permute-start | bytes 6291464 | tf_op jit(solution)/shard_map/ppermute | solution.py:87
  900.5 56.5 %collective-permute-start.83 = (bf16[512,2048]{1,0:T(8,128)(2,1)}, bf16[512,2048]{1,0:T(8,128)(2,1)}, u32[]{:S(2)}, u32[]{:S(2)}) collective-permute-start(bf16[512,2048]{1,0:T(8,128)(2,1)} %add_convert_fusion.3), channel_id=1, source_target_pairs={{2,4},{4,2},{3,5},{5,3},{10,12},{12,10},{11,13},{13,11},{18,20},{2... | collective-permute-start | bytes 6291464 | tf_op jit(solution)/shard_map/ppermute | solution.py:87
  (177 other events, 3235.6 us)
Sparse Core Ops, SparseCore 0:
  116.1 52.9 all-gather.1

commit v4 on v3

--- a/solution.py
+++ b/solution.py
@@ -725,6 +725,39 @@
     )(c.astype(jnp.int32)[None], own, other)
 
 
+def spread_half(own, other, c, half, base):
+    high, wide = own.shape
+    scalars = jnp.stack([c, 1 - c]).astype(jnp.int32)
+
+    def kernel(place_ref, own_ref, other_ref, *refs):
+        out_ref = refs[-1]
+
+        @pl.when(pl.program_id(0) == 0)
+        def _():
+            out_ref[...] = own_ref[...].astype(F32)
+
+        @pl.when(pl.program_id(0) == 1)
+        def _():
+            out_ref[...] = other_ref[...].astype(F32)
+
+    more = [] if base is None else [base]
+    return pl.pallas_call(
+        kernel,
+        grid_spec=pltpu.PrefetchScalarGridSpec(
+            num_scalar_prefetch=1,
+            grid=(2,),
+            in_specs=[pl.BlockSpec((high, wide), lambda side, place: (0, 0))] * 2
+            + [pl.BlockSpec(memory_space=pl.ANY)] * len(more),
+            out_specs=pl.BlockSpec((high, wide), lambda side, place: (2 * place[side] + half, 0)),
+        ),
+        out_shape=jax.ShapeDtypeStruct((4 * high, wide), F32),
+        input_output_aliases={3: 0} if more else {},
+        compiler_params=pltpu.CompilerParams(vmem_limit_bytes=48 << 20),
+        cost_estimate=cost(flops=own.size, transcendentals=0, bytes_accessed=12 * own.size),
+        name="spread_half",
+    )(scalars, own, other, *more)
+
+
 def dot(left, right):
     return jnp.dot(left, right, preferred_element_type=F32)
 
@@ -988,10 +1021,13 @@
     g_kv = jnp.transpose(g_kv, (0, 2, 1, 3)).reshape(shard, count * kv_local, 2, HEAD_DIM)
     grad_k = g_kv[:, :, 0].reshape(shard, count * k_width)
     grad_v = g_kv[:, :, 1].reshape(shard, count * k_width)
-    grad_k, grad_v = line.round((grad_k, grad_v))
+    (first,) = line.take("down0")
+    grad_down = spread_half(first, core_swap(first), c, 0, None)
+    grad_k, grad_v, grad_down = line.round((grad_k, grad_v, grad_down))
     (gains,) = line.take("gains")
     gains = by_core(gains, core_swap(gains), 0).astype(F32).reshape(shard, LANES)
-    grad_down = pair_rows(whole("down"))
+    (second,) = line.take("down1")
+    grad_down = spread_half(second, core_swap(second), c, 1, grad_down)
     return (
         layer_out,
         grad_tokens,

time: 1060 us -> 1050 us (level)
  blocking collectives: 0 us -> 12.7 us
    all_to_all x0 -> x1, blocking collectives: none -> 12.7 us  [exchange(): lax.all_to_all(field, 'fsdp', split_axis=0, concat_axis=0, tiled=True)]
    pallas_call x0 -> x2, Pallas kernels: none -> 11.7 us  [spread_half(): pl.pallas_call(kernel, grid_spec=pltpu.PrefetchScalarGridSpec(num_scalar_...]
    pallas_call x5 -> x4, Pallas kernels: 41.5 us -> 32.5 us  [spread(): pl.pallas_call(spread_kernel, grid_spec=pltpu.PrefetchScalarGridSpec(num_...]
    all_to_all x6 -> x5, waiting for transfers between devices: 25.4 us -> 20.3 us  [exchange(): lax.all_to_all(field, 'fsdp', split_axis=0, concat_axis=0, tiled=True)]
    all_to_all x6 -> x5, starting transfers between devices: 27.2 us -> 23 us  [exchange(): lax.all_to_all(field, 'fsdp', split_axis=0, concat_axis=0, tiled=True)]
  transfers between devices with their start and end apart: 96 -> 96, of which waited for: 43 -> 43; matrix products, arithmetic and copies ran while one was open for 20% -> 20% of each run, Pallas kernels for 16% -> 17%
where the time goes in v4:
time: 1050 us; the launch traced here: 1040 us
  waiting for transfers between devices  350 us (33%)
  Pallas kernels  219 us (21%)
  starting transfers between devices  187 us (18%)
  other arithmetic  118 us (11%)
  matrix products  69.3 us (7%)
  local copies, waits for them, and re-layouts  68.9 us (7%)
  between operations  16.4 us (2%)
  blocking collectives  12.7 us (1%)
    ppermute x35, waiting for transfers between devices, xor_send(): return lax.ppermute(field, 'fsdp', [(i, i ^ bit) for i in range(count)])  131 us
    ppermute x27, starting transfers between devices, z_move(): return lax.ppermute(field, 'zed', z_steps()[stage][0])  102 us
    ppermute x27, waiting for transfers between devices, z_move(): return lax.ppermute(field, 'zed', z_steps()[stage][0])  91.6 us
    convert_element_type x28, other arithmetic, add_low(): return (left.astype(F32) + right.astype(F32)).astype(BF)  64.4 us
    dot_general x11, matrix products, t_dot(): lax.dot_general(left, right, (((0,), (0,)), ((), ())), preferred_element_...  60.4 us
    ppermute x3, waiting for transfers between devices, z_down(): return lax.ppermute(field, 'zed', [(i + 1, i) for i in range(count - 1)])  48.6 us
    pallas_call x2, Pallas kernels, feed(): pl.pallas_call(feed_kernel, grid_spec=pltpu.PrefetchScalarGridSpec(num_sc...  41.8 us
    ppermute x35, starting transfers between devices, xor_send(): return lax.ppermute(field, 'fsdp', [(i, i ^ bit) for i in range(count)])  40.4 us
  transfers between devices with their start and end apart: 96, of which 43 were waited for; matrix products, arithmetic and copies ran while one was open for 20% of the time, Pallas kernels for 17%

profile of v4, /device:TPU:0, one launch (start us, length us, event | category | flops | bytes accessed | tf_op | source)
XLA Modules:
  0.0 1041.6 jit_solution(7084718728726699757)
XLA Ops:
  43.2 20.3 %collective-permute-done.3 = bf16[128,2048]{1,0:T(8,128)(2,1)S(1)} collective-permute-done((bf16[128,2048]{1,0:T(8,128)(2,1)S(1)}, bf16[128,2048]{1,0:T(8,128)(2,1)S(1)}, u32[]{:S(2)}, u32[]{:S(2)}) %collective-permute-start.3) | collective-permute-done | bytes 524320 | tf_op jit(solution)/shard_map/ppermute | solution.py:27
  119.7 12.0 %collective-permute-done.9.refs_2_ = bf16[1024,256]{1,0:T(8,128)(2,1)S(1)} collective-permute-done((bf16[1024,256]{1,0:T(8,128)(2,1)}, bf16[1024,256]{1,0:T(8,128)(2,1)S(1)}, u32[]{:S(2)}, u32[]{:S(2)}) %collective-permute-start.9) | collective-permute-done | bytes 524320 | tf_op jit(solution)/shard_map/ppermute | solution.py:132
  154.2 19.1 %attend.1 = (bf16[1024,512]{1,0:T(8,128)(2,1)}, f32[8,2,512,1]{3,2,1,0:T(8,128)}) custom-call(s32[2]{0:T(128)} %pad_add_fusion.place_ref, bf16[1024,512]{1,0:T(8,128)(2,1)} %copy-done.66, bf16[1024,256]{1,0:T(8,128)(2,1)} %copy-done.72, bf16[1024,256]{1,0:T(8,128)(2,1)} %collective-permute-done.8.refs_1_, bf16[1024,256]{1,0:T(8,128)(2,1)} %copy-done.67, ...), custom_call_target="tpu_custom_call" | custom-call | flops 268435456 | bytes 524288 | tf_op jit(solution)/shard_map/attend/pallas_call | solution.py:646
  198.9 16.3 %collective-permute-done.17 = bf16[256,2048]{1,0:T(8,128)(2,1)} collective-permute-done((bf16[256,2048]{1,0:T(8,128)(2,1)}, bf16[256,2048]{1,0:T(8,128)(2,1)}, u32[]{:S(2)}, u32[]{:S(2)}) %collective-permute-start.17) | collective-permute-done | bytes 1048608 | tf_op jit(solution)/shard_map/ppermute | solution.py:27
  222.8 20.0 %collective-permute-done.20.w1_ref.w10 = bf16[2048,1024]{1,0:T(8,128)(2,1)} collective-permute-done((bf16[2048,1024]{1,0:T(8,128)(2,1)}, bf16[2048,1024]{1,0:T(8,128)(2,1)}, u32[]{:S(2)}, u32[]{:S(2)}) %collective-permute-start.20) | collective-permute-done | bytes 4194336 | tf_op jit(solution)/shard_map/ppermute | solution.py:881
  263.7 20.8 %feed.2 = (bf16[1024,1024]{1,0:T(8,128)(2,1)}, bf16[1024,1024]{1,0:T(8,128)(2,1)}, bf16[1024,1024]{1,0:T(8,128)(2,1)}) custom-call(s32[2]{0:T(128)} %pad_add_fusion.place_ref, bf16[1024,2048]{1,0:T(8,128)(2,1)} %constant_dynamic-update-slice_fusion.8.h_ref, bf16[1024,2048]{1,0:T(8,128)(2,1)} %pad_maximum_fusion.cot_ref, ...), custom_call_target="tpu_custom_call" | custom-call | flops 402653184 | bytes 851968 | tf_op jit(solution)/shard_map/feed/pallas_call | solution.py:410
  289.1 21.0 %feed.3 = (bf16[1024,1024]{1,0:T(8,128)(2,1)}, bf16[1024,1024]{1,0:T(8,128)(2,1)}, bf16[1024,1024]{1,0:T(8,128)(2,1)}) custom-call(s32[2]{0:T(128)} %pad_add_fusion.place_ref, bf16[1024,2048]{1,0:T(8,128)(2,1)} %constant_dynamic-update-slice_fusion.8.h_ref, bf16[1024,2048]{1,0:T(8,128)(2,1)} %pad_maximum_fusion.cot_ref, ...), custom_call_target="tpu_custom_call" | custom-call | flops 402653184 | bytes 851968 | tf_op jit(solution)/shard_map/feed/pallas_call | solution.py:410
  316.3 13.7 %unfeed.3 = bf16[512,2048]{1,0:T(8,128)(2,1)S(1)} custom-call(s32[2]{0:T(128)S(1)} %copy-done.43, bf16[1024,1024]{1,0:T(8,128)(2,1)S(1)} %copy-done.5, bf16[1024,1024]{1,0:T(8,128)(2,1)} %get-tuple-element.181.dg1, bf16[1024,1024]{1,0:T(8,128)(2,1)} %get-tuple-element.182.du0, bf16[1024,1024]{1,0:T(8,128)(2,1)} %get-tuple-element.183.du1, ...), custom_call_target="tpu_custom_call" | custom-call | flops 268435456 | bytes 720896 | tf_op jit(solution)/shard_map/unfeed/pallas_call | solution.py:464
  336.5 12.7 %lower.1 = bf16[1024,2048]{1,0:T(8,128)(2,1)} custom-call(s32[2]{0:T(128)S(1)} %copy-done.43, bf16[1024,1024]{1,0:T(8,128)(2,1)S(1)} %copy-done.22, bf16[1024,1024]{1,0:T(8,128)(2,1)S(1)} %copy-done.24, bf16[2048,2048]{1,0:T(8,128)(2,1)} %w1.1, bf16[2048,2048]{1,0:T(8,128)(2,1)} %w1.1), custom_call_target="tpu_custom_call" | custom-call | flops 268435456 | bytes 524288 | tf_op jit(solution)/shard_map/lower/pallas_call | solution.py:494
  349.2 13.9 %unfeed.2 = bf16[512,2048]{1,0:T(8,128)(2,1)S(1)} custom-call(s32[2]{0:T(128)S(1)} %copy-done.43, bf16[1024,1024]{1,0:T(8,128)(2,1)S(1)} %copy-done.6, bf16[1024,1024]{1,0:T(8,128)(2,1)} %get-tuple-element.181.dg1, bf16[1024,1024]{1,0:T(8,128)(2,1)} %get-tuple-element.182.du0, bf16[1024,1024]{1,0:T(8,128)(2,1)} %get-tuple-element.183.du1, ...), custom_call_target="tpu_custom_call" | custom-call | flops 268435456 | bytes 720896 | tf_op jit(solution)/shard_map/unfeed/pallas_call | solution.py:464
  402.6 11.6 %collective-permute-done.29 = bf16[1024,1024]{1,0:T(8,128)(2,1)S(1)} collective-permute-done((bf16[1024,1024]{1,0:T(8,128)(2,1)S(1)}, bf16[1024,1024]{1,0:T(8,128)(2,1)S(1)}, u32[]{:S(2)}, u32[]{:S(2)}) %collective-permute-start.29) | collective-permute-done | bytes 2097184 | tf_op jit(solution)/shard_map/ppermute | solution.py:87
  453.3 16.7 %collective-permute-done.36 = bf16[1024,1024]{1,0:T(8,128)(2,1)S(1)} collective-permute-done((bf16[1024,1024]{1,0:T(8,128)(2,1)S(1)}, bf16[1024,1024]{1,0:T(8,128)(2,1)S(1)}, u32[]{:S(2)}, u32[]{:S(2)}) %collective-permute-start.36) | collective-permute-done | bytes 2097184 | tf_op jit(solution)/shard_map/ppermute | solution.py:87
  504.3 38.7 %attend_back.1 = (bf16[1024,512]{1,0:T(8,128)(2,1)}, bf16[1024,256]{1,0:T(8,128)(2,1)}, bf16[1024,256]{1,0:T(8,128)(2,1)}, bf16[1024,256]{1,0:T(8,128)(2,1)}, bf...) custom-call(s32[2]{0:T(128)} %pad_add_fusion.place_ref, bf16[1024,512]{1,0:T(8,128)(2,1)} %copy-done.66, ...), custom_call_target="tpu_custom_call" | custom-call | flops 536870912 | bytes 786432 | tf_op jit(solution)/shard_map/attend_back/pallas_call | solution.py:670
  620.9 37.6 %collective-permute-done.43 = bf16[1024,256]{1,0:T(8,128)(2,1)S(1)} collective-permute-done((bf16[1024,256]{1,0:T(8,128)(2,1)S(1)}, bf16[1024,256]{1,0:T(8,128)(2,1)S(1)}, u32[]{:S(2)}, u32[]{:S(2)}) %collective-permute-start.43) | collective-permute-done | bytes 524320 | tf_op jit(solution)/shard_map/ppermute | solution.py:137
  727.3 13.7 %collective-permute-start.70 = (bf16[512,2048]{1,0:T(8,128)(2,1)}, bf16[512,2048]{1,0:T(8,128)(2,1)}, u32[]{:S(2)}, u32[]{:S(2)}) collective-permute-start(bf16[512,2048]{1,0:T(8,128)(2,1)} %get-tuple-element.294), channel_id=1, source_target_pairs={{0,2},{6,4},{1,3},{7,5},{8,10},{14,12},{9,11},{15,13},{16,18},{22,... | collective-permute-start | bytes 6291464 | tf_op jit(solution)/shard_map/ppermute | solution.py:87
  759.3 13.8 %collective-permute-done.61 = bf16[256,128]{1,0:T(8,128)(2,1)S(1)} collective-permute-done((bf16[256,128]{1,0:T(8,128)(2,1)S(1)}, bf16[256,128]{1,0:T(8,128)(2,1)S(1)}, u32[]{:S(2)}, u32[]{:S(2)}) %collective-permute-start.61) | collective-permute-done | bytes 65568 | tf_op jit(solution)/shard_map/ppermute | solution.py:27
  781.3 12.9 %collective-permute-start.68 = (bf16[4,256,256]{2,1,0:T(8,128)(2,1)}, bf16[4,256,256]{2,1,0:T(8,128)(2,1)}, u32[]{:S(2)}, u32[]{:S(2)}) collective-permute-start(bf16[4,256,256]{2,1,0:T(8,128)(2,1)} %fusion.17), channel_id=1, source_target_pairs={{0,2},{6,4},{1,3},{7,5},{8,10},{14,12},{9,11},{15,13},{16,18},{22,... | collective-permute-start | bytes 1572872 | tf_op jit(solution)/shard_map/ppermute | solution.py:87
  817.3 12.6 %collective-permute-start.77 = (bf16[512,2048]{1,0:T(8,128)(2,1)}, bf16[512,2048]{1,0:T(8,128)(2,1)}, u32[]{:S(2)}, u32[]{:S(2)}) collective-permute-start(bf16[512,2048]{1,0:T(8,128)(2,1)} %get-tuple-element.293), channel_id=1, source_target_pairs={{0,2},{6,4},{1,3},{7,5},{8,10},{14,12},{9,11},{15,13},{16,18},{22,... | collective-permute-start | bytes 6291464 | tf_op jit(solution)/shard_map/ppermute | solution.py:87
  843.0 29.9 %collective-permute-done.77 = bf16[512,2048]{1,0:T(8,128)(2,1)} collective-permute-done((bf16[512,2048]{1,0:T(8,128)(2,1)}, bf16[512,2048]{1,0:T(8,128)(2,1)}, u32[]{:S(2)}, u32[]{:S(2)}) %collective-permute-start.77) | collective-permute-done | bytes 2097184 | tf_op jit(solution)/shard_map/ppermute | solution.py:87
  877.3 13.4 %spread.5 = f32[512,8192]{1,0:T(8,128)} custom-call(s32[1]{0:T(128)} %bitcast.1.place_ref, bf16[4,512,1024]{2,1,0:T(8,128)(2,1)} %all-to-all-done.3.own_ref, bf16[4,512,1024]{2,1,0:T(8,128)(2,1)} %collective-permute-done.72.other_ref), custom_call_target="tpu_custom_call" | custom-call | flops 65536 | bytes 786432 | tf_op jit(solution)/shard_map/spread/pallas_call | solution.py:711
  910.7 12.6 %all-to-all-done.4.own_ref = bf16[4,256,512]{2,1,0:T(8,128)(2,1)S(1)} async-done(((bf16[4,256,512]{2,1,0:T(8,128)(2,1)}), bf16[4,256,512]{2,1,0:T(8,128)(2,1)S(1)}, u32[]{:S(2)}, u32[]{:S(2)}) %all-to-all-start.4) | async-done | bytes 1048608 | tf_op jit(solution)/shard_map/all_to_all | solution.py:774
  937.1 13.4 %spread.4 = f32[512,8192]{1,0:T(8,128)} custom-call(s32[1]{0:T(128)} %bitcast.1.place_ref, bf16[4,512,1024]{2,1,0:T(8,128)(2,1)} %all-to-all-done.2.own_ref, bf16[4,512,1024]{2,1,0:T(8,128)(2,1)} %collective-permute-done.71.other_ref), custom_call_target="tpu_custom_call" | custom-call | flops 65536 | bytes 786432 | tf_op jit(solution)/shard_map/spread/pallas_call | solution.py:711
  965.8 12.7 %all_to_all.30 = bf16[4,256,256]{2,1,0:T(8,128)(2,1)} all-to-all(bf16[4,256,256]{2,1,0:T(8,128)(2,1)S(1)} %broadcast_select_fusion.7), channel_id=1, replica_groups=mesh['fsdp'=4,'zed'=4,'core'=2] {'fsdp'}, dimensions={0} | all-to-all | bytes 1048576 | tf_op jit(solution)/shard_map/all_to_all | solution.py:774
  1000.5 14.4 %collective-permute-done.86 = bf16[256,128]{1,0:T(8,128)(2,1)S(1)} collective-permute-done((bf16[256,128]{1,0:T(8,128)(2,1)S(1)}, bf16[256,128]{1,0:T(8,128)(2,1)S(1)}, u32[]{:S(2)}, u32[]{:S(2)}) %collective-permute-start.86) | collective-permute-done | bytes 65568 | tf_op jit(solution)/shard_map/ppermute | solution.py:87
  (574 shorter events, 601.8 us)
Async XLA Ops:
  69.5 103.8 %all-gather.2.cloned.1.call-start = ((), (), s32[]{:S(2)}) async-start(), calls=%async_computation.6 | async-start | bytes 5242880 | tf_op jit(solution)/shard_map/all_gather | solution.py:884
  116.0 57.3 %collective-permute-start.13 = (bf16[2048,1024]{1,0:T(8,128)(2,1)}, bf16[2048,1024]{1,0:T(8,128)(2,1)}, u32[]{:S(2)}, u32[]{:S(2)}) collective-permute-start(bf16[2048,1024]{1,0:T(8,128)(2,1)} %bitcast.11.w0_ref.w00), channel_id=1, source_target_pairs={{0,1},{1,0},{2,3},{3,2},{4,5},{5,4},{6,7},{7,6},{8,9},{9,8},{10,11... | collective-permute-start | bytes 12582920 | tf_op jit(solution)/shard_map/ppermute | solution.py:31
  149.1 93.7 %collective-permute-start.20 = (bf16[2048,1024]{1,0:T(8,128)(2,1)}, bf16[2048,1024]{1,0:T(8,128)(2,1)}, u32[]{:S(2)}, u32[]{:S(2)}) collective-permute-start(bf16[2048,1024]{1,0:T(8,128)(2,1)} %bitcast.11.w0_ref.w00), channel_id=1, source_target_pairs={{0,2},{2,0},{4,6},{6,4},{1,3},{3,1},{5,7},{7,5},{8,10},{10,8},{12,... | collective-permute-start | bytes 12582920 | tf_op jit(solution)/shard_map/ppermute | solution.py:881
  392.7 85.5 %collective-permute-start.39 = (bf16[2048,1024]{1,0:T(8,128)(2,1)}, bf16[2048,1024]{1,0:T(8,128)(2,1)S(1)}, u32[]{:S(2)}, u32[]{:S(2)}) collective-permute-start(bf16[2048,1024]{1,0:T(8,128)(2,1)} %convolution_convert_fusion.1), channel_id=1, source_target_pairs={{0,1},{1,0},{2,3},{3,2},{4,5},{5,4},{6,7},{7,6},{8,9},{9,8},{10,11... | collective-permute-start | bytes 12582920 | tf_op jit(solution)/shard_map/ppermute | solution.py:31
  452.0 91.1 %collective-permute-start.69 = (bf16[1024,2048]{1,0:T(8,128)(2,1)}, bf16[1024,2048]{1,0:T(8,128)(2,1)}, u32[]{:S(2)}, u32[]{:S(2)}) collective-permute-start(bf16[1024,2048]{1,0:T(8,128)(2,1)} %convolution_convert_fusion), channel_id=1, source_target_pairs={{0,1},{1,0},{2,3},{3,2},{4,5},{5,4},{6,7},{7,6},{8,9},{9,8},{10,11... | collective-permute-start | bytes 12582920 | tf_op jit(solution)/shard_map/ppermute | solution.py:31
  472.2 79.8 %collective-permute-start.37 = (bf16[1024,1024]{1,0:T(8,128)(2,1)}, bf16[1024,1024]{1,0:T(8,128)(2,1)}, u32[]{:S(2)}, u32[]{:S(2)}) collective-permute-start(bf16[1024,1024]{1,0:T(8,128)(2,1)} %add_convert_fusion.15), channel_id=1, source_target_pairs={{2,0},{4,6},{3,1},{5,7},{10,8},{12,14},{11,9},{13,15},{18,16},{20,... | collective-permute-start | bytes 6291464 | tf_op jit(solution)/shard_map/ppermute | solution.py:87
  476.0 76.1 %collective-permute-start.38 = (bf16[1024,1024]{1,0:T(8,128)(2,1)}, bf16[1024,1024]{1,0:T(8,128)(2,1)}, u32[]{:S(2)}, u32[]{:S(2)}) collective-permute-start(bf16[1024,1024]{1,0:T(8,128)(2,1)} %add_convert_fusion.14), channel_id=1, source_target_pairs={{2,4},{4,2},{3,5},{5,3},{10,12},{12,10},{11,13},{13,11},{18,20},{2... | collective-permute-start | bytes 6291464 | tf_op jit(solution)/shard_map/ppermute | solution.py:87
  489.9 62.1 %collective-permute-start.40 = (bf16[1024,1024]{1,0:T(8,128)(2,1)}, bf16[1024,1024]{1,0:T(8,128)(2,1)}, u32[]{:S(2)}, u32[]{:S(2)}) collective-permute-start(bf16[1024,1024]{1,0:T(8,128)(2,1)} %get-tuple-element.308), channel_id=1, source_target_pairs={{0,2},{6,4},{1,3},{7,5},{8,10},{14,12},{9,11},{15,13},{16,18},{22,... | collective-permute-start | bytes 6291464 | tf_op jit(solution)/shard_map/ppermute | solution.py:87
  581.6 78.4 %collective-permute-start.59 = (bf16[2048,512]{1,0:T(8,128)(2,1)}, bf16[2048,512]{1,0:T(8,128)(2,1)}, u32[]{:S(2)}, u32[]{:S(2)}) collective-permute-start(bf16[2048,512]{1,0:T(8,128)(2,1)} %pad_maximum_fusion.4), channel_id=1, source_target_pairs={{0,1},{1,0},{2,3},{3,2},{4,5},{5,4},{6,7},{7,6},{8,9},{9,8},{10,11... | collective-permute-start | bytes 6291464 | tf_op jit(solution)/shard_map/ppermute | solution.py:31
  598.0 78.3 %collective-permute-start.49 = (bf16[1024,1024]{1,0:T(8,128)(2,1)}, bf16[1024,1024]{1,0:T(8,128)(2,1)}, u32[]{:S(2)}, u32[]{:S(2)}) collective-permute-start(bf16[1024,1024]{1,0:T(8,128)(2,1)} %add_convert_fusion.13), channel_id=1, source_target_pairs={{2,0},{4,6},{3,1},{5,7},{10,8},{12,14},{11,9},{13,15},{18,16},{20,... | collective-permute-start | bytes 6291464 | tf_op jit(solution)/shard_map/ppermute | solution.py:87
  599.3 77.0 %collective-permute-start.50 = (bf16[1024,1024]{1,0:T(8,128)(2,1)}, bf16[1024,1024]{1,0:T(8,128)(2,1)}, u32[]{:S(2)}, u32[]{:S(2)}) collective-permute-start(bf16[1024,1024]{1,0:T(8,128)(2,1)} %add_convert_fusion.12), channel_id=1, source_target_pairs={{2,4},{4,2},{3,5},{5,3},{10,12},{12,10},{11,13},{13,11},{18,20},{2... | collective-permute-start | bytes 6291464 | tf_op jit(solution)/shard_map/ppermute | solution.py:87
  606.1 70.2 %collective-permute-start.51 = (bf16[1024,1024]{1,0:T(8,128)(2,1)}, bf16[1024,1024]{1,0:T(8,128)(2,1)}, u32[]{:S(2)}, u32[]{:S(2)}) collective-permute-start(bf16[1024,1024]{1,0:T(8,128)(2,1)} %get-tuple-element.219), channel_id=1, source_target_pairs={{0,2},{6,4},{1,3},{7,5},{8,10},{14,12},{9,11},{15,13},{16,18},{22,... | collective-permute-start | bytes 6291464 | tf_op jit(solution)/shard_map/ppermute | solution.py:87
  663.7 79.7 %collective-permute-start.60 = (bf16[2048,512]{1,0:T(8,128)(2,1)}, bf16[2048,512]{1,0:T(8,128)(2,1)}, u32[]{:S(2)}, u32[]{:S(2)}) collective-permute-start(bf16[2048,512]{1,0:T(8,128)(2,1)} %add_convert_fusion.9), channel_id=1, source_target_pairs={{0,2},{6,4},{1,3},{7,5},{8,10},{14,12},{9,11},{15,13},{16,18},{22,... | collective-permute-start | bytes 6291464 | tf_op jit(solution)/shard_map/ppermute | solution.py:87
  710.2 84.0 %all-to-all-start.3 = ((bf16[4,512,1024]{2,1,0:T(8,128)(2,1)}), bf16[4,512,1024]{2,1,0:T(8,128)(2,1)}, u32[]{:S(2)}, u32[]{:S(2)}) async-start(bf16[4,512,1024]{2,1,0:T(8,128)(2,1)} %bitcast.170), calls=%async_computation.3 | async-start | bytes 8388608 | tf_op jit(solution)/shard_map/all_to_all | solution.py:774
  727.3 69.0 %collective-permute-start.70 = (bf16[512,2048]{1,0:T(8,128)(2,1)}, bf16[512,2048]{1,0:T(8,128)(2,1)}, u32[]{:S(2)}, u32[]{:S(2)}) collective-permute-start(bf16[512,2048]{1,0:T(8,128)(2,1)} %get-tuple-element.294), channel_id=1, source_target_pairs={{0,2},{6,4},{1,3},{7,5},{8,10},{14,12},{9,11},{15,13},{16,18},{22,... | collective-permute-start | bytes 6291464 | tf_op jit(solution)/shard_map/ppermute | solution.py:87
  748.6 59.5 %collective-permute-start.66 = (bf16[1024,1024]{1,0:T(8,128)(2,1)}, bf16[1024,1024]{1,0:T(8,128)(2,1)}, u32[]{:S(2)}, u32[]{:S(2)}) collective-permute-start(bf16[1024,1024]{1,0:T(8,128)(2,1)} %add_convert_fusion.8), channel_id=1, source_target_pairs={{2,0},{4,6},{3,1},{5,7},{10,8},{12,14},{11,9},{13,15},{18,16},{20,... | collective-permute-start | bytes 6291464 | tf_op jit(solution)/shard_map/ppermute | solution.py:87
  754.0 54.1 %collective-permute-start.67 = (bf16[2048,512]{1,0:T(8,128)(2,1)}, bf16[2048,512]{1,0:T(8,128)(2,1)}, u32[]{:S(2)}, u32[]{:S(2)}) collective-permute-start(bf16[2048,512]{1,0:T(8,128)(2,1)} %add_convert_fusion.7), channel_id=1, source_target_pairs={{2,4},{4,2},{3,5},{5,3},{10,12},{12,10},{11,13},{13,11},{18,20},{2... | collective-permute-start | bytes 6291464 | tf_op jit(solution)/shard_map/ppermute | solution.py:87
  794.2 78.7 %collective-permute-start.72 = (bf16[4,512,1024]{2,1,0:T(8,128)(2,1)}, bf16[4,512,1024]{2,1,0:T(8,128)(2,1)}, u32[]{:S(2)}, u32[]{:S(2)}) collective-permute-start(bf16[4,512,1024]{2,1,0:T(8,128)(2,1)} %all-to-all-done.3.own_ref), channel_id=1, source_target_pairs={{0,1},{1,0},{2,3},{3,2},{4,5},{5,4},{6,7},{7,6},{8,9},{9,8},{10,11... | collective-permute-start | bytes 12582920 | tf_op jit(solution)/shard_map/ppermute | solution.py:31
  812.4 60.5 %all-to-all-start.2 = ((bf16[4,512,1024]{2,1,0:T(8,128)(2,1)}), bf16[4,512,1024]{2,1,0:T(8,128)(2,1)}, u32[]{:S(2)}, u32[]{:S(2)}) async-start(bf16[4,512,1024]{2,1,0:T(8,128)(2,1)} %bitcast.171), calls=%async_computation.2 | async-start | bytes 8388608 | tf_op jit(solution)/shard_map/all_to_all | solution.py:774
  817.3 55.6 %collective-permute-start.77 = (bf16[512,2048]{1,0:T(8,128)(2,1)}, bf16[512,2048]{1,0:T(8,128)(2,1)}, u32[]{:S(2)}, u32[]{:S(2)}) collective-permute-start(bf16[512,2048]{1,0:T(8,128)(2,1)} %get-tuple-element.293), channel_id=1, source_target_pairs={{0,2},{6,4},{1,3},{7,5},{8,10},{14,12},{9,11},{15,13},{16,18},{22,... | collective-permute-start | bytes 6291464 | tf_op jit(solution)/shard_map/ppermute | solution.py:87
  837.7 53.0 %collective-permute-start.75 = (bf16[512,2048]{1,0:T(8,128)(2,1)}, bf16[512,2048]{1,0:T(8,128)(2,1)}, u32[]{:S(2)}, u32[]{:S(2)}) collective-permute-start(bf16[512,2048]{1,0:T(8,128)(2,1)} %add_convert_fusion.5), channel_id=1, source_target_pairs={{2,4},{4,2},{3,5},{5,3},{10,12},{12,10},{11,13},{13,11},{18,20},{2... | collective-permute-start | bytes 6291464 | tf_op jit(solution)/shard_map/ppermute | solution.py:87
  872.9 64.2 %collective-permute-start.71 = (bf16[4,512,1024]{2,1,0:T(8,128)(2,1)}, bf16[4,512,1024]{2,1,0:T(8,128)(2,1)}, u32[]{:S(2)}, u32[]{:S(2)}) collective-permute-start(bf16[4,512,1024]{2,1,0:T(8,128)(2,1)} %all-to-all-done.2.own_ref), channel_id=1, source_target_pairs={{0,1},{1,0},{2,3},{3,2},{4,5},{5,4},{6,7},{7,6},{8,9},{9,8},{10,11... | collective-permute-start | bytes 12582920 | tf_op jit(solution)/shard_map/ppermute | solution.py:31
  895.5 61.5 %collective-permute-start.81 = (bf16[512,2048]{1,0:T(8,128)(2,1)}, bf16[512,2048]{1,0:T(8,128)(2,1)}, u32[]{:S(2)}, u32[]{:S(2)}) collective-permute-start(bf16[512,2048]{1,0:T(8,128)(2,1)} %add_convert_fusion.4), channel_id=1, source_target_pairs={{2,0},{4,6},{3,1},{5,7},{10,8},{12,14},{11,9},{13,15},{18,16},{20,... | collective-permute-start | bytes 6291464 | tf_op jit(solution)/shard_map/ppermute | solution.py:87
  900.5 56.5 %collective-permute-start.83 = (bf16[512,2048]{1,0:T(8,128)(2,1)}, bf16[512,2048]{1,0:T(8,128)(2,1)}, u32[]{:S(2)}, u32[]{:S(2)}) collective-permute-start(bf16[512,2048]{1,0:T(8,128)(2,1)} %add_convert_fusion.3), channel_id=1, source_target_pairs={{2,4},{4,2},{3,5},{5,3},{10,12},{12,10},{11,13},{13,11},{18,20},{2... | collective-permute-start | bytes 6291464 | tf_op jit(solution)/shard_map/ppermute | solution.py:87
  (177 other events, 3260.8 us)
Sparse Core Ops, SparseCore 0:
  116.1 52.9 all-gather.1
